TPU v7x, 32 devices: a whole 2x2x4 slice. The times are simulated.
32 devices in a mesh: rep: 4 (over x, core), fsdp: 4 (over z), seq: 2 (over y).
Axes of the slice: x: 2, y: 2, z: 4, core: 2. Of those that a mesh axis runs over, the one named last changes fastest.
Arguments:
- tokens: bfloat16 [16, 592, 1024], P(('rep', 'fsdp'), 'seq'), may hold values from -6 to 6
- slot_mask: int32 [16], P(('rep', 'fsdp')), may hold values 0 or 1
- cotangent: bfloat16 [16, 592, 1024], P(('rep', 'fsdp'), 'seq'), may hold values from -6 to 6
- w_qkv: float32 [1024, 3072], P('fsdp'), may hold values from -0.25 to 0.25
- w_out: float32 [1024, 1024], P('fsdp'), may hold values from -0.75 to 0.75
- w_fc1: float32 [1024, 4096], P('fsdp'), may hold values from -0.1875 to 0.1875
- w_fc2: float32 [4096, 1024], P('fsdp'), may hold values from -0.125 to 0.125
- ln_gains: float32 [2, 1024], P(None, 'fsdp'), may hold values from 0.5 to 1.5
- biases: float32 [6, 1024], P(None, 'fsdp'), may hold values from -2 to 2
- fc1_bias: float32 [4096], P('fsdp'), may hold values from -2 to 2
Outputs:
- output: bfloat16 [16, 592, 1024], P(('rep', 'fsdp'), 'seq')
- grad_tokens: bfloat16 [16, 592, 1024], P(('rep', 'fsdp'), 'seq')
- grad_w_qkv: float32 [1024, 3072], P('fsdp')
- grad_w_out: float32 [1024, 1024], P('fsdp')
- grad_w_fc1: float32 [1024, 4096], P('fsdp')
- grad_w_fc2: float32 [4096, 1024], P('fsdp')
- grad_ln_gains: float32 [2, 1024], P(None, 'fsdp')
- grad_biases: float32 [6, 1024], P(None, 'fsdp')
- grad_fc1_bias: float32 [4096], P('fsdp')
All inputs are finite; a program needn't handle non-finite values. No bound on the sum of `slot_mask` on one device may be relied on, other than what follows from the above.
Results may differ from a plain program's by a relative error of at most 0.02.
The roundings to bfloat16 on the way count: a program that leaves them out, or rounds other values in their place, can miss the bound.
Values may be sent and summed in bfloat16 or wider, within the bound.
No kernel may reach another device: no remote copies, remote signals or barrier semaphores. Data moves between devices by JAX's collectives and lax.ppermute only.
A program may use at most 192 MiB of HBM per device.

v0:
```python
import jax
import jax.numpy as jnp
from jax import lax
from jax.sharding import PartitionSpec as P

HEADS = 16
HEAD_DIM = 64
IMG_TOK = 577


EPSILON = 1e-05
NEGATIVE = -1e30


def normalize(inputs, gain_row, shift_row):
    center = inputs - jnp.mean(inputs, axis=-1, keepdims=True)
    inverse = lax.rsqrt(jnp.mean(center * center, axis=-1, keepdims=True) + EPSILON)
    scaled = center * inverse
    return (scaled * gain_row + shift_row, scaled, inverse)


def norm_back(grad_in, scaled, inverse, gain_row):
    weighted = grad_in * gain_row
    return inverse * (
        weighted
        - jnp.mean(weighted, axis=-1, keepdims=True)
        - scaled * jnp.mean(weighted * scaled, axis=-1, keepdims=True)
    )


def across_rows(left_rows, right_rows):
    return lax.dot_general(
        left_rows, right_rows, (((0,), (0,)), ((), ())), preferred_element_type=jnp.float32
    )


def times_transposed(left_rows, right_rows):
    return lax.dot_general(
        left_rows, right_rows, (((1,), (1,)), ((), ())), preferred_element_type=jnp.float32
    )


def split_heads(matrix):
    return matrix.reshape(matrix.shape[0], HEADS, HEAD_DIM)


def masked_scores(query_rows, key_rows):
    scores = jnp.einsum(
        "qhd,khd->hqk",
        split_heads(query_rows),
        split_heads(key_rows),
        preferred_element_type=jnp.float32,
    )
    valid_keys = jnp.arange(key_rows.shape[0]) < IMG_TOK
    return jnp.where(valid_keys[None, None, :], scores, NEGATIVE)


def attend_slot(blocks_in):
    query_rows, key_rows, value_rows = blocks_in
    scores = masked_scores(query_rows, key_rows)
    highest = jnp.max(scores, axis=-1, keepdims=True)
    exponent = jnp.exp(scores - highest)
    total_sum = jnp.sum(exponent, axis=-1, keepdims=True)
    weights = (exponent / total_sum).astype(jnp.bfloat16)
    mixed_rows = jnp.einsum(
        "hqk,khd->qhd", weights, split_heads(value_rows), preferred_element_type=jnp.float32
    )
    return (mixed_rows.reshape(query_rows.shape[0], -1), highest + jnp.log(total_sum))


def attend_back(blocks_in):
    query_rows, key_rows, value_rows, log_total, grad_rows = blocks_in
    scores = masked_scores(query_rows, key_rows)
    probability = jnp.exp(scores - log_total)
    grad_heads = split_heads(grad_rows)
    grad_probs = jnp.einsum(
        "qhd,khd->hqk", grad_heads, split_heads(value_rows), preferred_element_type=jnp.float32
    )
    inner_sum = jnp.sum(probability * grad_probs, axis=-1, keepdims=True)
    grad_scores = (probability * (grad_probs - inner_sum)).astype(jnp.bfloat16)
    grad_query = jnp.einsum(
        "hqk,khd->qhd", grad_scores, split_heads(key_rows), preferred_element_type=jnp.float32
    )
    grad_key = jnp.einsum(
        "hqk,qhd->khd", grad_scores, split_heads(query_rows), preferred_element_type=jnp.float32
    )
    grad_value = jnp.einsum(
        "hqk,qhd->khd",
        probability.astype(jnp.bfloat16),
        grad_heads,
        preferred_element_type=jnp.float32,
    )
    key_count = key_rows.shape[0]
    return (
        grad_query.reshape(query_rows.shape[0], -1),
        grad_key.reshape(key_count, -1),
        grad_value.reshape(key_count, -1),
    )


def on_device(tokens, slot_mask, cotangent, w_qkv, w_out, w_fc1, w_fc2, ln_gains, biases, fc1_bias):
    slot_count, row_count, feature_width = tokens.shape
    low_qkv = w_qkv.astype(jnp.bfloat16)
    low_out = w_out.astype(jnp.bfloat16)
    low_fc1 = w_fc1.astype(jnp.bfloat16)
    low_fc2 = w_fc2.astype(jnp.bfloat16)
    low_gains = ln_gains.astype(jnp.bfloat16)
    low_biases = biases.astype(jnp.bfloat16)
    low_fc1_bias = fc1_bias.astype(jnp.bfloat16)
    gathered = (
        lax.all_gather(low_qkv, "fsdp", axis=0, tiled=True),
        lax.all_gather(low_out, "fsdp", axis=0, tiled=True),
        lax.all_gather(low_fc1, "fsdp", axis=0, tiled=True),
        lax.all_gather(low_fc2, "fsdp", axis=0, tiled=True),
        lax.all_gather(low_gains, "fsdp", axis=1, tiled=True),
        lax.all_gather(low_biases, "fsdp", axis=1, tiled=True),
        lax.all_gather(low_fc1_bias, "fsdp", axis=0, tiled=True),
    )
    big_qkv, big_out, big_fc1, big_fc2, gain_rows, bias_rows, fc1_shift = gathered
    gain_values = gain_rows.astype(jnp.float32)
    shift_values = bias_rows.astype(jnp.float32)
    hidden_shift = fc1_shift.astype(jnp.float32)
    head_scale = HEAD_DIM ** (-0.5)
    positions = lax.axis_index("seq") * row_count + jnp.arange(row_count)
    keep_mask = (
        slot_mask.astype(jnp.float32)[:, None] * (positions < IMG_TOK).astype(jnp.float32)[None, :]
    )
    keep_mask = keep_mask.reshape(-1, 1)
    inputs = tokens.astype(jnp.float32).reshape(-1, feature_width)
    normed_full, scaled_one, inverse_one = normalize(inputs, gain_values[0], shift_values[0])
    normed = normed_full.astype(jnp.bfloat16)
    joined = jnp.dot(normed, big_qkv, preferred_element_type=jnp.float32)
    queries = ((joined[:, :feature_width] + shift_values[1]) * head_scale).astype(jnp.bfloat16)
    keys_local = (
        joined[:, feature_width : 2 * feature_width]
        .astype(jnp.bfloat16)
        .reshape(slot_count, row_count, feature_width)
    )
    values_local = (
        (joined[:, 2 * feature_width :] + shift_values[2])
        .astype(jnp.bfloat16)
        .reshape(slot_count, row_count, feature_width)
    )
    slot_queries = queries.reshape(slot_count, row_count, feature_width)
    keys_all, values_all = (
        lax.all_gather(keys_local, "seq", axis=1, tiled=True),
        lax.all_gather(values_local, "seq", axis=1, tiled=True),
    )
    mixed_rows, log_total = lax.map(attend_slot, (slot_queries, keys_all, values_all))
    mixed_low = mixed_rows.reshape(-1, feature_width).astype(jnp.bfloat16)
    middle = inputs + (
        jnp.dot(mixed_low, big_out, preferred_element_type=jnp.float32) + shift_values[3]
    )
    normed_two_full, scaled_two, inverse_two = normalize(middle, gain_values[1], shift_values[4])
    normed_two = normed_two_full.astype(jnp.bfloat16)
    hidden = jnp.dot(normed_two, big_fc1, preferred_element_type=jnp.float32) + hidden_shift
    gate_values = jax.nn.sigmoid(1.702 * hidden)
    active = (hidden * gate_values).astype(jnp.bfloat16)
    result = jnp.dot(active, big_fc2, preferred_element_type=jnp.float32) + shift_values[5]
    output = ((middle + result) * keep_mask).astype(jnp.bfloat16).reshape(tokens.shape)
    again = (
        lax.all_gather(low_qkv, "fsdp", axis=0, tiled=True),
        lax.all_gather(low_out, "fsdp", axis=0, tiled=True),
        lax.all_gather(low_fc1, "fsdp", axis=0, tiled=True),
        lax.all_gather(low_fc2, "fsdp", axis=0, tiled=True),
        lax.all_gather(low_gains, "fsdp", axis=1, tiled=True),
        lax.all_gather(low_biases, "fsdp", axis=1, tiled=True),
        lax.all_gather(low_fc1_bias, "fsdp", axis=0, tiled=True),
    )
    back_qkv, back_out, back_fc1, back_fc2, back_gain_rows = (
        again[0],
        again[1],
        again[2],
        again[3],
        again[4],
    )
    back_gains = back_gain_rows.astype(jnp.float32)
    incoming = cotangent.astype(jnp.float32).reshape(-1, feature_width) * keep_mask
    grad_result = incoming.astype(jnp.bfloat16)
    grad_fc2 = across_rows(active, grad_result)
    grad_shift_five = jnp.sum(grad_result.astype(jnp.float32), axis=0)
    grad_active = times_transposed(grad_result, back_fc2)
    grad_hidden = (
        grad_active * (gate_values + 1.702 * hidden * gate_values * (1.0 - gate_values))
    ).astype(jnp.bfloat16)
    grad_fc1 = across_rows(normed_two, grad_hidden)
    grad_hidden_shift = jnp.sum(grad_hidden.astype(jnp.float32), axis=0)
    grad_normed_two = times_transposed(grad_hidden, back_fc1)
    grad_gain_two = jnp.sum(grad_normed_two * scaled_two, axis=0)
    grad_shift_four = jnp.sum(grad_normed_two, axis=0)
    grad_middle = incoming + norm_back(grad_normed_two, scaled_two, inverse_two, back_gains[1])
    grad_branch = grad_middle.astype(jnp.bfloat16)
    grad_out = across_rows(mixed_low, grad_branch)
    grad_shift_three = jnp.sum(grad_branch.astype(jnp.float32), axis=0)
    grad_mixed = times_transposed(grad_branch, back_out).astype(jnp.bfloat16)
    grad_query, key_part, value_part = lax.map(
        attend_back,
        (
            slot_queries,
            keys_all,
            values_all,
            log_total,
            grad_mixed.reshape(slot_count, row_count, feature_width),
        ),
    )
    grad_keys, grad_values = (
        lax.psum_scatter(
            key_part.astype(jnp.bfloat16), "seq", scatter_dimension=1, tiled=True
        ).astype(jnp.float32),
        lax.psum_scatter(
            value_part.astype(jnp.bfloat16), "seq", scatter_dimension=1, tiled=True
        ).astype(jnp.float32),
    )
    query_grad_low = (grad_query.astype(jnp.bfloat16) * head_scale).reshape(-1, feature_width)
    key_grad_low = grad_keys.astype(jnp.bfloat16).reshape(-1, feature_width)
    value_grad_low = grad_values.astype(jnp.bfloat16).reshape(-1, feature_width)
    grad_joined = jnp.concatenate([query_grad_low, key_grad_low, value_grad_low], axis=1)
    grad_qkv = across_rows(normed, grad_joined)
    grad_shift_one = jnp.sum(query_grad_low.astype(jnp.float32), axis=0)
    grad_shift_two = jnp.sum(value_grad_low.astype(jnp.float32), axis=0)
    grad_normed = times_transposed(grad_joined, back_qkv)
    grad_gain_one = jnp.sum(grad_normed * scaled_one, axis=0)
    grad_shift_zero = jnp.sum(grad_normed, axis=0)
    grad_inputs = grad_middle + norm_back(grad_normed, scaled_one, inverse_one, back_gains[0])
    grad_tokens = grad_inputs.astype(jnp.bfloat16).reshape(tokens.shape)
    grad_gains = jnp.stack([grad_gain_one, grad_gain_two])
    grad_shifts = jnp.stack(
        [
            grad_shift_zero,
            grad_shift_one,
            grad_shift_two,
            grad_shift_three,
            grad_shift_four,
            grad_shift_five,
        ]
    )
    shards = (
        lax.psum_scatter(
            grad_qkv.astype(jnp.bfloat16), "fsdp", scatter_dimension=0, tiled=True
        ).astype(jnp.float32),
        lax.psum_scatter(
            grad_out.astype(jnp.bfloat16), "fsdp", scatter_dimension=0, tiled=True
        ).astype(jnp.float32),
        lax.psum_scatter(
            grad_fc1.astype(jnp.bfloat16), "fsdp", scatter_dimension=0, tiled=True
        ).astype(jnp.float32),
        lax.psum_scatter(
            grad_fc2.astype(jnp.bfloat16), "fsdp", scatter_dimension=0, tiled=True
        ).astype(jnp.float32),
        lax.psum_scatter(
            grad_gains.astype(jnp.bfloat16), "fsdp", scatter_dimension=1, tiled=True
        ).astype(jnp.float32),
        lax.psum_scatter(
            grad_shifts.astype(jnp.bfloat16), "fsdp", scatter_dimension=1, tiled=True
        ).astype(jnp.float32),
        lax.psum_scatter(
            grad_hidden_shift.astype(jnp.bfloat16), "fsdp", scatter_dimension=0, tiled=True
        ).astype(jnp.float32),
    )
    summed = (
        lax.psum(shards[0].astype(jnp.bfloat16), ("rep", "seq")).astype(jnp.float32),
        lax.psum(shards[1].astype(jnp.bfloat16), ("rep", "seq")).astype(jnp.float32),
        lax.psum(shards[2].astype(jnp.bfloat16), ("rep", "seq")).astype(jnp.float32),
        lax.psum(shards[3].astype(jnp.bfloat16), ("rep", "seq")).astype(jnp.float32),
        lax.psum(shards[4].astype(jnp.bfloat16), ("rep", "seq")).astype(jnp.float32),
        lax.psum(shards[5].astype(jnp.bfloat16), ("rep", "seq")).astype(jnp.float32),
        lax.psum(shards[6].astype(jnp.bfloat16), ("rep", "seq")).astype(jnp.float32),
    )
    return (
        output,
        grad_tokens,
        summed[0],
        summed[1],
        summed[2],
        summed[3],
        summed[4],
        summed[5],
        summed[6],
    )


def solution(mesh):
    return jax.shard_map(
        on_device,
        mesh=mesh,
        in_specs=(
            P(("rep", "fsdp"), "seq", None),
            P(("rep", "fsdp")),
            P(("rep", "fsdp"), "seq", None),
            P("fsdp", None),
            P("fsdp", None),
            P("fsdp", None),
            P("fsdp", None),
            P(None, "fsdp"),
            P(None, "fsdp"),
            P("fsdp"),
        ),
        out_specs=(
            P(("rep", "fsdp"), "seq", None),
            P(("rep", "fsdp"), "seq", None),
            P("fsdp", None),
            P("fsdp", None),
            P("fsdp", None),
            P("fsdp", None),
            P(None, "fsdp"),
            P(None, "fsdp"),
            P("fsdp"),
        ),
        check_vma=False,
    )
```

profile of v0, /device:TPU:0, one launch (start us, length us, event | category | flops | bytes accessed | tf_op | source)
XLA Modules:
  0.0 1236.7 jit_solution(1024592312134364579)
XLA Ops:
  10.7 12.6 %all_gather.32 = bf16[2,1024]{1,0:T(2,128)(2,1)S(1)} all-gather(bf16[2,256]{1,0:T(2,128)(2,1)S(1)} %convert_element_type.210), channel_id=1, replica_groups=mesh['rep'=4,'fsdp'=4,'seq'=2] {'fsdp'}, dimensions={1}, use_global_device_ids=true | all-gather | bytes 5120 | tf_op jit(solution)/shard_map/all_gather | solution.py:115
  23.3 14.3 %all_gather.33 = bf16[6,1024]{1,0:T(8,128)(2,1)S(1)} all-gather(bf16[6,256]{1,0:T(8,128)(2,1)S(1)} %convert_element_type.212), channel_id=1, replica_groups=mesh['rep'=4,'fsdp'=4,'seq'=2] {'fsdp'}, dimensions={1}, use_global_device_ids=true | all-gather | bytes 15360 | tf_op jit(solution)/shard_map/all_gather | solution.py:116
  38.1 90.8 %all-gather.9.cloned.1.call-done = bf16[1024,3072]{1,0:T(8,128)(2,1)} async-done(((bf16[256,3072]{1,0:T(8,128)(2,1)}), bf16[1024,3072]{1,0:T(8,128)(2,1)}) %all-gather.9.cloned.1.call-update) | async-done | bytes 6291472 | tf_op jit(solution)/shard_map/all_gather | solution.py:111
  149.5 11.9 all_gather.39
  163.7 19.9 %all-gather.17.cloned.1.call-done = bf16[592,1024]{1,0:T(8,128)(2,1)} async-done(((bf16[296,1024]{1,0:T(8,128)(2,1)}), bf16[592,1024]{1,0:T(8,128)(2,1)}) %all-gather.17.cloned.1.call-update) | async-done | bytes 1212432 | tf_op jit(solution)/shard_map/all_gather | solution.py:147
  197.9 33.1 %all-gather.11.cloned.1.call-done = bf16[1024,1024]{1,0:T(8,128)(2,1)} async-done(((bf16[256,1024]{1,0:T(8,128)(2,1)}), bf16[1024,1024]{1,0:T(8,128)(2,1)}) %all-gather.11.cloned.1.call-update) | async-done | bytes 2097168 | tf_op jit(solution)/shard_map/all_gather | solution.py:112
  234.1 147.3 %all-gather.13.cloned.1.call-done = bf16[1024,4096]{1,0:T(8,128)(2,1)} async-done(((bf16[256,4096]{1,0:T(8,128)(2,1)}), bf16[1024,4096]{1,0:T(8,128)(2,1)}) %all-gather.13.cloned.1.call-update) | async-done | bytes 8388624 | tf_op jit(solution)/shard_map/all_gather | solution.py:113
  381.4 8.5 convolution_add_fusion
  389.9 141.4 %all-gather.15.cloned.1.call-done = bf16[4096,1024]{1,0:T(8,128)(2,1)} async-done(((bf16[1024,1024]{1,0:T(8,128)(2,1)}), bf16[4096,1024]{1,0:T(8,128)(2,1)}) %all-gather.15.cloned.1.call-update) | async-done | bytes 8388624 | tf_op jit(solution)/shard_map/all_gather | solution.py:114
  531.3 9.0 fusion.61
  549.0 8.5 fusion.9
  567.0 9.8 multiply_reduce_fusion
  619.9 7.4 convolution_convert_fusion.2
  628.3 9.7 convolution_convert_fusion
  638.1 8.8 convolution_convert_fusion.1
  655.7 7.1 reduce-scatter.17.cloned.1.call-done
  662.7 112.4 %reduce-scatter.15.cloned.1.call-done = bf16[256,3072]{1,0:T(8,128)(2,1)} async-done(((bf16[1024,3072]{1,0:T(8,128)(2,1)}), bf16[256,3072]{1,0:T(8,128)(2,1)}) %reduce-scatter.15.cloned.1.call-update) | async-done | bytes 1572880 | tf_op jit(solution)/shard_map/reduce_scatter | solution.py:238
  775.1 147.5 %reduce-scatter.21.cloned.1.call-done = bf16[1024,1024]{1,0:T(8,128)(2,1)} async-done(((bf16[4096,1024]{1,0:T(8,128)(2,1)}), bf16[1024,1024]{1,0:T(8,128)(2,1)}) %reduce-scatter.21.cloned.1.call-update) | async-done | bytes 2097168 | tf_op jit(solution)/shard_map/reduce_scatter | solution.py:247
  922.6 147.6 %reduce-scatter.19.cloned.1.call-done = bf16[256,4096]{1,0:T(8,128)(2,1)} async-done(((bf16[1024,4096]{1,0:T(8,128)(2,1)}), bf16[256,4096]{1,0:T(8,128)(2,1)}) %reduce-scatter.19.cloned.1.call-update) | async-done | bytes 2097168 | tf_op jit(solution)/shard_map/reduce_scatter | solution.py:244
  1072.1 11.4 all-reduce
  1083.5 8.6 fusion.25
  1094.4 18.9 %reduce-scatter.23.cloned.1.call-done = bf16[6,256]{1,0:T(8,128)(2,1)} async-done(((bf16[6,1024]{1,0:T(8,128)(2,1)}), bf16[6,256]{1,0:T(8,128)(2,1)}) %reduce-scatter.23.cloned.1.call-update) | async-done | bytes 3088 | tf_op jit(solution)/shard_map/reduce_scatter | solution.py:253
  1113.3 14.1 %all-reduce.1 = (bf16[2,256]{1,0:T(2,128)(2,1)S(1)}, bf16[6,256]{1,0:T(8,128)(2,1)S(1)}, bf16[1024]{0:T(1024)(128)(2,1)S(1)}) all-reduce(bf16[2,256]{1,0:T(2,128)(2,1)S(1)} %copy.40, bf16[6,256]{1,0:T(8,128)(2,1)} %reduce-scatter.23.cloned.1.call-done, ...), channel_id=1, replica_groups=mesh['rep'=4,'fsdp'=4,'seq'=2] {'rep','seq'}, use_global_device_ids=true, to_apply=%region_24.25 | all-reduce | flops 3072 | bytes 12288 | tf_op jit(solution)/shard_map/psum | solution.py:265
  1129.2 91.1 %all-reduce.5.cloned.1.call-done = (bf16[256,3072]{1,0:T(8,128)(2,1)}, bf16[256,1024]{1,0:T(8,128)(2,1)}, bf16[256,4096]{1,0:T(8,128)(2,1)}, bf16[1024,1024]{1,0:T(8,128)(2,1)}) async-done(((bf16[256,3072]{1,0:T(8,128)(2,1)}, bf16[256,1024]{1,0:T(8,128)(2,1)}, bf16[256,4096]{1,0:T(8,128)(2,1)}, bf16[1024,1024]{1,0:T(8,128)(2,1)}), (bf16[256,3072]{1,0:T(8,128)(2,1)}, bf16[256,1024]{1,0:T(8,128)(2,1)}, ...) | async-done | bytes 6291472 | tf_op jit(solution)/shard_map/psum | solution.py:261
  (153 shorter events, 129.0 us)
Async XLA Ops:
  7.2 30.4 %copy-start.2 = (bf16[1,296,1024]{2,1,0:T(8,128)(2,1)S(1)}, bf16[1,296,1024]{2,1,0:T(8,128)(2,1)}, u32[]{:S(2)}) copy-start(bf16[1,296,1024]{2,1,0:T(8,128)(2,1)} %param.10) | copy-start | bytes 1818628
  7.2 121.7 %all-gather.9.cloned.1.call-start = ((), (), s32[]{:S(2)}) async-start(), calls=%async_computation.8 | async-start | bytes 7864320 | tf_op jit(solution)/shard_map/all_gather | solution.py:111
  10.6 151.2 %all-gather.19.cloned.1.call-start = ((), (), s32[]{:S(2)}) async-start(), calls=%async_computation.18 | async-start | bytes 1818624 | tf_op jit(solution)/shard_map/all_gather | solution.py:146
  136.7 46.9 %all-gather.17.cloned.1.call-start = ((), (), s32[]{:S(2)}) async-start(), calls=%async_computation.17 | async-start | bytes 1818624 | tf_op jit(solution)/shard_map/all_gather | solution.py:147
  139.7 91.3 %all-gather.11.cloned.1.call-start = ((), (), s32[]{:S(2)}) async-start(), calls=%async_computation.9 | async-start | bytes 2621440 | tf_op jit(solution)/shard_map/all_gather | solution.py:112
  140.7 240.7 %all-gather.13.cloned.1.call-start = ((), (), s32[]{:S(2)}) async-start(), calls=%async_computation.10 | async-start | bytes 10485760 | tf_op jit(solution)/shard_map/all_gather | solution.py:113
  144.8 386.4 %all-gather.15.cloned.1.call-start = ((), (), s32[]{:S(2)}) async-start(), calls=%async_computation.11 | async-start | bytes 10485760 | tf_op jit(solution)/shard_map/all_gather | solution.py:114
  148.7 457.0 %reduce-scatter.27.cloned.1.call-start = ((), (), s32[]{:S(2)}) async-start(), calls=%async_computation.20 | async-start | bytes 1818624
  161.7 24.3 %copy-start.5 = (bf16[296,1024]{0,1:T(8,128)(2,1)}, bf16[296,1024]{0,1:T(8,128)(2,1)S(1)}, u32[]{:S(2)}) copy-start(bf16[296,1024]{0,1:T(8,128)(2,1)S(1)} %copy.32) | copy-start | bytes 1818628
  188.2 4.9 copy-start
  188.2 4.9 copy-start.7
  531.3 9.1 copy-start.20
  566.9 49.0 %reduce-scatter.25.cloned.1.call-start = ((), (), s32[]{:S(2)}) async-start(), calls=%async_computation.19 | async-start | bytes 1818624
  576.8 6.6 copy-start.6
  595.8 67.0 %reduce-scatter.17.cloned.1.call-start = ((), (), s32[]{:S(2)}) async-start(), calls=%async_computation.13 | async-start | bytes 2621440 | tf_op jit(solution)/shard_map/reduce_scatter | solution.py:241
  599.9 175.2 %reduce-scatter.15.cloned.1.call-start = ((), (), s32[]{:S(2)}) async-start(), calls=%async_computation.12 | async-start | bytes 7864320 | tf_op jit(solution)/shard_map/reduce_scatter | solution.py:238
  627.3 295.3 %reduce-scatter.21.cloned.1.call-start = ((), (), s32[]{:S(2)}) async-start(), calls=%async_computation.15 | async-start | bytes 10485760 | tf_op jit(solution)/shard_map/reduce_scatter | solution.py:247
  638.0 432.2 %reduce-scatter.19.cloned.1.call-start = ((), (), s32[]{:S(2)}) async-start(), calls=%async_computation.14 | async-start | bytes 10485760 | tf_op jit(solution)/shard_map/reduce_scatter | solution.py:244
  646.9 446.6 %reduce-scatter.29.cloned.1.call-start = ((), (), s32[]{:S(2)}) async-start(), calls=%async_computation.21 | async-start | bytes 327680
  654.7 458.6 %reduce-scatter.23.cloned.1.call-start = ((), (), s32[]{:S(2)}) async-start(), calls=%async_computation.16 | async-start | bytes 20480 | tf_op jit(solution)/shard_map/reduce_scatter | solution.py:253
  655.6 564.7 %all-reduce.5.cloned.1.call-start = ((), (), s32[]{:S(2)}) async-start(), calls=%async_computation.22 | async-start | bytes 12582912 | tf_op jit(solution)/shard_map/psum | solution.py:261
  1083.5 8.7 copy-start.16
  1083.5 8.7 copy-start.4
  1092.2 21.2 %dynamic-slice-start = ((bf16[4096]{0:T(1024)(128)(2,1)}, u32[]{:T(128)}), bf16[1024]{0:T(1024)(128)(2,1)S(1)}, s32[]{:S(2)}) async-start(bf16[4096]{0:T(1024)(128)(2,1)} %copy-done.16, u32[]{:T(128)} %multiply.49), calls=%async_computation.23 | async-start | bytes 4608
  (15 other events, 33.0 us)
Sparse Core Ops, SparseCore 0:
  10.7 118.1 all-gather.8
  136.8 21.4 all-gather.18
  160.4 23.1 all-gather.16
  185.0 45.9 all-gather.10
  233.0 148.3 all-gather.12
  383.4 147.8 all-gather.14
  567.1 20.3 reduce-scatter.26
  595.9 20.0 reduce-scatter.24
  618.8 43.8 reduce-scatter.16
  665.0 110.0 reduce-scatter.14
  777.6 144.9 reduce-scatter.20
  925.0 145.1 reduce-scatter.18
  1073.1 20.3 reduce-scatter.28
  1096.2 17.1 reduce-scatter.22
  1117.2 103.0 all-reduce.4
where the time goes:
time: 1240 us
  waiting for transfers between devices  963 us (78%)
  matrix products  109 us (9%)
  blocking collectives  64.3 us (5%)
  local copies, waits for them, and re-layouts  42.3 us (3%)
  other arithmetic  41.2 us (3%)
  between operations  16.1 us (1%)
    reduce_scatter x1, waiting for transfers between devices, on_device(): lax.psum_scatter(grad_fc1.astype(jnp.bfloat16), 'fsdp', scatter_dimension...  148 us
    reduce_scatter x1, waiting for transfers between devices, on_device(): lax.psum_scatter(grad_fc2.astype(jnp.bfloat16), 'fsdp', scatter_dimension...  148 us
    all_gather x1, waiting for transfers between devices, on_device(): lax.all_gather(low_fc1, 'fsdp', axis=0, tiled=True)  147 us
    all_gather x1, waiting for transfers between devices, on_device(): lax.all_gather(low_fc2, 'fsdp', axis=0, tiled=True)  141 us
    reduce_scatter x1, waiting for transfers between devices, on_device(): lax.psum_scatter(grad_qkv.astype(jnp.bfloat16), 'fsdp', scatter_dimension...  112 us
    psum x1, waiting for transfers between devices, on_device(): lax.psum(shards[0].astype(jnp.bfloat16), ('rep', 'seq')).astype(jnp.float32)  91.1 us
    all_gather x1, waiting for transfers between devices, on_device(): lax.all_gather(low_qkv, 'fsdp', axis=0, tiled=True)  90.8 us
    unnamed x58, local copies, waits for them, and re-layouts  33.7 us
  transfers between devices with their start and end apart: 15, of which 12 were waited for; matrix products, arithmetic and copies ran while one was open for 11% of the time, Pallas kernels for 0%

commit v1 on v0

v1 whole, which is shorter than its diff:
```python
import functools

import jax
import jax.numpy as jnp
from jax import lax
from jax.experimental import pallas as pl
from jax.experimental.pallas import tpu as pltpu
from jax.sharding import PartitionSpec as P

HEADS = 16
HEAD_DIM = 64
IMG_TOK = 577
EPSILON = 1e-05
NEGATIVE = -1e30
LANES = 128
BF = jnp.bfloat16
F32 = jnp.float32

ANY = pl.BlockSpec(memory_space=pl.ANY)
VM = pl.BlockSpec(memory_space=pltpu.VMEM)
SM = pl.BlockSpec(memory_space=pltpu.SMEM)

ORDER = (0, 2, 1, 3)


def mm(a, b):
    return lax.dot_general(a, b, (((1,), (0,)), ((), ())), preferred_element_type=F32)


def mmt(a, b):
    return lax.dot_general(a, b, (((1,), (1,)), ((), ())), preferred_element_type=F32)


def tmm(a, b):
    return lax.dot_general(a, b, (((0,), (0,)), ((), ())), preferred_element_type=F32)


def normalize(inputs):
    center = inputs - jnp.mean(inputs, axis=-1, keepdims=True)
    inverse = lax.rsqrt(jnp.mean(center * center, axis=-1, keepdims=True) + EPSILON)
    return center * inverse, inverse


def norm_back(grad_in, scaled, inverse, gain_row):
    weighted = grad_in * gain_row
    return inverse * (
        weighted
        - jnp.mean(weighted, axis=-1, keepdims=True)
        - scaled * jnp.mean(weighted * scaled, axis=-1, keepdims=True)
    )


def at(index, size):
    return pl.ds(pl.multiple_of(index * size, size), size)


def flip(r, d):
    return jnp.bitwise_xor(r, d) if d else r


def fetch(copies, sems):
    handles = [pltpu.make_async_copy(s, t, sems.at[i]) for i, (s, t) in enumerate(copies)]
    for handle in handles:
        handle.start()
    return handles


def finish(handles):
    for handle in handles:
        handle.wait()


def call(body, ins, specs, outs, scratch, flops, name, out_specs=None):
    moved = sum(a.size * a.dtype.itemsize for a in ins)
    moved += sum(s.size * s.dtype.itemsize for s in outs)
    return pl.pallas_call(
        body,
        out_shape=outs,
        in_specs=specs,
        out_specs=out_specs or [VM] * len(outs),
        scratch_shapes=scratch,
        compiler_params=pltpu.CompilerParams(vmem_limit_bytes=56 << 20),
        cost_estimate=pl.CostEstimate(flops=flops, bytes_accessed=moved, transcendentals=0),
        name=name,
    )(*ins)


def shape(dims, dtype):
    return jax.ShapeDtypeStruct(dims, dtype)


def column_copies(refs, w, ids, n, relative=False):
    r, z = ids[0], ids[2]
    q = w.shape[1] // 4
    slots = [(ORDER.index(d), d) for d in range(4)]
    if len(refs) == 1:
        if not relative:
            return [(refs[0], w)]
        return [
            (refs[0].at[:, at(flip(r, d), q)], w.at[:, pl.ds(s * q, q)]) for s, d in slots
        ]
    rows = w.shape[0] // n
    here = at(z, rows)
    if relative:
        copies = [
            (refs[0].at[:, at(flip(r, d), q)], w.at[here, pl.ds(s * q, q)]) for s, d in slots
        ]
    else:
        copies = [(refs[0], w.at[here, :])]
    for k in range(1, n):
        there = at(lax.rem(z - k + n, n), rows)
        for s, d in slots:
            columns = pl.ds(s * q, q) if relative else at(flip(r, d), q)
            copies.append((refs[1 + (k - 1) * 4 + d], w.at[there, columns]))
    return copies


def row_copies(refs, w, ids, n):
    r, z = ids[0], ids[2]
    if len(refs) == 1:
        return [(refs[0], w)]
    h = w.shape[0] // (4 * n)
    copies = [(refs[0].at[i], w.at[at(i * n + z, h), :]) for i in range(4)]
    for k in range(1, n):
        there = lax.rem(z - k + n, n)
        for d in range(4):
            copies.append(
                (refs[1 + (k - 1) * 4 + d], w.at[at(flip(r, d) * n + there, h), :])
            )
    return copies


def split(refs, *counts):
    refs = list(refs)
    out = []
    for count in counts:
        out.append(refs[:count])
        refs = refs[count:]
    return out + [refs]


def qkv_kernel(n, pieces, ids, own, near, vec, qb, vb, *refs):
    weights, (normed, queries, keys, values), (w, sems) = split(refs, pieces, 4)
    handles = fetch(column_copies(weights, w, ids, n), sems)
    rows = own.shape[0]
    for i, part in enumerate((own, near)):
        scaled, _ = normalize(part[...].astype(F32))
        normed[i * rows : (i + 1) * rows, :] = (scaled * vec[0:1, :] + vec[2:3, :]).astype(BF)
    finish(handles)
    scale = HEAD_DIM ** (-0.5)

    def step(i, carry):
        joined = mm(normed[...], w[:, at(i, 3 * LANES)])
        here = at(i, LANES)
        queries[:, here] = ((joined[:, :LANES] + qb[:, here]) * scale).astype(BF)
        keys[:, here] = joined[:, LANES : 2 * LANES].astype(BF)
        values[:, here] = (joined[:, 2 * LANES :] + vb[:, here]).astype(BF)
        return carry

    lax.fori_loop(0, 4, step, 0)


def valid_keys(ids, rows, real):
    index = lax.broadcasted_iota(jnp.int32, (1, 2 * rows), 1)
    second = (index >= rows).astype(jnp.int32)
    local = index - second * rows
    position = jnp.bitwise_xor(second, ids[1]) * real + local
    return (local < real) & (position < IMG_TOK)


def head_half(value, half):
    lane = lax.broadcasted_iota(jnp.int32, value.shape, 1)
    keep = (lane < HEAD_DIM) if half == 0 else (lane >= HEAD_DIM)
    return jnp.where(keep, value, jnp.zeros_like(value))


def softmax(scores, valid):
    scores = jnp.where(valid, scores, NEGATIVE)
    exponent = jnp.exp(scores - jnp.max(scores, axis=-1, keepdims=True))
    return exponent * (1.0 / jnp.sum(exponent, axis=-1, keepdims=True))


def attend_kernel(rows, real, ids, queries, keys, values, mixed_own, mixed_near):
    valid = valid_keys(ids, rows, real)
    keys_of = [head_half(keys[...], half) for half in range(2)]
    values_of = [head_half(values[...], half) for half in range(2)]
    for i, target in enumerate((mixed_own, mixed_near)):
        block = queries[i * rows : (i + 1) * rows, :]
        total = None
        for half in range(2):
            weights = softmax(mmt(block, keys_of[half]), valid).astype(BF)
            part = mm(weights, values_of[half])
            total = part if total is None else total + part
        target[...] = total.astype(BF)


def attend(ids, queries, keys, values, rows, real):
    wide = queries.shape[1]
    block = pl.BlockSpec((2 * rows, LANES), lambda i, ids: (0, i))
    half = pl.BlockSpec((rows, LANES), lambda i, ids: (0, i))
    return pl.pallas_call(
        functools.partial(attend_kernel, rows, real),
        grid_spec=pltpu.PrefetchScalarGridSpec(
            num_scalar_prefetch=1,
            grid=(wide // LANES,),
            in_specs=[block] * 3,
            out_specs=[half] * 2,
        ),
        out_shape=[shape((rows, wide), BF)] * 2,
        compiler_params=pltpu.CompilerParams(vmem_limit_bytes=56 << 20),
        cost_estimate=pl.CostEstimate(
            flops=8 * (2 * rows) ** 2 * wide,
            bytes_accessed=8 * rows * wide * 2,
            transcendentals=0,
        ),
        name="attend",
    )(ids, queries, keys, values)


def slot_of(i):
    return ((i & 1) << 1) | (i >> 1)


def attend_back_kernel(
    rows, real, ids, queries, keys, values, grad_own, grad_near, near, far, sums
):
    i = pl.program_id(0)
    valid = valid_keys(ids, rows, real)
    keys_of = [head_half(keys[...], half) for half in range(2)]
    values_of = [head_half(values[...], half) for half in range(2)]
    grad_k = grad_v = None
    grad_q = []
    for part, grad_ref in enumerate((grad_own, grad_near)):
        block = queries[part * rows : (part + 1) * rows, :]
        grad = grad_ref[...]
        total = None
        for half in range(2):
            probs = softmax(mmt(block, keys_of[half]), valid)
            grad_probs = mmt(grad, values_of[half])
            inner = jnp.sum(probs * grad_probs, axis=-1, keepdims=True)
            grad_scores = (probs * (grad_probs - inner)).astype(BF)
            first = mm(grad_scores, keys_of[half])
            total = first if total is None else total + first
            second = tmm(grad_scores, head_half(block, half))
            third = tmm(probs.astype(BF), head_half(grad, half))
            grad_k = second if grad_k is None else grad_k + second
            grad_v = third if grad_v is None else grad_v + third
        grad_q.append(total)
    scale = HEAD_DIM ** (-0.5)
    grad_q = jnp.concatenate(grad_q, axis=0).astype(BF).astype(F32) * scale
    pieces = [grad_q.astype(BF), grad_k.astype(BF), grad_v.astype(BF)]
    for kind, piece in enumerate(pieces):
        columns = slice(kind * LANES, (kind + 1) * LANES)
        sums[:, columns] = jnp.sum(piece.astype(F32), axis=0, keepdims=True)

        @pl.when(i < 2)
        def _():
            near[:, columns] = piece

        @pl.when(i >= 2)
        def _():
            far[:, columns] = piece


def attend_back(ids, queries, keys, values, grad_own, grad_near, rows, real):
    wide = queries.shape[1]

    def column(i, ids):
        return (0, jnp.bitwise_xor(ids[0], slot_of(i)))

    block = pl.BlockSpec((2 * rows, LANES), column)
    half = pl.BlockSpec((rows, LANES), column)
    pair = (2, 2 * rows, 3 * LANES)
    return pl.pallas_call(
        functools.partial(attend_back_kernel, rows, real),
        grid_spec=pltpu.PrefetchScalarGridSpec(
            num_scalar_prefetch=1,
            grid=(4,),
            in_specs=[block] * 3 + [half] * 2,
            out_specs=[
                pl.BlockSpec((None,) + pair[1:], lambda i, ids: (jnp.minimum(i, 1), 0, 0)),
                pl.BlockSpec((None,) + pair[1:], lambda i, ids: (jnp.maximum(i - 2, 0), 0, 0)),
                pl.BlockSpec((None, 1, 3 * LANES), lambda i, ids: (i, 0, 0)),
            ],
        ),
        out_shape=[shape(pair, BF), shape(pair, BF), shape((4, 1, 3 * LANES), F32)],
        compiler_params=pltpu.CompilerParams(vmem_limit_bytes=56 << 20),
        cost_estimate=pl.CostEstimate(
            flops=20 * (2 * rows) ** 2 * wide,
            bytes_accessed=16 * rows * wide * 2,
            transcendentals=0,
        ),
        name="attend_back",
    )(ids, queries, keys, values, grad_own, grad_near)


def project_kernel(n, pieces, ids, tokens, mixed_own, mixed_near, vec, *refs):
    weights, (mixed, middle, normed), (w, sems) = split(refs, pieces, 3)
    handles = fetch(column_copies(weights, w, ids, n), sems)
    y = ids[1]
    half = mixed_own.shape[1]
    mixed[:, at(y, half)] = mixed_own[...]
    mixed[:, at(1 - y, half)] = mixed_near[...]
    finish(handles)
    total = tokens[...].astype(F32) + (mm(mixed[...], w[...]) + vec[5:6, :])
    middle[...] = total
    scaled, _ = normalize(total)
    normed[...] = (scaled * vec[1:2, :] + vec[6:7, :]).astype(BF)


def mlp_kernel(n, one, two, ids, n_own, n_near, g_own, g_near, fb, *refs):
    ones, twos, outs, scratch = split(refs, one, two, 7)
    act_near, act_far, gh_near, gh_far, grad_own, grad_near, sums = outs
    w1, w2, normed, grads, total, sems = scratch
    r = ids[0]
    rows = n_own.shape[0]
    handles = fetch(column_copies(ones, w1, ids, n) + row_copies(twos, w2, ids, n), sems)
    normed[:rows, :] = n_own[...]
    normed[rows:, :] = n_near[...]
    grads[:rows, :] = g_own[...]
    grads[rows:, :] = g_near[...]
    total[...] = jnp.zeros_like(total)
    finish(handles)
    wide = w1.shape[1] // 4

    def step(i, carry):
        here = at(i, wide)
        hidden = mm(normed[...], w1[:, here]) + fb[:, here]
        gate = 1.0 / (1.0 + jnp.exp(-1.702 * hidden))
        active = (hidden * gate).astype(BF)
        grad_active = mmt(grads[...], w2[here, :])
        grad_hidden = (
            grad_active * (gate + 1.702 * hidden * gate * (1.0 - gate))
        ).astype(BF)
        sums[:, here] = jnp.sum(grad_hidden.astype(F32), axis=0, keepdims=True)
        total[...] += mmt(grad_hidden, w1[:, here])
        d = jnp.bitwise_xor(r, i)

        @pl.when((d & 1) == 0)
        def _():
            act_near[d >> 1] = active
            gh_near[d >> 1] = grad_hidden

        @pl.when((d & 1) == 1)
        def _():
            act_far[d >> 1] = active
            gh_far[d >> 1] = grad_hidden

        return carry

    lax.fori_loop(0, 4, step, 0)
    grad_own[...] = total[:rows, :]
    grad_near[...] = total[rows:, :].astype(BF)


def result_kernel(n, two, ids, act_near, act_far, *refs):
    twos, (own, near), (w2, total, sems) = split(refs, two, 2)
    r = ids[0]
    handles = fetch(row_copies(twos, w2, ids, n), sems)
    rows = own.shape[0]
    wide = w2.shape[0] // 4
    finish(handles)
    for s, d in enumerate(ORDER):
        part = act_near if s < 2 else act_far
        value = mm(part[s % 2], w2[at(flip(r, d), wide), :])
        if s:
            value = value + total[...]
        if s < 3:
            total[...] = value
    own[...] = value[:rows, :]
    near[...] = value[rows:, :].astype(BF)


def middle_back_kernel(
    n, pieces, ids, grad_own, grad_recv, middle, incoming, vec, *refs
):
    weights, outs, (w, work, sems) = split(refs, pieces, 5)
    grad_middle, branch, mixed_own, mixed_near, sums = outs
    handles = fetch(column_copies(weights, w, ids, n), sems)
    y = ids[1]
    grad = grad_own[...] + grad_recv[...].astype(F32)
    scaled, inverse = normalize(middle[...])
    sums[0:1, :] = jnp.sum(grad * scaled, axis=0, keepdims=True)
    sums[1:2, :] = jnp.sum(grad, axis=0, keepdims=True)
    arriving = incoming[...].astype(F32)
    sums[3:4, :] = jnp.sum(arriving, axis=0, keepdims=True)
    total = arriving + norm_back(grad, scaled, inverse, vec[1:2, :])
    grad_middle[...] = total
    low = total.astype(BF)
    branch[...] = low
    sums[2:3, :] = jnp.sum(low.astype(F32), axis=0, keepdims=True)
    finish(handles)
    work[...] = mmt(branch[...], w[...]).astype(BF)
    half = work.shape[1] // 2
    mixed_own[...] = work[:, at(y, half)]
    mixed_near[...] = work[:, at(1 - y, half)]


def qkv_back_kernel(n, pieces, ids, near, far, *refs):
    weights, (own, other), (w, grads, sems) = split(refs, pieces, 2)
    wide = near.shape[2]
    copies = column_copies(weights, w, ids, n, relative=True)
    for s in range(4):
        source = (near if s < 2 else far).at[s % 2]
        copies.append((source, grads.at[:, pl.ds(s * wide, wide)]))
    finish(fetch(copies, sems))
    rows = own.shape[0]
    step_rows = 256

    def step(i, carry):
        here = at(i, step_rows)
        value = mmt(grads[...], w[here, :])
        own[:, here] = value[:rows, :]
        other[:, here] = value[rows:, :].astype(BF)
        return carry

    lax.fori_loop(0, w.shape[0] // step_rows, step, 0)


def tokens_back_kernel(grad_own, grad_recv, tokens, grad_middle, vec, out, sums):
    grad = grad_own[...] + grad_recv[...].astype(F32)
    scaled, inverse = normalize(tokens[...].astype(F32))
    sums[0:1, :] = jnp.sum(grad * scaled, axis=0, keepdims=True)
    sums[1:2, :] = jnp.sum(grad, axis=0, keepdims=True)
    total = grad_middle[...] + norm_back(grad, scaled, inverse, vec[0:1, :])
    out[...] = total.astype(BF)[: out.shape[0], :]


def weight_kernel(lefts, rights, left_slot, right_slot, *refs):
    left_refs, right_refs, (out,), (a, b, sems) = split(refs, lefts, rights, 1)
    copies = []
    for parts, target, slot in ((left_refs, a, left_slot), (right_refs, b, right_slot)):
        start = 0
        for part in parts:
            source = part if slot is None else part.at[slot]
            count = source.shape[0]
            copies.append((source, target.at[pl.ds(start, count), :]))
            start += count
    finish(fetch(copies, sems))
    step_rows = 256

    def step(i, carry):
        here = at(i, step_rows)
        out[here, :] = tmm(a[:, here], b[...]).astype(out.dtype)
        return carry

    lax.fori_loop(0, out.shape[0] // step_rows, step, 0)


def weight_grad(left, right, left_slot, right_slot, dtype, name):
    def span(parts, slot):
        dims = [p.shape if slot is None else p.shape[1:] for p in parts]
        return sum(d[0] for d in dims), dims[0][1]

    depth, rows = span(left, left_slot)
    _, columns = span(right, right_slot)
    return call(
        functools.partial(weight_kernel, len(left), len(right), left_slot, right_slot),
        [*left, *right],
        [ANY] * (len(left) + len(right)),
        [shape((rows, columns), dtype)],
        [
            pltpu.VMEM((depth, rows), BF),
            pltpu.VMEM((depth, columns), BF),
            pltpu.SemaphoreType.DMA((len(left) + len(right),)),
        ],
        2 * depth * rows * columns,
        name,
    )[0]


def out_grad_kernel(ids, mixed, mixed_far, branch, branch_far, send, keep, a, b, sems):
    r, y = ids[0], ids[1]
    rows = mixed.shape[0]
    half = branch.shape[1] // 2
    quarters = half // LANES
    copies = []
    for i, (left, right) in enumerate(((mixed, branch), (mixed_far, branch_far))):
        here = pl.ds(i * rows, rows)
        copies.append((left, a.at[here, :]))
        for s, (dy, d) in enumerate(((1, 2), (1, 0), (0, 2), (0, 0))):
            block = flip(y, dy) * quarters + flip(r, d)
            copies.append((right.at[:, at(block, LANES)], b.at[here, pl.ds(s * LANES, LANES)]))
    finish(fetch(copies, sems))
    step_rows = 256

    def step(i, carry):
        here = at(i, step_rows)
        value = tmm(a[:, here], b[...])
        send[here, :] = value[:, : 2 * LANES].astype(BF)
        keep[here, :] = value[:, 2 * LANES :]
        return carry

    lax.fori_loop(0, a.shape[1] // step_rows, step, 0)


def combine_kernel(n, ids, keep, recv, own, *sends):
    z = ids[2]
    rows = own.shape[0]
    for k in range(n):
        here = at(lax.rem(z + k, n), rows)
        value = keep[here, :] + recv[here, :].astype(F32)
        if k:
            sends[k - 1][...] = value.astype(BF)
        else:
            own[...] = value


def place_kernel(kind, ids, *refs):
    pieces, (out,), _ = split(refs, 8, 1)
    r, y = ids[0], ids[1]
    for dy in range(2):
        for d in range(4):
            piece = pieces[dy * 4 + d]
            block = flip(y, dy) * 4 + flip(r, d)
            if kind == "rows":
                out[at(block, piece.shape[0]), :] = piece[...].astype(F32)
                continue
            groups = piece.shape[1] // LANES
            for g in range(groups):
                columns = at(block + g * 8, LANES)
                out[:, columns] = piece[:, g * LANES : (g + 1) * LANES].astype(F32)


def on_device(sizes, tokens, slot_mask, cotangent, w_qkv, w_out, w_fc1, w_fc2, ln_gains, biases, fc1_bias):
    n, reps, seqs = sizes
    slot_count, real, wide = tokens.shape
    assert slot_count == 1 and reps == 4 and seqs == 2
    direct = n == 4
    rows = -(-real // 16) * 16
    hidden = fc1_bias.shape[0] * n
    half, part_hidden = wide // 2, hidden // 2
    h = hidden // n // 8
    r, y, z = lax.axis_index("rep"), lax.axis_index("seq"), lax.axis_index("fsdp")
    ids = jnp.stack([r, y, z]).astype(jnp.int32)

    def core(v):
        return lax.ppermute(v, "rep", [(i, i ^ 1) for i in range(reps)])

    def across(v):
        return lax.ppermute(v, "rep", [(i, i ^ 2) for i in range(reps)])

    def near(v):
        return lax.ppermute(v, "seq", [(0, 1), (1, 0)])

    def shift(v, k):
        return lax.ppermute(v, "fsdp", [(i, (i + k) % n) for i in range(n)])

    def qkv_part(start, size):
        parts = [
            lax.dynamic_slice_in_dim(w_qkv, kind * wide + y * half + start, size, axis=1)
            for kind in range(3)
        ]
        return [p.astype(BF) for p in parts]

    def qkv_half():
        parts = qkv_part(0, half)
        return jnp.concatenate(
            [p[:, i * LANES : (i + 1) * LANES] for i in range(4) for p in parts], axis=1
        )

    def fc1_half():
        grid = w_fc1.reshape(w_fc1.shape[0], n, 2, 4, h)
        grid = lax.dynamic_index_in_dim(grid, y, axis=2, keepdims=False).astype(BF)
        return grid.transpose(0, 2, 1, 3).reshape(w_fc1.shape[0], part_hidden)

    def fc1_half_direct():
        blocks = []
        for zz in range(n):
            start = zz * (hidden // n) + y * (4 * h)
            blocks.append(lax.dynamic_slice_in_dim(w_fc1, start, 4 * h, axis=1).astype(BF))
        return jnp.concatenate(
            [b[:, i * h : (i + 1) * h] for i in range(4) for b in blocks], axis=1
        )

    fc2_half = lax.dynamic_slice_in_dim(w_fc2, y * 4 * h, 4 * h, axis=0).astype(BF)
    fc2_half = fc2_half.reshape(4, h, wide)
    out_own = w_out.astype(BF)

    def gather(own, piece):
        arrays = [own]
        for k in range(1, n):
            first = shift(piece, k)
            second = across(first)
            arrays += [first, core(first), second, core(second)]
        return arrays

    if direct:
        qkv_piece = jnp.concatenate(qkv_part(r * LANES, LANES), axis=1)
        out_piece = lax.dynamic_slice_in_dim(w_out, r * (wide // 4), wide // 4, axis=1).astype(BF)
        fc1_piece = jnp.concatenate(
            [
                lax.dynamic_slice_in_dim(
                    w_fc1, zz * (hidden // n) + y * (4 * h) + r * h, h, axis=1
                ).astype(BF)
                for zz in range(n)
            ],
            axis=1,
        )
        fc2_piece = lax.dynamic_slice_in_dim(w_fc2, y * (4 * h) + r * h, h, axis=0).astype(BF)
        all_qkv = gather(qkv_half(), qkv_piece)
        all_out = gather(out_own, out_piece)
        all_fc1 = gather(fc1_half_direct(), fc1_piece)
        all_fc2 = gather(fc2_half, fc2_piece)
    else:
        whole = functools.partial(lax.all_gather, axis_name="fsdp", axis=0, tiled=True)
        all_qkv, all_out, all_fc1 = [whole(qkv_half())], [whole(out_own)], [whole(fc1_half())]
        everyone = lax.all_gather(fc2_half, "fsdp", axis=1, tiled=True)
        all_fc2 = [everyone.reshape(part_hidden, wide)]

    small = jnp.concatenate(
        [ln_gains, biases, fc1_bias.reshape(hidden // wide, wide // n)], axis=0
    ).astype(BF)
    if direct:
        gathered = jnp.zeros((n,) + small.shape, BF)
        for k in range(n):
            block = shift(small, k) if k else small
            gathered = lax.dynamic_update_slice_in_dim(
                gathered, block[None], lax.rem(z - k + n, n), axis=0
            )
    else:
        gathered = lax.all_gather(small, "fsdp", axis=0)
    gathered = gathered.astype(F32)
    vec = gathered[:, :8].transpose(1, 0, 2).reshape(8, wide)
    hidden_shift = gathered[:, 8:].reshape(n, 2, 4, h)
    hidden_shift = lax.dynamic_index_in_dim(hidden_shift, y, axis=1, keepdims=False)
    hidden_shift = hidden_shift.transpose(1, 0, 2).reshape(1, part_hidden)
    query_shift = lax.dynamic_slice(vec, (3, y * half), (1, half))
    value_shift = lax.dynamic_slice(vec, (4, y * half), (1, half))

    pad = ((0, rows - real), (0, 0))
    tok = jnp.pad(tokens[0], pad)
    tok_near = near(tok)
    positions = y * real + jnp.arange(real)
    keep = slot_mask.astype(F32)[0] * (positions < IMG_TOK).astype(F32)
    keep = keep[:, None]
    grads = jnp.pad((cotangent[0].astype(F32) * keep).astype(BF), pad)
    grads_near = near(grads)
    grads_far, grads_near_far = core(grads), core(grads_near)

    count = len(all_qkv)
    sems = lambda c: pltpu.SemaphoreType.DMA((c,))
    two = 2 * rows
    normed, queries, keys, values = call(
        functools.partial(qkv_kernel, n, count),
        [ids, tok, tok_near, vec, query_shift, value_shift, *all_qkv],
        [SM] + [VM] * 5 + [ANY] * count,
        [shape((two, wide), BF)] + [shape((two, half), BF)] * 3,
        [pltpu.VMEM((wide, 3 * half), BF), sems(count + 8)],
        2 * two * wide * 3 * half,
        "qkv",
    )
    normed_far = core(normed)
    mixed_own, mixed_send = attend(ids, queries, keys, values, rows, real)
    mixed_recv = near(mixed_send)
    mixed, middle, normed_two = call(
        functools.partial(project_kernel, n, count),
        [ids, tok, mixed_own, mixed_recv, vec, *all_out],
        [SM] + [VM] * 4 + [ANY] * count,
        [shape((rows, wide), BF), shape((rows, wide), F32), shape((rows, wide), BF)],
        [pltpu.VMEM((wide, wide), BF), sems(count + 8)],
        2 * rows * wide * wide,
        "project",
    )
    normed_two_near = near(normed_two)
    pair = (2, two, part_hidden // 4)
    act_near, act_far, gh_near, gh_far, gtwo_own, gtwo_send, hidden_sums = call(
        functools.partial(mlp_kernel, n, count, count),
        [ids, normed_two, normed_two_near, grads, grads_near, hidden_shift, *all_fc1, *all_fc2],
        [SM] + [VM] * 5 + [ANY] * (2 * count),
        [shape(pair, BF)] * 4
        + [shape((rows, wide), F32), shape((rows, wide), BF), shape((1, part_hidden), F32)],
        [
            pltpu.VMEM((wide, part_hidden), BF),
            pltpu.VMEM((part_hidden, wide), BF),
            pltpu.VMEM((two, wide), BF),
            pltpu.VMEM((two, wide), BF),
            pltpu.VMEM((two, wide), F32),
            sems(2 * count + 16),
        ],
        6 * two * wide * part_hidden,
        "mlp",
    )
    gtwo_recv = near(gtwo_send)
    act_other, gh_other = core(act_far), core(gh_far)
    normed_two_far, normed_two_near_far = core(normed_two), core(normed_two_near)
    mixed_far = core(mixed)

    result_own, result_send = call(
        functools.partial(result_kernel, n, count),
        [ids, act_near, act_far, *all_fc2],
        [SM] + [VM] * 2 + [ANY] * count,
        [shape((rows, wide), F32), shape((rows, wide), BF)],
        [
            pltpu.VMEM((part_hidden, wide), BF),
            pltpu.VMEM((two, wide), F32),
            sems(count + 8),
        ],
        2 * two * wide * part_hidden,
        "result",
    )
    result_recv = near(result_send)
    total = middle[:real] + (
        result_own[:real] + result_recv[:real].astype(F32) + vec[7:8, :]
    )
    output = (total * keep).astype(BF)[None]

    def reduce_plane(make):
        sent = across(make(1, BF))
        return make(0, F32), sent

    def reduce_rows(kept, received):
        count_rows = kept.shape[0] // n
        if direct:
            outs = [shape((count_rows, kept.shape[1]), F32)]
            outs += [shape((count_rows, kept.shape[1]), BF)] * (n - 1)
            mine, *sends = call(
                functools.partial(combine_kernel, n),
                [ids, kept, received],
                [SM, VM, VM],
                outs,
                [],
                kept.size,
                "combine",
            )
            total = mine
            for k in range(1, n):
                total = total + shift(sends[k - 1], k).astype(F32)
            return total.astype(BF)
        summed = (kept + received.astype(F32)).astype(BF)
        return lax.psum_scatter(summed, "fsdp", scatter_dimension=0, tiled=True)

    def spread(piece, dims, kind):
        pieces = [piece, near(piece)]
        pieces = [[p, across(p)] for p in pieces]
        pieces = [[a, core(a), b, core(b)] for a, b in pieces]
        flat = pieces[0] + pieces[1]
        if direct:
            return call(
                functools.partial(place_kernel, kind),
                [ids, *flat],
                [SM] + [VM] * 8,
                [shape(dims, F32)],
                [],
                dims[0] * dims[1],
                "place",
            )[0]
        stack = jnp.stack(flat)
        order = (jnp.bitwise_xor(jnp.arange(2), y) * 4)[:, None]
        order = (order + jnp.bitwise_xor(jnp.arange(4), r)[None, :]).reshape(-1)
        stack = jnp.take(stack, order, axis=0).astype(F32)
        if kind == "rows":
            return stack.reshape(dims)
        groups = dims[1] // (8 * min(h, LANES)) if kind == "hidden" else dims[1] // (8 * LANES)
        stack = stack.reshape(8, dims[0], groups, -1)
        return stack.transpose(1, 2, 0, 3).reshape(dims)

    grad_fc2 = spread(
        reduce_rows(
            *reduce_plane(
                lambda s, t: weight_grad(
                    [act_near, act_other],
                    [grads, grads_near, grads_far, grads_near_far],
                    s,
                    None,
                    t,
                    "grad_fc2",
                )
            )
        ),
        w_fc2.shape,
        "rows",
    )
    grad_fc1 = spread(
        reduce_rows(
            *reduce_plane(
                lambda s, t: weight_grad(
                    [normed_two, normed_two_near, normed_two_far, normed_two_near_far],
                    [gh_near, gh_other],
                    None,
                    s,
                    t,
                    "grad_fc1",
                )
            )
        ),
        w_fc1.shape,
        "hidden",
    )

    grad_middle, branch, gmix_own, gmix_send, sums_two = call(
        functools.partial(middle_back_kernel, n, count),
        [ids, gtwo_own, gtwo_recv, middle, grads, vec, *all_out],
        [SM] + [VM] * 5 + [ANY] * count,
        [
            shape((rows, wide), F32),
            shape((rows, wide), BF),
            shape((rows, half), BF),
            shape((rows, half), BF),
            shape((4, wide), F32),
        ],
        [pltpu.VMEM((wide, wide), BF), pltpu.VMEM((rows, wide), BF), sems(count + 8)],
        2 * rows * wide * wide,
        "middle_back",
    )
    gmix_recv = near(gmix_send)
    branch_far = core(branch)
    gj_near, gj_far, joined_sums = attend_back(
        ids, queries, keys, values, gmix_own, gmix_recv, rows, real
    )
    gj_other = core(gj_far)
    gone_own, gone_send = call(
        functools.partial(qkv_back_kernel, n, count),
        [ids, gj_near, gj_far, *all_qkv],
        [SM] + [ANY] * (2 + count),
        [shape((rows, wide), F32), shape((rows, wide), BF)],
        [
            pltpu.VMEM((wide, 3 * half), BF),
            pltpu.VMEM((two, 3 * half), BF),
            sems(count + 16),
        ],
        2 * two * wide * 3 * half,
        "qkv_back",
    )
    gone_recv = near(gone_send)
    grad_qkv = spread(
        reduce_rows(
            *reduce_plane(
                lambda s, t: weight_grad(
                    [normed, normed_far], [gj_near, gj_other], None, s, t, "grad_qkv"
                )
            )
        ),
        w_qkv.shape,
        "columns",
    )
    out_send, out_keep = call(
        out_grad_kernel,
        [ids, mixed, mixed_far, branch, branch_far],
        [SM] + [ANY] * 4,
        [shape((wide, 2 * LANES), BF), shape((wide, 2 * LANES), F32)],
        [pltpu.VMEM((two, wide), BF), pltpu.VMEM((two, 4 * LANES), BF), sems(10)],
        2 * two * wide * 4 * LANES,
        "grad_out",
    )
    out_recv = near(out_send).astype(F32)
    out_sum = out_keep + out_recv
    out_cross = across(out_sum[:, :LANES].astype(BF))
    grad_out = spread(reduce_rows(out_sum[:, LANES:], out_cross), w_out.shape, "columns")

    grad_tokens, sums_one = call(
        tokens_back_kernel,
        [gone_own, gone_recv, tok, grad_middle, vec],
        [VM] * 5,
        [shape((real, wide), BF), shape((2, wide), F32)],
        [],
        rows * wide,
        "tokens_back",
    )
    grad_tokens = grad_tokens[None]

    wanted = jnp.bitwise_xor(jnp.arange(4), r)
    slots = ((wanted & 1) << 1) | (wanted >> 1)
    chosen = (slots[:, None] == jnp.arange(4)[None, :]).astype(F32)
    joined_sums = jnp.sum(chosen[:, :, None] * joined_sums[None, :, 0, :], axis=1)
    here = (jnp.arange(2) == y).astype(F32)

    def spread_half(row):
        return (here[:, None] * row.reshape(1, half)).reshape(1, wide)

    query_sums = spread_half(joined_sums[:, :LANES])
    value_sums = spread_half(joined_sums[:, 2 * LANES :])
    hidden_sums = hidden_sums.reshape(4, n, h).transpose(1, 0, 2).reshape(n, 1, 4 * h)
    hidden_sums = (hidden_sums * here[None, :, None]).reshape(hidden // wide, wide)
    block = jnp.concatenate(
        [
            sums_one[0:1],
            sums_two[0:1],
            sums_one[1:2],
            query_sums,
            value_sums,
            sums_two[2:3],
            sums_two[1:2],
            sums_two[3:4],
            hidden_sums,
        ],
        axis=0,
    )
    if direct:
        block = block + core(block)
        block = block + near(block)
        block = block + across(block)
        total = block
        for k in range(1, n):
            total = total + shift(block, k)
        block = total
    else:
        block = lax.psum(block, ("rep", "seq", "fsdp"))
    narrow = lax.dynamic_slice_in_dim(block[:8], z * (wide // n), wide // n, axis=1)
    flat = lax.dynamic_slice_in_dim(block[8:].reshape(-1), z * (hidden // n), hidden // n)
    return (
        output,
        grad_tokens,
        grad_qkv,
        grad_out,
        grad_fc1,
        grad_fc2,
        narrow[:2],
        narrow[2:],
        flat,
    )


def solution(mesh):
    sizes = (mesh.shape["fsdp"], mesh.shape["rep"], mesh.shape["seq"])
    return jax.shard_map(
        functools.partial(on_device, sizes),
        mesh=mesh,
        in_specs=(
            P(("rep", "fsdp"), "seq", None),
            P(("rep", "fsdp")),
            P(("rep", "fsdp"), "seq", None),
            P("fsdp", None),
            P("fsdp", None),
            P("fsdp", None),
            P("fsdp", None),
            P(None, "fsdp"),
            P(None, "fsdp"),
            P("fsdp"),
        ),
        out_specs=(
            P(("rep", "fsdp"), "seq", None),
            P(("rep", "fsdp"), "seq", None),
            P("fsdp", None),
            P("fsdp", None),
            P("fsdp", None),
            P("fsdp", None),
            P(None, "fsdp"),
            P(None, "fsdp"),
            P("fsdp"),
        ),
        check_vma=False,
    )
```

time: 1240 us -> 515 us (0.42)
  waiting for transfers between devices: 963 us -> 183 us
  Pallas kernels: 0 us -> 147 us
  starting transfers between devices: 1.09 us -> 120 us
  matrix products: 109 us -> 0 us
  blocking collectives: 64.3 us -> 0 us
  other arithmetic: 41.2 us -> 10.5 us
  between operations: 16.1 us -> 3.43 us
    reduce_scatter x5 -> x0, waiting for transfers between devices: 433 us -> none  [the longest x1 148 us: on_device(): lax.psum_scatter(grad_fc1.astype(jnp.bfloat16), 'fsdp', scatter_dimension...]
    all_gather x6 -> x0, waiting for transfers between devices: 432 us -> none  [the longest x1 147 us: on_device(): lax.all_gather(low_fc1, 'fsdp', axis=0, tiled=True)]
    ppermute x0 -> x120, waiting for transfers between devices: none -> 183 us  [the longest x25 68.4 us: across(): return lax.ppermute(v, 'rep', [(i, i ^ 2) for i in range(reps)])]
    pallas_call x0 -> x24, Pallas kernels: none -> 147 us  [the longest x22 118 us: call(): pl.pallas_call(body, out_shape=outs, in_specs=specs, out_specs=out_specs...]
    ppermute x0 -> x120, starting transfers between devices: none -> 120 us  [the longest x30 74.3 us: shift(): return lax.ppermute(v, 'fsdp', [(i, (i + k) % n) for i in range(n)])]
    dot_general x18 -> x0, matrix products: 109 us -> none  [the longest x4 29.9 us: across_rows(): lax.dot_general(left_rows, right_rows, (((0,), (0,)), ((), ())), preferre...]
    psum x1 -> x0, waiting for transfers between devices: 91.1 us -> none  [on_device(): lax.psum(shards[0].astype(jnp.bfloat16), ('rep', 'seq')).astype(jnp.float32)]
    all_gather x3 -> x0, blocking collectives: 38.8 us -> none  [the longest x1 14.3 us: on_device(): lax.all_gather(low_biases, 'fsdp', axis=1, tiled=True)]
  transfers between devices with their start and end apart: 15 -> 120, of which waited for: 12 -> 28; matrix products, arithmetic and copies ran while one was open for 11% -> 9% of each run, Pallas kernels for 0% -> 25%
where the time goes in v1:
time: 515 us; the launch traced here: 508 us
  waiting for transfers between devices  183 us (36%)
  Pallas kernels  147 us (29%)
  starting transfers between devices  120 us (23%)
  local copies, waits for them, and re-layouts  44.6 us (9%)
  other arithmetic  10.5 us (2%)
    pallas_call x22, Pallas kernels, call(): pl.pallas_call(body, out_shape=outs, in_specs=specs, out_specs=out_specs...  118 us
    ppermute x30, starting transfers between devices, shift(): return lax.ppermute(v, 'fsdp', [(i, (i + k) % n) for i in range(n)])  74.3 us
    ppermute x25, waiting for transfers between devices, across(): return lax.ppermute(v, 'rep', [(i, i ^ 2) for i in range(reps)])  68.4 us
    ppermute x30, waiting for transfers between devices, shift(): return lax.ppermute(v, 'fsdp', [(i, (i + k) % n) for i in range(n)])  56.9 us
    ppermute x14, waiting for transfers between devices, near(): return lax.ppermute(v, 'seq', [(0, 1), (1, 0)])  56.8 us
    unnamed x252, local copies, waits for them, and re-layouts  25.2 us
    ppermute x25, starting transfers between devices, across(): return lax.ppermute(v, 'rep', [(i, i ^ 2) for i in range(reps)])  25.1 us
    pallas_call x1, Pallas kernels, attend_back(): pl.pallas_call(functools.partial(attend_back_kernel, rows, real), grid_sp...  19.7 us
  transfers between devices with their start and end apart: 120, of which 28 were waited for; matrix products, arithmetic and copies ran while one was open for 9% of the time, Pallas kernels for 25%

profile of v1, /device:TPU:0, one launch (start us, length us, event | category | flops | bytes accessed | tf_op | source)
XLA Modules:
  0.0 508.5 jit_solution(13059859306605304595)
XLA Ops:
  43.7 5.3 %collective-permute-done.25.refs_9_ = bf16[256,256]{1,0:T(8,128)(2,1)S(1)} collective-permute-done((bf16[256,256]{1,0:T(8,128)(2,1)S(1)}, bf16[256,256]{1,0:T(8,128)(2,1)S(1)}, u32[]{:S(2)}, u32[]{:S(2)}) %collective-permute-start.25) | collective-permute-done | bytes 131104 | tf_op jit(solution)/shard_map/ppermute | solution.py:547
  70.0 16.3 %collective-permute-done.35.refs_5_ = bf16[256,512]{1,0:T(8,128)(2,1)} collective-permute-done((bf16[256,512]{1,0:T(8,128)(2,1)S(1)}, bf16[256,512]{1,0:T(8,128)(2,1)}, u32[]{:S(2)}, u32[]{:S(2)}) %collective-permute-start.35) | collective-permute-done | bytes 262176 | tf_op jit(solution)/shard_map/ppermute | solution.py:547
  86.8 12.3 %collective-permute-done.47.refs_18_.refs_5_ = bf16[128,1024]{1,0:T(8,128)(2,1)} collective-permute-done((bf16[128,1024]{1,0:T(8,128)(2,1)}, bf16[128,1024]{1,0:T(8,128)(2,1)}, u32[]{:S(2)}, u32[]{:S(2)}) %collective-permute-start.47) | collective-permute-done | bytes 262176 | tf_op jit(solution)/shard_map/ppermute | solution.py:547
  127.8 8.0 %qkv.1 = (bf16[608,1024]{1,0:T(8,128)(2,1)}, bf16[608,512]{1,0:T(8,128)(2,1)}, bf16[608,512]{1,0:T(8,128)(2,1)}, bf16[608,512]{1,0:T(8,128)(2,1)}) custom-call(s32[3]{0:T(128)} %pad_add_fusion.ids, bf16[304,1024]{1,0:T(8,128)(2,1)} %copy-done.2, bf16[304,1024]{1,0:T(8,128)(2,1)} %copy-done.80, f32[8,1024]{1,0:T(8,128)} %bitcast.67, ...), custom_call_target="tpu_custom_call" | custom-call | flops 1912602624 | bytes 7540748 | tf_op jit(solution)/shard_map/qkv/pallas_call | solution.py:76
  136.5 10.0 %attend.1 = (bf16[304,512]{1,0:T(8,128)(2,1)}, bf16[304,512]{1,0:T(8,128)(2,1)}) custom-call(s32[3]{0:T(128)} %pad_add_fusion.ids, bf16[608,512]{1,0:T(8,128)(2,1)} %get-tuple-element.57.queries, bf16[608,512]{1,0:T(8,128)(2,1)} %get-tuple-element.58.keys, bf16[608,512]{1,0:T(8,128)(2,1)} %get-tuple-element.59.values), custom_call_target="tpu_custom_call" | custom-call | flops 1514143744 | bytes 2490368 | tf_op jit(solution)/shard_map/attend/pallas_call | solution.py:201
  156.6 12.7 %collective-permute-done.16.mixed_near = bf16[304,512]{1,0:T(8,128)(2,1)S(1)} collective-permute-done((bf16[304,512]{1,0:T(8,128)(2,1)}, bf16[304,512]{1,0:T(8,128)(2,1)S(1)}, u32[]{:S(2)}, u32[]{:S(2)}) %collective-permute-start.16) | collective-permute-done | bytes 311328 | tf_op jit(solution)/shard_map/ppermute | solution.py:544
  182.2 9.0 %collective-permute-done.29.n_near.refs_1_ = bf16[304,1024]{1,0:T(8,128)(2,1)} collective-permute-done((bf16[304,1024]{1,0:T(8,128)(2,1)}, bf16[304,1024]{1,0:T(8,128)(2,1)}, u32[]{:S(2)}, u32[]{:S(2)}) %collective-permute-start.29) | collective-permute-done | bytes 622624 | tf_op jit(solution)/shard_map/ppermute | solution.py:544
  191.3 18.3 %mlp.1 = (bf16[2,608,512]{2,1,0:T(8,128)(2,1)}, bf16[2,608,512]{2,1,0:T(8,128)(2,1)}, bf16[2,608,512]{2,1,0:T(8,128)(2,1)}, bf16[2,608,512]{2,1,0:T(8,128)(2,1)}...) custom-call(s32[3]{0:T(128)} %pad_add_fusion.ids, ...), custom_call_target="tpu_custom_call" | custom-call | flops 7650410496 | bytes 17743884 | tf_op jit(solution)/shard_map/mlp/pallas_call | solution.py:76
  210.9 13.9 %collective-permute-done.56.grad_recv = bf16[304,1024]{1,0:T(8,128)(2,1)S(1)} collective-permute-done((bf16[304,1024]{1,0:T(8,128)(2,1)}, bf16[304,1024]{1,0:T(8,128)(2,1)S(1)}, u32[]{:S(2)}, u32[]{:S(2)}) %collective-permute-start.56) | collective-permute-done | bytes 622624 | tf_op jit(solution)/shard_map/ppermute | solution.py:544
  225.6 5.5 %middle_back.1 = (f32[304,1024]{1,0:T(8,128)}, bf16[304,1024]{1,0:T(8,128)(2,1)}, bf16[304,512]{1,0:T(8,128)(2,1)}, bf16[304,512]{1,0:T(8,128)(2,1)}, f32[4,1024]{1,0:T(4,128)}) custom-call(s32[3]{0:T(128)} %pad_add_fusion.ids, f32[304,1024]{1,0:T(8,128)} %get-tuple-element.68.grad_own, bf16[304,1024]{1,0:T(8,128)(2,1)} %copy-done.26, ...), custom_call_target="tpu_custom_call" | custom-call | flops 637534208 | bytes 8372236 | tf_op jit(solution)/shard_map/middle_back/pallas_call | solution.py:76
  232.6 6.0 %collective-permute-done.57.grad_near = bf16[304,512]{1,0:T(8,128)(2,1)S(1)} collective-permute-done((bf16[304,512]{1,0:T(8,128)(2,1)}, bf16[304,512]{1,0:T(8,128)(2,1)S(1)}, u32[]{:S(2)}, u32[]{:S(2)}) %collective-permute-start.57) | collective-permute-done | bytes 311328 | tf_op jit(solution)/shard_map/ppermute | solution.py:544
  239.3 19.7 %attend_back.1 = (bf16[2,608,384]{2,1,0:T(8,128)(2,1)}, bf16[2,608,384]{2,1,0:T(8,128)(2,1)}, f32[4,1,384]{2,1,0:T(1,128)}) custom-call(s32[3]{0:T(128)} %pad_add_fusion.ids, bf16[608,512]{1,0:T(8,128)(2,1)} %get-tuple-element.57.queries, bf16[608,512]{1,0:T(8,128)(2,1)} %get-tuple-element.58.keys, bf16[608,512]{1,0:T(8,128)(2,1)} %get-tuple-element.59.values, ...), custom_call_target="tpu_custom_call" | custom-call | flops 3785359360 | bytes 4980736 | tf_op jit(solution)/shard_map/attend_back/pallas_call | solution.py:274
  259.2 7.5 %qkv_back.1 = (f32[304,1024]{1,0:T(8,128)}, bf16[304,1024]{1,0:T(8,128)(2,1)}) custom-call(s32[3]{0:T(128)} %pad_add_fusion.ids, bf16[2,608,384]{2,1,0:T(8,128)(2,1)} %get-tuple-element.72.near.refs_2_, bf16[2,608,384]{2,1,0:T(8,128)(2,1)} %get-tuple-element.73.far, bf16[256,1536]{1,0:T(8,128)(2,1)} %slice_dynamic-update-slice_fusion.16.refs_0_, ...), custom_call_target="tpu_custom_call" | custom-call | flops 1912602624 | bytes 6881292 | tf_op jit(solution)/shard_map/qkv_back/pallas_call | solution.py:76
  273.3 10.1 %collective-permute-done.58.grad_recv = bf16[304,1024]{1,0:T(8,128)(2,1)S(1)} collective-permute-done((bf16[304,1024]{1,0:T(8,128)(2,1)}, bf16[304,1024]{1,0:T(8,128)(2,1)S(1)}, u32[]{:S(2)}, u32[]{:S(2)}) %collective-permute-start.58) | collective-permute-done | bytes 622624 | tf_op jit(solution)/shard_map/ppermute | solution.py:544
  295.9 5.4 %grad_fc1.3 = bf16[1024,512]{1,0:T(8,128)(2,1)} custom-call(bf16[304,1024]{1,0:T(8,128)(2,1)} %get-tuple-element.63.n_own.refs_0_, bf16[304,1024]{1,0:T(8,128)(2,1)} %collective-permute-done.29.n_near.refs_1_, bf16[304,1024]{1,0:T(8,128)(2,1)} %collective-permute-done.86.refs_2_, bf16[304,1024]{1,0:T(8,128)(2,1)} %collective-permute-done.87.refs_3_, ...), custom_call_target="tpu_custom_call" | custom-call | flops 1275068416 | bytes 6029312 | tf_op jit(solution)/shard_map/grad_fc1/pallas_call | solution.py:76
  307.2 7.9 %result.1 = (f32[304,1024]{1,0:T(8,128)}, bf16[304,1024]{1,0:T(8,128)(2,1)}) custom-call(s32[3]{0:T(128)} %pad_add_fusion.ids, bf16[2,608,512]{2,1,0:T(8,128)(2,1)} %get-tuple-element.64.act_near.refs_0_, bf16[2,608,512]{2,1,0:T(8,128)(2,1)} %get-tuple-element.65.act_far, bf16[4,128,1024]{2,1,0:T(8,128)(2,1)} %bitcast.64, bf16[128,1024]{1,0:T(8,128)(2,1)} %copy-done.82, ...), custom_call_target="tpu_custom_call" | custom-call | flops 2550136832 | bytes 8552460 | tf_op jit(solution)/shard_map/result/pallas_call | solution.py:76
  317.0 31.5 %collective-permute-done.75.recv = bf16[1024,128]{1,0:T(8,128)(2,1)S(1)} collective-permute-done((bf16[1024,128]{1,0:T(8,128)(2,1)S(1)}, bf16[1024,128]{1,0:T(8,128)(2,1)S(1)}, u32[]{:S(2)}, u32[]{:S(2)}) %collective-permute-start.75) | collective-permute-done | bytes 262176 | tf_op jit(solution)/shard_map/ppermute | solution.py:541
  352.8 5.4 %collective-permute-start.76 = (bf16[256,128]{1,0:T(8,128)(2,1)}, bf16[256,128]{1,0:T(8,128)(2,1)S(1)}, u32[]{:S(2)}, u32[]{:S(2)}) collective-permute-start(bf16[256,128]{1,0:T(8,128)(2,1)} %get-tuple-element.88), channel_id=1, source_target_pairs={{0,2},{2,4},{4,6},{6,0},{1,3},{3,5},{5,7},{7,1},{8,10},{10,12},{12... | collective-permute-start | bytes 196616 | tf_op jit(solution)/shard_map/ppermute | solution.py:547
  363.7 5.7 %collective-permute-done.77 = bf16[256,128]{1,0:T(8,128)(2,1)S(1)} collective-permute-done((bf16[256,128]{1,0:T(8,128)(2,1)}, bf16[256,128]{1,0:T(8,128)(2,1)S(1)}, u32[]{:S(2)}, u32[]{:S(2)}) %collective-permute-start.77) | collective-permute-done | bytes 65568 | tf_op jit(solution)/shard_map/ppermute | solution.py:547
  383.1 5.3 %grad_qkv.3 = bf16[1024,384]{1,0:T(8,128)(2,1)} custom-call(bf16[608,1024]{1,0:T(8,128)(2,1)} %get-tuple-element.78.refs_0_, bf16[608,1024]{1,0:T(8,128)(2,1)} %copy-done.4, bf16[2,608,384]{2,1,0:T(8,128)(2,1)} %get-tuple-element.72.near.refs_2_, bf16[2,608,384]{2,1,0:T(8,128)(2,1)} %copy-done.7), custom_call_target="tpu_custom_call" | custom-call | flops 956301312 | bytes 5144576 | tf_op jit(solution)/shard_map/grad_qkv/pallas_call | solution.py:76
  407.8 6.0 %grad_fc1.2.keep = f32[1024,512]{1,0:T(8,128)} custom-call(bf16[304,1024]{1,0:T(8,128)(2,1)} %get-tuple-element.63.n_own.refs_0_, bf16[304,1024]{1,0:T(8,128)(2,1)} %collective-permute-done.29.n_near.refs_1_, bf16[304,1024]{1,0:T(8,128)(2,1)} %collective-permute-done.86.refs_2_, bf16[304,1024]{1,0:T(8,128)(2,1)} %collective-permute-done.87.refs_3_, ...), custom_call_target="tpu_custom_call" | custom-call | flops 1275068416 | bytes 7077888 | tf_op jit(solution)/shard_map/grad_fc1/pallas_call | solution.py:76
  424.0 14.9 %collective-permute-start.92 = (bf16[256,512]{1,0:T(8,128)(2,1)}, bf16[256,512]{1,0:T(8,128)(2,1)S(1)}, u32[]{:S(2)}, u32[]{:S(2)}) collective-permute-start(bf16[256,512]{1,0:T(8,128)(2,1)} %get-tuple-element.96), channel_id=1, source_target_pairs={{0,6},{2,0},{4,2},{6,4},{1,7},{3,1},{5,3},{7,5},{8,14},{10,8},{12,... | collective-permute-start | bytes 786440 | tf_op jit(solution)/shard_map/ppermute | solution.py:547
  440.3 5.5 %grad_qkv.2.keep = f32[1024,384]{1,0:T(8,128)} custom-call(bf16[608,1024]{1,0:T(8,128)(2,1)} %get-tuple-element.78.refs_0_, bf16[608,1024]{1,0:T(8,128)(2,1)} %copy-done.4, bf16[2,608,384]{2,1,0:T(8,128)(2,1)} %get-tuple-element.72.near.refs_2_, bf16[2,608,384]{2,1,0:T(8,128)(2,1)} %copy-done.7), custom_call_target="tpu_custom_call" | custom-call | flops 956301312 | bytes 5931008 | tf_op jit(solution)/shard_map/grad_qkv/pallas_call | solution.py:76
  460.1 7.7 %collective-permute-done.63 = bf16[256,384]{1,0:T(8,128)(2,1)} collective-permute-done((bf16[256,384]{1,0:T(8,128)(2,1)}, bf16[256,384]{1,0:T(8,128)(2,1)}, u32[]{:S(2)}, u32[]{:S(2)}) %collective-permute-start.63) | collective-permute-done | bytes 196640 | tf_op jit(solution)/shard_map/ppermute | solution.py:547
  (557 shorter events, 255.4 us)
Async XLA Ops:
  2.7 29.2 %collective-permute-start.1 = (bf16[12,256]{1,0:T(8,128)(2,1)S(1)}, bf16[12,256]{1,0:T(8,128)(2,1)S(1)}, u32[]{:S(2)}, u32[]{:S(2)}) collective-permute-start(bf16[12,256]{1,0:T(8,128)(2,1)S(1)} %pad_maximum_fusion.2), channel_id=1, source_target_pairs={{0,2},{2,4},{4,6},{6,0},{1,3},{3,5},{5,7},{7,1},{8,10},{10,12},{12... | collective-permute-start | bytes 18440 | tf_op jit(solution)/shard_map/ppermute | solution.py:547
  5.8 28.8 %collective-permute-start.2 = (bf16[12,256]{1,0:T(8,128)(2,1)S(1)}, bf16[12,256]{1,0:T(8,128)(2,1)S(1)}, u32[]{:S(2)}, u32[]{:S(2)}) collective-permute-start(bf16[12,256]{1,0:T(8,128)(2,1)S(1)} %pad_maximum_fusion.2), channel_id=1, source_target_pairs={{0,4},{2,6},{4,0},{6,2},{1,5},{3,7},{5,1},{7,3},{8,12},{10,14},{12... | collective-permute-start | bytes 18440 | tf_op jit(solution)/shard_map/ppermute | solution.py:547
  8.4 29.3 %collective-permute-start.3 = (bf16[12,256]{1,0:T(8,128)(2,1)S(1)}, bf16[12,256]{1,0:T(8,128)(2,1)S(1)}, u32[]{:S(2)}, u32[]{:S(2)}) collective-permute-start(bf16[12,256]{1,0:T(8,128)(2,1)S(1)} %pad_maximum_fusion.2), channel_id=1, source_target_pairs={{0,6},{2,0},{4,2},{6,4},{1,7},{3,1},{5,3},{7,5},{8,14},{10,8},{12,... | collective-permute-start | bytes 18440 | tf_op jit(solution)/shard_map/ppermute | solution.py:547
  10.7 27.0 %collective-permute-start.17 = (bf16[256,256]{1,0:T(8,128)(2,1)S(1)}, bf16[256,256]{1,0:T(8,128)(2,1)S(1)}, u32[]{:S(2)}, u32[]{:S(2)}) collective-permute-start(bf16[256,256]{1,0:T(8,128)(2,1)S(1)} %dynamic-slice_convert_fusion.9), channel_id=1, source_target_pairs={{0,2},{2,4},{4,6},{6,0},{1,3},{3,5},{5,7},{7,1},{8,10},{10,12},{12... | collective-permute-start | bytes 393224 | tf_op jit(solution)/shard_map/ppermute | solution.py:547
  11.5 30.1 %collective-permute-start.21 = (bf16[256,256]{1,0:T(8,128)(2,1)S(1)}, bf16[256,256]{1,0:T(8,128)(2,1)S(1)}, u32[]{:S(2)}, u32[]{:S(2)}) collective-permute-start(bf16[256,256]{1,0:T(8,128)(2,1)S(1)} %dynamic-slice_convert_fusion.9), channel_id=1, source_target_pairs={{0,4},{2,6},{4,0},{6,2},{1,5},{3,7},{5,1},{7,3},{8,12},{10,14},{12... | collective-permute-start | bytes 393224 | tf_op jit(solution)/shard_map/ppermute | solution.py:547
  65.4 33.7 %collective-permute-start.47 = (bf16[128,1024]{1,0:T(8,128)(2,1)}, bf16[128,1024]{1,0:T(8,128)(2,1)}, u32[]{:S(2)}, u32[]{:S(2)}) collective-permute-start(bf16[128,1024]{1,0:T(8,128)(2,1)} %dynamic-slice_convert_fusion.1), channel_id=1, source_target_pairs={{0,4},{2,6},{4,0},{6,2},{1,5},{3,7},{5,1},{7,3},{8,12},{10,14},{12... | collective-permute-start | bytes 786440 | tf_op jit(solution)/shard_map/ppermute | solution.py:547
  66.7 33.3 %collective-permute-start.51 = (bf16[128,1024]{1,0:T(8,128)(2,1)}, bf16[128,1024]{1,0:T(8,128)(2,1)}, u32[]{:S(2)}, u32[]{:S(2)}) collective-permute-start(bf16[128,1024]{1,0:T(8,128)(2,1)} %dynamic-slice_convert_fusion.1), channel_id=1, source_target_pairs={{0,6},{2,0},{4,2},{6,4},{1,7},{3,1},{5,3},{7,5},{8,14},{10,8},{12,... | collective-permute-start | bytes 786440 | tf_op jit(solution)/shard_map/ppermute | solution.py:547
  146.5 29.9 %collective-permute-start.30 = (bf16[304,1024]{1,0:T(8,128)(2,1)S(1)}, bf16[304,1024]{1,0:T(8,128)(2,1)S(1)}, u32[]{:S(2)}, u32[]{:S(2)}) collective-permute-start(bf16[304,1024]{1,0:T(8,128)(2,1)S(1)} %pad.8.g_own.incoming.refs_2_), channel_id=1, source_target_pairs={{0,1},{1,0},{2,3},{3,2},{4,5},{5,4},{6,7},{7,6},{8,9},{9,8},{10,11... | collective-permute-start | bytes 1867784 | tf_op jit(solution)/shard_map/ppermute | solution.py:544
  210.2 48.8 %collective-permute-start.101 = (bf16[304,1024]{1,0:T(8,128)(2,1)S(1)}, bf16[304,1024]{1,0:T(8,128)(2,1)S(1)}, u32[]{:S(2)}, u32[]{:S(2)}) collective-permute-start(bf16[304,1024]{1,0:T(8,128)(2,1)S(1)} %copy-done.1), channel_id=1, source_target_pairs={{0,8},{8,0},{16,24},{24,16},{1,9},{9,1},{17,25},{25,17},{2,10},{10... | collective-permute-start | bytes 1867784 | tf_op jit(solution)/shard_map/ppermute | solution.py:538
  210.3 56.4 %collective-permute-start.102 = (bf16[304,1024]{1,0:T(8,128)(2,1)}, bf16[304,1024]{1,0:T(8,128)(2,1)S(1)}, u32[]{:S(2)}, u32[]{:S(2)}) collective-permute-start(bf16[304,1024]{1,0:T(8,128)(2,1)} %copy-done.8), channel_id=1, source_target_pairs={{0,8},{8,0},{16,24},{24,16},{1,9},{9,1},{17,25},{25,17},{2,10},{10... | collective-permute-start | bytes 1867784 | tf_op jit(solution)/shard_map/ppermute | solution.py:538
  210.8 56.6 %collective-permute-start.72 = (bf16[304,1024]{1,0:T(8,128)(2,1)S(1)}, bf16[304,1024]{1,0:T(8,128)(2,1)S(1)}, u32[]{:S(2)}, u32[]{:S(2)}) collective-permute-start(bf16[304,1024]{1,0:T(8,128)(2,1)S(1)} %copy-done.23), channel_id=1, source_target_pairs={{0,8},{8,0},{16,24},{24,16},{1,9},{9,1},{17,25},{25,17},{2,10},{10... | collective-permute-start | bytes 1867784 | tf_op jit(solution)/shard_map/ppermute | solution.py:538
  231.6 36.1 %collective-permute-start.100 = (bf16[2,608,512]{2,1,0:T(8,128)(2,1)}, bf16[2,608,512]{2,1,0:T(8,128)(2,1)S(1)}, u32[]{:S(2)}, u32[]{:S(2)}) collective-permute-start(bf16[2,608,512]{2,1,0:T(8,128)(2,1)} %get-tuple-element.65.act_far), channel_id=1, source_target_pairs={{0,8},{8,0},{16,24},{24,16},{1,9},{9,1},{17,25},{25,17},{2,10},{10... | collective-permute-start | bytes 3735560 | tf_op jit(solution)/shard_map/ppermute | solution.py:538
  238.6 57.2 %collective-permute-start.88 = (bf16[2,608,512]{2,1,0:T(8,128)(2,1)}, bf16[2,608,512]{2,1,0:T(8,128)(2,1)}, u32[]{:S(2)}, u32[]{:S(2)}) collective-permute-start(bf16[2,608,512]{2,1,0:T(8,128)(2,1)} %get-tuple-element.92), channel_id=1, source_target_pairs={{0,8},{8,0},{16,24},{24,16},{1,9},{9,1},{17,25},{25,17},{2,10},{10... | collective-permute-start | bytes 3735560 | tf_op jit(solution)/shard_map/ppermute | solution.py:538
  267.4 38.6 %collective-permute-start.59 = (bf16[608,1024]{1,0:T(8,128)(2,1)S(1)}, bf16[608,1024]{1,0:T(8,128)(2,1)S(1)}, u32[]{:S(2)}, u32[]{:S(2)}) collective-permute-start(bf16[608,1024]{1,0:T(8,128)(2,1)S(1)} %copy-done.3), channel_id=1, source_target_pairs={{0,8},{8,0},{16,24},{24,16},{1,9},{9,1},{17,25},{25,17},{2,10},{10... | collective-permute-start | bytes 3735560 | tf_op jit(solution)/shard_map/ppermute | solution.py:538
  267.8 26.9 %collective-permute-start.86 = (bf16[304,1024]{1,0:T(8,128)(2,1)S(1)}, bf16[304,1024]{1,0:T(8,128)(2,1)}, u32[]{:S(2)}, u32[]{:S(2)}) collective-permute-start(bf16[304,1024]{1,0:T(8,128)(2,1)S(1)} %copy-done.9), channel_id=1, source_target_pairs={{0,8},{8,0},{16,24},{24,16},{1,9},{9,1},{17,25},{25,17},{2,10},{10... | collective-permute-start | bytes 1867784 | tf_op jit(solution)/shard_map/ppermute | solution.py:538
  268.2 26.5 %collective-permute-start.87 = (bf16[304,1024]{1,0:T(8,128)(2,1)}, bf16[304,1024]{1,0:T(8,128)(2,1)}, u32[]{:S(2)}, u32[]{:S(2)}) collective-permute-start(bf16[304,1024]{1,0:T(8,128)(2,1)} %collective-permute-done.29.n_near.refs_1_), channel_id=1, source_target_pairs={{0,8},{8,0},{16,24},{24,16},{1,9},{9,1},{17,25},{25,17},{2,10},{10... | collective-permute-start | bytes 1867784 | tf_op jit(solution)/shard_map/ppermute | solution.py:538
  294.6 86.9 %collective-permute-start.60 = (bf16[2,608,384]{2,1,0:T(8,128)(2,1)}, bf16[2,608,384]{2,1,0:T(8,128)(2,1)S(1)}, u32[]{:S(2)}, u32[]{:S(2)}) collective-permute-start(bf16[2,608,384]{2,1,0:T(8,128)(2,1)} %get-tuple-element.73.far), channel_id=1, source_target_pairs={{0,8},{8,0},{16,24},{24,16},{1,9},{9,1},{17,25},{25,17},{2,10},{10... | collective-permute-start | bytes 2801672 | tf_op jit(solution)/shard_map/ppermute | solution.py:538
  294.6 95.8 %collective-permute-start.103 = (bf16[512,1024]{1,0:T(8,128)(2,1)}, bf16[512,1024]{1,0:T(8,128)(2,1)S(1)}, u32[]{:S(2)}, u32[]{:S(2)}) collective-permute-start(bf16[512,1024]{1,0:T(8,128)(2,1)} %grad_fc2.3), channel_id=1, source_target_pairs={{0,16},{8,24},{16,0},{24,8},{1,17},{9,25},{17,1},{25,9},{2,18},{10... | collective-permute-start | bytes 3145736 | tf_op jit(solution)/shard_map/ppermute | solution.py:541
  301.3 106.4 %collective-permute-start.89 = (bf16[1024,512]{1,0:T(8,128)(2,1)}, bf16[1024,512]{1,0:T(8,128)(2,1)S(1)}, u32[]{:S(2)}, u32[]{:S(2)}) collective-permute-start(bf16[1024,512]{1,0:T(8,128)(2,1)} %grad_fc1.3), channel_id=1, source_target_pairs={{0,16},{8,24},{16,0},{24,8},{1,17},{9,25},{17,1},{25,9},{2,18},{10... | collective-permute-start | bytes 3145736 | tf_op jit(solution)/shard_map/ppermute | solution.py:541
  306.0 42.5 %collective-permute-start.75 = (bf16[1024,128]{1,0:T(8,128)(2,1)S(1)}, bf16[1024,128]{1,0:T(8,128)(2,1)S(1)}, u32[]{:S(2)}, u32[]{:S(2)}) collective-permute-start(bf16[1024,128]{1,0:T(8,128)(2,1)S(1)} %slice.272), channel_id=1, source_target_pairs={{0,16},{8,24},{16,0},{24,8},{1,17},{9,25},{17,1},{25,9},{2,18},{10... | collective-permute-start | bytes 786440 | tf_op jit(solution)/shard_map/ppermute | solution.py:541
  315.7 59.1 %collective-permute-start.55 = (bf16[304,1024]{1,0:T(8,128)(2,1)}, bf16[304,1024]{1,0:T(8,128)(2,1)S(1)}, u32[]{:S(2)}, u32[]{:S(2)}) collective-permute-start(bf16[304,1024]{1,0:T(8,128)(2,1)} %get-tuple-element.67), channel_id=1, source_target_pairs={{0,1},{1,0},{2,3},{3,2},{4,5},{5,4},{6,7},{7,6},{8,9},{9,8},{10,11... | collective-permute-start | bytes 1867784 | tf_op jit(solution)/shard_map/ppermute | solution.py:544
  388.4 51.9 %collective-permute-start.61 = (bf16[1024,384]{1,0:T(8,128)(2,1)}, bf16[1024,384]{1,0:T(8,128)(2,1)S(1)}, u32[]{:S(2)}, u32[]{:S(2)}) collective-permute-start(bf16[1024,384]{1,0:T(8,128)(2,1)} %grad_qkv.3), channel_id=1, source_target_pairs={{0,16},{8,24},{16,0},{24,8},{1,17},{9,25},{17,1},{25,9},{2,18},{10... | collective-permute-start | bytes 2359304 | tf_op jit(solution)/shard_map/ppermute | solution.py:541
  417.1 32.6 %collective-permute-start.90 = (bf16[256,512]{1,0:T(8,128)(2,1)}, bf16[256,512]{1,0:T(8,128)(2,1)S(1)}, u32[]{:S(2)}, u32[]{:S(2)}) collective-permute-start(bf16[256,512]{1,0:T(8,128)(2,1)} %get-tuple-element.94), channel_id=1, source_target_pairs={{0,2},{2,4},{4,6},{6,0},{1,3},{3,5},{5,7},{7,1},{8,10},{10,12},{12... | collective-permute-start | bytes 786440 | tf_op jit(solution)/shard_map/ppermute | solution.py:547
  422.2 27.6 %collective-permute-start.91 = (bf16[256,512]{1,0:T(8,128)(2,1)}, bf16[256,512]{1,0:T(8,128)(2,1)S(1)}, u32[]{:S(2)}, u32[]{:S(2)}) collective-permute-start(bf16[256,512]{1,0:T(8,128)(2,1)} %get-tuple-element.95), channel_id=1, source_target_pairs={{0,4},{2,6},{4,0},{6,2},{1,5},{3,7},{5,1},{7,3},{8,12},{10,14},{12... | collective-permute-start | bytes 786440 | tf_op jit(solution)/shard_map/ppermute | solution.py:547
  (205 other events, 2862.8 us)

commit v2 on v1

v2 whole, which is shorter than its diff:
```python
import functools

import jax
import jax.numpy as jnp
from jax import lax
from jax.experimental import pallas as pl
from jax.experimental.pallas import tpu as pltpu
from jax.sharding import Mesh
from jax.sharding import PartitionSpec as P

HEADS = 16
HEAD_DIM = 64
IMG_TOK = 577
EPSILON = 1e-05
NEGATIVE = -1e30
LANES = 128
BF = jnp.bfloat16
F32 = jnp.float32

ANY = pl.BlockSpec(memory_space=pl.ANY)
VM = pl.BlockSpec(memory_space=pltpu.VMEM)
SM = pl.BlockSpec(memory_space=pltpu.SMEM)

ORDER = (0, 2, 1, 3)
OUT_LANE = 3 * LANES


def mm(a, b):
    return lax.dot_general(a, b, (((1,), (0,)), ((), ())), preferred_element_type=F32)


def mmt(a, b):
    return lax.dot_general(a, b, (((1,), (1,)), ((), ())), preferred_element_type=F32)


def tmm(a, b):
    return lax.dot_general(a, b, (((0,), (0,)), ((), ())), preferred_element_type=F32)


def normalize(inputs):
    center = inputs - jnp.mean(inputs, axis=-1, keepdims=True)
    inverse = lax.rsqrt(jnp.mean(center * center, axis=-1, keepdims=True) + EPSILON)
    return center * inverse, inverse


def norm_back(grad_in, scaled, inverse, gain_row):
    weighted = grad_in * gain_row
    return inverse * (
        weighted
        - jnp.mean(weighted, axis=-1, keepdims=True)
        - scaled * jnp.mean(weighted * scaled, axis=-1, keepdims=True)
    )


def at(index, size):
    return pl.ds(pl.multiple_of(index * size, size), size)


def flip(r, d):
    return jnp.bitwise_xor(r, d) if d else r


def fetch(copies, sems):
    handles = [pltpu.make_async_copy(s, t, sems.at[i]) for i, (s, t) in enumerate(copies)]
    for handle in handles:
        handle.start()
    return handles


def finish(handles):
    for handle in handles:
        handle.wait()


COST = pl.CostEstimate(flops=1 << 33, bytes_accessed=1 << 18, transcendentals=0)


def call(body, ins, specs, outs, scratch, name, out_specs=None):
    return pl.pallas_call(
        body,
        out_shape=outs,
        in_specs=specs,
        out_specs=out_specs or [VM] * len(outs),
        scratch_shapes=scratch,
        compiler_params=pltpu.CompilerParams(vmem_limit_bytes=56 << 20),
        cost_estimate=COST,
        name=name,
    )(*ins)


def shape(dims, dtype):
    return jax.ShapeDtypeStruct(dims, dtype)


def column_copies(refs, w, ids, lane=0, relative=False):
    rows, q = w.shape[0], w.shape[1] // 4
    copies = []
    for d in range(4):
        slot = pl.ds(ORDER.index(d) * q, q) if relative else at(flip(ids[0], d), q)
        source = refs[d & 1].at[pl.ds((d >> 1) * rows, rows), pl.ds(lane, q)]
        copies.append((source, w.at[:, slot]))
    return copies


def row_copies(refs, w, ids):
    q = w.shape[0] // 4
    return [
        (refs[d & 1].at[pl.ds((d >> 1) * q, q), :], w.at[at(flip(ids[0], d), q), :])
        for d in range(4)
    ]


def split(refs, *counts):
    refs = list(refs)
    out = []
    for count in counts:
        out.append(refs[:count])
        refs = refs[count:]
    return out + [refs]


def qkv_kernel(ids, own, near, vec, *refs):
    weights, (normed, queries, keys, values), (w, sems) = split(refs, 2, 4)
    handles = fetch(column_copies(weights, w, ids), sems)
    rows = own.shape[0]
    for i, part in enumerate((own, near)):
        scaled, _ = normalize(part[...].astype(F32))
        normed[i * rows : (i + 1) * rows, :] = (scaled * vec[0:1, :] + vec[2:3, :]).astype(BF)
    finish(handles)
    scale = HEAD_DIM ** (-0.5)
    first = ids[1] * (queries.shape[1] // LANES)

    def step(i, carry):
        joined = mm(normed[...], w[:, at(i, 3 * LANES)])
        here = at(i, LANES)
        there = at(first + i, LANES)
        queries[:, here] = ((joined[:, :LANES] + vec[3:4, there]) * scale).astype(BF)
        keys[:, here] = joined[:, LANES : 2 * LANES].astype(BF)
        values[:, here] = (joined[:, 2 * LANES :] + vec[4:5, there]).astype(BF)
        return carry

    lax.fori_loop(0, 4, step, 0)


def valid_keys(ids, rows, real):
    index = lax.broadcasted_iota(jnp.int32, (2 * rows, 1), 0)
    second = (index >= rows).astype(jnp.int32)
    local = index - second * rows
    position = jnp.bitwise_xor(second, ids[1]) * real + local
    return (local < real) & (position < IMG_TOK)


def head_half(value, half):
    lane = lax.broadcasted_iota(jnp.int32, value.shape, 1)
    keep = (lane < HEAD_DIM) if half == 0 else (lane >= HEAD_DIM)
    return jnp.where(keep, value, jnp.zeros_like(value))


def with_lanes(value, half, columns):
    lane = lax.broadcasted_iota(jnp.int32, value.shape, 1)
    out = head_half(value, half)
    for i, column in enumerate(columns):
        out = jnp.where(lane == (1 - half) * HEAD_DIM + i, column, out)
    return out


def three_parts(column):
    high = column.astype(BF)
    rest = column - high.astype(F32)
    middle = rest.astype(BF)
    return [high, middle, (rest - middle.astype(F32)).astype(BF)]


def key_shift(ids, rows, real):
    shift = jnp.where(valid_keys(ids, rows, real), 0.0, NEGATIVE)
    return shift.astype(BF)


def attend_kernel(rows, real, ids, queries, keys, values, mixed_own, mixed_near, totals):
    one = jnp.ones((1, 1), BF)
    shift = key_shift(ids, rows, real)
    keys_of = [with_lanes(keys[...], half, [shift]) for half in range(2)]
    values_of = [head_half(values[...], half) for half in range(2)]
    for i, target in enumerate((mixed_own, mixed_near)):
        block = queries[i * rows : (i + 1) * rows, :]
        total = None
        for half in range(2):
            scores = mmt(keys_of[half], with_lanes(block, half, [one]))
            highest = jnp.max(scores, axis=0, keepdims=True)
            exponent = jnp.exp(scores - highest)
            sums = jnp.sum(exponent, axis=0, keepdims=True)
            totals[2 * half + i : 2 * half + i + 1, :] = highest + jnp.log(sums)
            part = tmm(values_of[half], exponent.astype(BF)) * (1.0 / sums)
            total = part if total is None else total + part
        target[...] = total.T.astype(BF)


def attend(ids, queries, keys, values, rows, real):
    wide = queries.shape[1]
    steps = wide // LANES
    block = pl.BlockSpec((2 * rows, LANES), lambda i, ids: (0, i))
    half = pl.BlockSpec((rows, LANES), lambda i, ids: (0, i))
    return pl.pallas_call(
        functools.partial(attend_kernel, rows, real),
        grid_spec=pltpu.PrefetchScalarGridSpec(
            num_scalar_prefetch=1,
            grid=(steps,),
            in_specs=[block] * 3,
            out_specs=[half] * 2 + [pl.BlockSpec((None, 4, rows), lambda i, ids: (i, 0, 0))],
        ),
        out_shape=[shape((rows, wide), BF)] * 2 + [shape((steps, 4, rows), F32)],
        compiler_params=pltpu.CompilerParams(vmem_limit_bytes=56 << 20),
        cost_estimate=COST,
        name="attend",
    )(ids, queries, keys, values)


def attend_back_kernel(
    rows, real, ids, queries, keys, values, mixed_own, mixed_near, grad_own, grad_near,
    totals, out, sums,
):
    one = jnp.ones((1, 1), BF)
    shift = key_shift(ids, rows, real)
    keys_of = [head_half(keys[...], half) for half in range(2)]
    wide_keys = [with_lanes(keys[...], half, [shift, one, one, one]) for half in range(2)]
    wide_values = [with_lanes(values[...], half, [one, one, one]) for half in range(2)]
    lines = jnp.concatenate([totals[...], jnp.zeros_like(totals[...])], axis=0).T
    grad_k = grad_v = None
    grad_q = []
    for part, (mixed, grad_ref) in enumerate(((mixed_own, grad_own), (mixed_near, grad_near))):
        block = queries[part * rows : (part + 1) * rows, :]
        grad = grad_ref[...]
        product = grad.astype(F32) * mixed[...].astype(F32)
        total = None
        for half in range(2):
            line = three_parts(-lines[:, 2 * half + part : 2 * half + part + 1])
            probs = jnp.exp(mmt(wide_keys[half], with_lanes(block, half, [one, *line])))
            inner = jnp.sum(head_half(product, half), axis=1, keepdims=True)
            wide_grad = with_lanes(grad, half, three_parts(-inner))
            grad_scores = (probs * mmt(wide_values[half], wide_grad)).astype(BF)
            first = tmm(keys_of[half], grad_scores)
            total = first if total is None else total + first
            second = mm(grad_scores, head_half(block, half))
            third = mm(probs.astype(BF), head_half(grad, half))
            grad_k = second if grad_k is None else grad_k + second
            grad_v = third if grad_v is None else grad_v + third
        grad_q.append(total.T)
    scale = HEAD_DIM ** (-0.5)
    grad_q = jnp.concatenate(grad_q, axis=0).astype(BF).astype(F32) * scale
    pieces = [grad_q.astype(BF), grad_k.astype(BF), grad_v.astype(BF)]
    for kind, piece in enumerate(pieces):
        columns = slice(kind * LANES, (kind + 1) * LANES)
        sums[:, columns] = jnp.sum(piece.astype(F32), axis=0, keepdims=True)
        out[:, columns] = piece


def attend_back(ids, saved, mixed, grads, totals, rows, real, first):
    def index(i, ids):
        return jnp.bitwise_xor(ids[0], first + 2 * i)

    block = pl.BlockSpec((2 * rows, LANES), lambda i, ids: (0, index(i, ids)))
    half = pl.BlockSpec((rows, LANES), lambda i, ids: (0, index(i, ids)))
    lines = pl.BlockSpec((None, 4, rows), lambda i, ids: (index(i, ids), 0, 0))
    whole = pl.BlockSpec((None, 2 * rows, 3 * LANES), lambda i, ids: (i, 0, 0))
    line = pl.BlockSpec((None, 1, 3 * LANES), lambda i, ids: (i, 0, 0))
    return pl.pallas_call(
        functools.partial(attend_back_kernel, rows, real),
        grid_spec=pltpu.PrefetchScalarGridSpec(
            num_scalar_prefetch=1,
            grid=(2,),
            in_specs=[block] * 3 + [half] * 4 + [lines],
            out_specs=[whole, line],
        ),
        out_shape=[shape((2, 2 * rows, 3 * LANES), BF), shape((2, 1, 3 * LANES), F32)],
        compiler_params=pltpu.CompilerParams(vmem_limit_bytes=56 << 20),
        cost_estimate=COST,
        name="attend_back",
    )(ids, *saved, *mixed, *grads, totals)


def project_kernel(ids, tokens, mixed_own, mixed_near, vec, *refs):
    weights, (mixed, middle, normed), (w, sems) = split(refs, 2, 3)
    handles = fetch(column_copies(weights, w, ids, OUT_LANE), sems)
    y = ids[1]
    half = mixed_own.shape[1]
    mixed[:, at(y, half)] = mixed_own[...]
    mixed[:, at(1 - y, half)] = mixed_near[...]
    finish(handles)
    total = tokens[...].astype(F32) + (mm(mixed[...], w[...]) + vec[5:6, :])
    middle[...] = total
    scaled, _ = normalize(total)
    normed[...] = (scaled * vec[1:2, :] + vec[6:7, :]).astype(BF)


def mlp_kernel(ids, n_own, n_near, g_own, g_near, fb, *refs):
    ones, twos, outs, scratch = split(refs, 2, 2, 5)
    near, far, grad_own, grad_near, sums = outs
    w1, w2, normed, grads, total, sems = scratch
    r = ids[0]
    rows = n_own.shape[0]
    handles = fetch(column_copies(ones, w1, ids) + row_copies(twos, w2, ids), sems)
    normed[:rows, :] = n_own[...]
    normed[rows:, :] = n_near[...]
    grads[:rows, :] = g_own[...]
    grads[rows:, :] = g_near[...]
    wide = w1.shape[1] // 4
    far[:, 4 * wide :] = normed[...]
    total[...] = jnp.zeros_like(total)
    finish(handles)

    def step(i, carry):
        here = at(i, wide)
        hidden = mm(normed[...], w1[:, here]) + fb[:, here]
        gate = 1.0 / (1.0 + jnp.exp(-1.702 * hidden))
        active = (hidden * gate).astype(BF)
        grad_active = mmt(grads[...], w2[here, :])
        grad_hidden = (
            grad_active * (gate + 1.702 * hidden * gate * (1.0 - gate))
        ).astype(BF)
        sums[:, here] = jnp.sum(grad_hidden.astype(F32), axis=0, keepdims=True)
        total[...] += mmt(grad_hidden, w1[:, here])
        d = jnp.bitwise_xor(r, i)

        @pl.when((d & 1) == 0)
        def _():
            near[:, at(d >> 1, wide)] = grad_hidden
            near[:, at(2 + (d >> 1), wide)] = active

        @pl.when((d & 1) == 1)
        def _():
            far[:, at(d >> 1, wide)] = grad_hidden
            far[:, at(2 + (d >> 1), wide)] = active

        return carry

    lax.fori_loop(0, 4, step, 0)
    grad_own[...] = total[:rows, :]
    grad_near[...] = total[rows:, :].astype(BF)


def result_kernel(ids, near, far, *refs):
    twos, (own, other), (w2, total, sems) = split(refs, 2, 2)
    r = ids[0]
    finish(fetch(row_copies(twos, w2, ids), sems))
    rows = own.shape[0]
    wide = w2.shape[0] // 4
    for s, d in enumerate(ORDER):
        part = near if s < 2 else far
        slot = 2 + s % 2
        value = mm(part[:, slot * wide : (slot + 1) * wide], w2[at(flip(r, d), wide), :])
        if s:
            value = value + total[...]
        if s < 3:
            total[...] = value
    own[...] = value[:rows, :]
    other[...] = value[rows:, :].astype(BF)


def middle_back_kernel(ids, grad_own, grad_recv, middle, incoming, vec, *refs):
    weights, outs, (w, work, sems) = split(refs, 2, 5)
    grad_middle, branch, mixed_own, mixed_near, sums = outs
    handles = fetch(column_copies(weights, w, ids, OUT_LANE), sems)
    y = ids[1]
    grad = grad_own[...] + grad_recv[...].astype(F32)
    scaled, inverse = normalize(middle[...])
    sums[0:1, :] = jnp.sum(grad * scaled, axis=0, keepdims=True)
    sums[1:2, :] = jnp.sum(grad, axis=0, keepdims=True)
    arriving = incoming[...].astype(F32)
    sums[3:4, :] = jnp.sum(arriving, axis=0, keepdims=True)
    total = arriving + norm_back(grad, scaled, inverse, vec[1:2, :])
    grad_middle[...] = total
    low = total.astype(BF)
    branch[...] = low
    sums[2:3, :] = jnp.sum(low.astype(F32), axis=0, keepdims=True)
    finish(handles)
    work[...] = mmt(branch[...], w[...]).astype(BF)
    half = work.shape[1] // 2
    mixed_own[...] = work[:, at(y, half)]
    mixed_near[...] = work[:, at(1 - y, half)]


def qkv_back_kernel(ids, near, far, *refs):
    weights, (own, other), (w, grads, sems) = split(refs, 2, 2)
    wide = near.shape[2]
    copies = column_copies(weights, w, ids, relative=True)
    for s in range(4):
        source = (near if s < 2 else far).at[s % 2]
        copies.append((source, grads.at[:, pl.ds(s * wide, wide)]))
    finish(fetch(copies, sems))
    rows = own.shape[0]
    step_rows = 256

    def step(i, carry):
        here = at(i, step_rows)
        value = mmt(grads[...], w[here, :])
        own[:, here] = value[:rows, :]
        other[:, here] = value[rows:, :].astype(BF)
        return carry

    lax.fori_loop(0, w.shape[0] // step_rows, step, 0)


def tokens_back_kernel(ids, grad_own, grad_recv, tokens, grad_middle, vec, out, sums):
    grad = grad_own[...] + grad_recv[...].astype(F32)
    scaled, inverse = normalize(tokens[...].astype(F32))
    sums[0:1, :] = jnp.sum(grad * scaled, axis=0, keepdims=True)
    sums[1:2, :] = jnp.sum(grad, axis=0, keepdims=True)
    total = grad_middle[...] + norm_back(grad, scaled, inverse, vec[0:1, :])
    out[...] = total.astype(BF)[: out.shape[0], :]


def window(ref, pick):
    if pick is None:
        return ref
    if len(ref.shape) == 3:
        return ref.at[pick]
    return ref.at[:, pl.ds(*pick)]


def extent(array, pick):
    if pick is None:
        return array.shape
    if array.ndim == 3:
        return array.shape[1:]
    return (array.shape[0], pick[1])


def weight_kernel(left_picks, right_picks, more, ids, *refs):
    left_refs, right_refs, extra, rest = split(refs, len(left_picks), len(right_picks), more)
    *outs, a, b, sems = rest
    copies = []
    for parts, target, picks in ((left_refs, a, left_picks), (right_refs, b, right_picks)):
        start = 0
        for part, pick in zip(parts, picks):
            source = window(part, pick)
            count = source.shape[0]
            copies.append((source, target.at[pl.ds(start, count), :]))
            start += count
    finish(fetch(copies, sems))
    if len(outs) > 1:
        rows = outs[0].shape[0]
        for k, out in enumerate(outs):
            here = at(lax.rem(ids[2] + k, len(outs)), rows)
            value = tmm(a[:, here], b[...])
            if more:
                value = value + extra[0][here, :].astype(F32)
            out[...] = value.astype(out.dtype)
        return
    (out,) = outs
    step_rows = 256

    def step(i, carry):
        here = at(i, step_rows)
        value = tmm(a[:, here], b[...])
        if more:
            value = value + extra[0][here, :].astype(F32)
        out[here, :] = value.astype(out.dtype)
        return carry

    lax.fori_loop(0, out.shape[0] // step_rows, step, 0)


def weight_grad(ids, left, right, name, extra=(), blocks=1):
    def span(parts):
        dims = [extent(*p) for p in parts]
        return sum(d[0] for d in dims), dims[0][1]

    depth, rows = span(left)
    _, columns = span(right)
    kinds = [F32] + [BF] * (blocks - 1) if blocks > 1 else [BF]
    return call(
        functools.partial(
            weight_kernel, [p for _, p in left], [p for _, p in right], len(extra)
        ),
        [ids] + [a for a, _ in left] + [a for a, _ in right] + list(extra),
        [SM] + [ANY] * (len(left) + len(right)) + [VM] * len(extra),
        [shape((rows // blocks, columns), kind) for kind in kinds],
        [
            pltpu.VMEM((depth, rows), BF),
            pltpu.VMEM((depth, columns), BF),
            pltpu.SemaphoreType.DMA((len(left) + len(right),)),
        ],
        name,
    )


def out_grad_kernel(ids, mixed, mixed_far, branch, branch_far, send, keep, a, b, sems):
    r, y = ids[0], ids[1]
    rows = mixed.shape[0]
    half = branch.shape[1] // 2
    quarters = half // LANES
    copies = []
    for i, (left, right) in enumerate(((mixed, branch), (mixed_far, branch_far))):
        here = pl.ds(i * rows, rows)
        copies.append((left, a.at[here, :]))
        for s, (dy, d) in enumerate(((1, 2), (1, 0), (0, 2), (0, 0))):
            block = flip(y, dy) * quarters + flip(r, d)
            copies.append((right.at[:, at(block, LANES)], b.at[here, pl.ds(s * LANES, LANES)]))
    finish(fetch(copies, sems))
    step_rows = 256

    def step(i, carry):
        here = at(i, step_rows)
        value = tmm(a[:, here], b[...])
        send[here, :] = value[:, : 2 * LANES].astype(BF)
        keep[here, :] = value[:, 2 * LANES :]
        return carry

    lax.fori_loop(0, a.shape[1] // step_rows, step, 0)


def combine_kernel(ids, keep, recv, *outs):
    rows = outs[0].shape[0]
    for k, out in enumerate(outs):
        here = at(lax.rem(ids[2] + k, len(outs)), rows)
        out[...] = (keep[here, :] + recv[here, :].astype(F32)).astype(out.dtype)


def join(parts):
    return parts[0] if len(parts) == 1 else jnp.concatenate(parts, axis=1)


def cast_qkv_kernel(ids, first, second, third, fourth, gains, biases, shift, out, low):
    rows = first.shape[0]
    out[:rows, :] = join([part[...].astype(BF) for part in (first, second, third, fourth)])
    low[...] = jnp.zeros_like(low)
    width = gains.shape[1]
    low[0:2, :width] = gains[...]
    low[2:8, :width] = biases[...]
    low[8:12, :width] = shift[...]
    out[rows:, :] = low[...].astype(BF)


def cast_rest_kernel(n, ids, *refs):
    ones, (two_part,), (one, two) = split(refs, n, 1)
    one[...] = join([part[...].astype(BF) for part in ones])
    two[...] = two_part[...].astype(BF)


def cast(body, ids, blocks, outs, scratch, name):
    specs = [pl.BlockSpec(block, lambda i, ids, at=at: at(ids)) for _, block, at in blocks]
    return pl.pallas_call(
        body,
        grid_spec=pltpu.PrefetchScalarGridSpec(
            num_scalar_prefetch=1,
            grid=(1,),
            in_specs=specs,
            out_specs=[pl.BlockSpec(o.shape, lambda i, ids: (0, 0)) for o in outs],
            scratch_shapes=scratch,
        ),
        out_shape=outs,
        compiler_params=pltpu.CompilerParams(vmem_limit_bytes=56 << 20),
        cost_estimate=COST,
        name=name,
    )(ids, *[array for array, _, _ in blocks])


def stack_kernel(n, ids, *refs):
    parts, (out, *more), _ = split(refs, 2 * n, 1 if len(refs) == 2 * n + 1 else 2)
    rows = out.shape[1]
    for i, part in enumerate(parts):
        there = lax.rem(ids[2] - i % n + n, n)
        out[(i // n) * n + there] = part[:rows, :]
        if more and i < n:
            width = more[0].shape[1] // n
            low = part[rows:, :width].astype(F32)
            more[0][:, at(there, width)] = low


def place_kernel(kind, ids, *refs):
    sources, (out,), _ = split(refs, 4, 1)
    for d, source in enumerate(sources):
        for dy in range(2):
            block = flip(ids[1], dy) * 4 + flip(ids[0], d)
            piece = source[dy].astype(F32)
            if kind == "rows":
                out[at(block, piece.shape[0]), :] = piece
                continue
            for g in range(piece.shape[1] // LANES):
                columns = at(block + g * 8, LANES)
                out[:, columns] = piece[:, g * LANES : (g + 1) * LANES]


def place(ids, sources, dims, kind):
    count, rows, columns = sources[0].shape
    steps = 4
    if kind == "rows":
        inside = pl.BlockSpec((count, rows, columns // steps), lambda i, ids: (0, 0, i))
        outside = pl.BlockSpec((dims[0], dims[1] // steps), lambda i, ids: (0, i))
    else:
        inside = pl.BlockSpec((count, rows // steps, columns), lambda i, ids: (0, i, 0))
        outside = pl.BlockSpec((dims[0] // steps, dims[1]), lambda i, ids: (i, 0))
    return pl.pallas_call(
        functools.partial(place_kernel, kind),
        grid_spec=pltpu.PrefetchScalarGridSpec(
            num_scalar_prefetch=1, grid=(steps,), in_specs=[inside] * 4, out_specs=outside
        ),
        out_shape=shape(dims, F32),
        compiler_params=pltpu.CompilerParams(vmem_limit_bytes=40 << 20),
        cost_estimate=COST,
        name="place",
    )(ids, *sources)


def after(value, *others):
    return lax.optimization_barrier((value, *others))[0]


def on_device(n, tokens, slot_mask, cotangent, w_qkv, w_out, w_fc1, w_fc2, ln_gains, biases, fc1_bias):
    slot_count, real, wide = tokens.shape
    assert slot_count == 1
    direct = n == 4
    rows = -(-real // 16) * 16
    hidden = fc1_bias.shape[0] * n
    half, part_hidden = wide // 2, hidden // 2
    h = hidden // n // 8
    x, c = lax.axis_index("x"), lax.axis_index("core")
    y, z = lax.axis_index("seq"), lax.axis_index("fsdp")
    r = 2 * x + c
    ids = jnp.stack([r, y, z]).astype(jnp.int32)
    swap = [(0, 1), (1, 0)]

    def core(v):
        return lax.ppermute(v, "core", swap)

    def across(v):
        return lax.ppermute(v, "x", swap)

    def near(v):
        return lax.ppermute(v, "seq", swap)

    def shift(v, k):
        return lax.ppermute(v, "fsdp", [(i, (i + k) % n) for i in range(n)])

    def scatter_rows(outs):
        if len(outs) == 1:
            value = lax.psum_scatter(outs[0], "fsdp", scatter_dimension=0, tiled=True)
        else:
            value = outs[0]
            for k in range(1, n):
                value = value + shift(outs[k], k).astype(F32)
        return value.astype(BF)

    clock = [ids]

    def tick(*values):
        clock[0] = lax.optimization_barrier((ids, *values))[0]

    def run(body, ins, specs, outs, scratch, name):
        results = call(body, [clock[0], *ins], [SM] + specs, outs, scratch, name)
        tick(results[0])
        return results

    pad = ((0, rows - real), (0, 0))
    tok = jnp.pad(tokens[0], pad)
    tok_near = near(tok)
    positions = y * real + jnp.arange(real)
    keep = slot_mask.astype(F32)[0] * (positions < IMG_TOK).astype(F32)
    keep = keep[:, None]
    grads = jnp.pad((cotangent[0].astype(F32) * keep).astype(BF), pad)
    grads_near = near(after(grads, tok_near))

    sems = lambda c: pltpu.SemaphoreType.DMA((c,))
    few = hidden // wide
    shift_rows = fc1_bias.reshape(few, wide // n)
    quarter = part_hidden // 4
    own_rows = wide // n

    def both_cores(v):
        return [v, core(v)]

    if direct:
        q = lambda ids: ids[1] * 4 + ids[0]
        blocks = [(w_qkv, (own_rows, LANES), lambda ids, k=k: (0, k * 8 + q(ids))) for k in range(3)]
        blocks += [(w_out, (own_rows, wide // 4), lambda ids: (0, ids[0]))]
        blocks += [(v, v.shape, lambda ids: (0, 0)) for v in (ln_gains, biases, shift_rows)]
        across_lanes = OUT_LANE + wide // 4
        (qkv_piece,) = cast(
            cast_qkv_kernel,
            ids,
            blocks,
            [shape((own_rows + 16, across_lanes), BF)],
            [pltpu.VMEM((16, across_lanes), F32)],
            "cast_qkv",
        )
        tick(qkv_piece)
        blocks = [(w_fc1, (own_rows, LANES), lambda ids, k=k: (0, k * 8 + q(ids))) for k in range(n)]
        blocks += [(w_fc2, (h, wide), lambda ids: (q(ids), 0))]
        one_piece, two_piece = cast(
            functools.partial(cast_rest_kernel, n),
            clock[0],
            blocks,
            [shape((own_rows, quarter), BF), shape((h, wide), BF)],
            [],
            "cast_rest",
        )
        tick(one_piece)

        def over_z(piece, before=None, gate=()):
            parts = [piece]
            for k in range(1, n):
                ready = piece if before is None else after(piece, before[k], *gate)
                parts.append(shift(ready, k))
            return parts

        def over_x(parts, own, *gates):
            others = [own]
            for k in range(1, n):
                gate = gates[min(k, len(gates)) - 1] if gates else ()
                others.append(across(after(parts[k], *gate)))
            return others

        def stack(parts, others, name, more=()):
            dims = (2 * n, parts[0].shape[0] - (16 if more else 0), parts[0].shape[1])
            whole, *rest = run(
                functools.partial(stack_kernel, n),
                parts + others,
                [VM] * (2 * n),
                [shape(dims, BF), *more],
                [],
                name,
            )
            return both_cores(whole.reshape(dims[0] * dims[1], dims[2])), rest

        qkv_parts = over_z(qkv_piece)
        qkv_own = across(qkv_piece)
        one_own, two_own = across(one_piece), across(two_piece)
        one_parts = over_z(one_piece, qkv_parts)
        all_qkv, (vec,) = stack(
            qkv_parts,
            over_x(qkv_parts, qkv_own, (), (), (tok_near,)),
            "stack_qkv",
            [shape((16, wide), F32)],
        )
    else:
        cut = lambda v, start, size, axis: lax.dynamic_slice_in_dim(v, start, size, axis).astype(BF)
        qkv_piece = jnp.concatenate(
            [cut(w_qkv, k * wide + y * half + r * LANES, LANES, 1) for k in range(3)]
            + [cut(w_out, r * (wide // 4), wide // 4, 1)],
            axis=1,
        )
        grid = w_fc1.reshape(w_fc1.shape[0], n, 8, h)
        one_piece = cut(grid, y * 4 + r, 1, 2).reshape(w_fc1.shape[0], n * h)
        two_piece = cut(w_fc2, (y * 4 + r) * h, h, 0)

        def whole(v):
            v = lax.all_gather(v, "fsdp", axis=0, tiled=True)
            return both_cores(jnp.concatenate([v, across(v)], axis=0))

        all_qkv, all_one, all_two = map(whole, (qkv_piece, one_piece, two_piece))
        small = jnp.concatenate([ln_gains, biases, shift_rows], axis=0).astype(BF)
        vec = lax.all_gather(small, "fsdp", axis=0).astype(F32).transpose(1, 0, 2)
        vec = jnp.pad(vec.reshape(-1, wide), ((0, 4), (0, 0)))

    two = 2 * rows
    normed, queries, keys, values = run(
        qkv_kernel,
        [tok, tok_near, vec, *all_qkv],
        [VM] * 3 + [ANY] * 2,
        [shape((two, wide), BF)] + [shape((two, half), BF)] * 3,
        [pltpu.VMEM((wide, 3 * half), BF), sems(4)],
        "qkv",
    )
    hidden_shift = vec[8:12].reshape(few, n, wide // n).transpose(1, 0, 2).reshape(n, 2, 4, h)
    hidden_shift = lax.dynamic_index_in_dim(hidden_shift, y, axis=1, keepdims=False)
    hidden_shift = hidden_shift.transpose(1, 0, 2).reshape(1, part_hidden)
    normed_far = core(normed)
    saved = (queries, keys, values)
    mixed_own, mixed_send, totals = attend(clock[0], *saved, rows, real)
    mixed_parts = (mixed_own, mixed_send)
    tick(mixed_own)
    if direct:
        mixed_send = after(mixed_send, grads_near, *one_parts[1:])
        two_parts = over_z(two_piece, qkv_parts, [normed])
    mixed_recv = near(mixed_send)
    grads_far, grads_near_far = core(grads), core(grads_near)
    mixed, middle, normed_two = run(
        project_kernel,
        [tok, mixed_own, mixed_recv, vec, *all_qkv],
        [VM] * 4 + [ANY] * 2,
        [shape((rows, wide), BF), shape((rows, wide), F32), shape((rows, wide), BF)],
        [pltpu.VMEM((wide, wide), BF), sems(4)],
        "project",
    )
    if direct:
        one_others = over_x(one_parts, one_own, (mixed_own,))
        normed_two_near = near(after(normed_two, *one_others))
    else:
        normed_two_near = near(normed_two)
    if direct:
        all_one, _ = stack(one_parts, one_others, "stack_one")
        tick(normed_two_near)
        all_two, _ = stack(two_parts, over_x(two_parts, two_own, (mixed,)), "stack_two")
    act_near, act_far, gtwo_own, gtwo_send, hidden_sums = run(
        mlp_kernel,
        [normed_two, normed_two_near, grads, grads_near, hidden_shift, *all_one, *all_two],
        [VM] * 5 + [ANY] * 4,
        [
            shape((two, 4 * quarter), BF),
            shape((two, 4 * quarter + wide), BF),
            shape((rows, wide), F32),
            shape((rows, wide), BF),
            shape((1, part_hidden), F32),
        ],
        [
            pltpu.VMEM((wide, part_hidden), BF),
            pltpu.VMEM((part_hidden, wide), BF),
            pltpu.VMEM((two, wide), BF),
            pltpu.VMEM((two, wide), BF),
            pltpu.VMEM((two, wide), F32),
            sems(8),
        ],
        "mlp",
    )
    gtwo_recv = near(gtwo_send)
    act_other = core(act_far)
    mixed_far = core(mixed)

    def spread(part):
        pair = jnp.stack([part, near(part)])
        return pair, across(pair)

    def land(pairs, dims, kind):
        pairs = [pairs[0], core(pairs[0]), pairs[1], core(pairs[1])]
        if direct:
            return place(ids, pairs, dims, kind)
        stack = jnp.stack(pairs, axis=1).reshape((8,) + pairs[0].shape[1:])
        order = (jnp.bitwise_xor(jnp.arange(2), y) * 4)[:, None]
        order = (order + jnp.bitwise_xor(jnp.arange(4), r)[None, :]).reshape(-1)
        stack = jnp.take(stack, order, axis=0).astype(F32)
        if kind == "rows":
            return stack.reshape(dims)
        groups = dims[1] // (8 * (h if kind == "hidden" else LANES))
        stack = stack.reshape(8, dims[0], groups, -1)
        return stack.transpose(1, 2, 0, 3).reshape(dims)

    blocks = n if direct else 1

    def grad(left, right, name, extra=()):
        values = weight_grad(clock[0], left, right, name, extra, blocks if extra else 1)
        tick(values[0])
        return values if extra else values[0]

    all_grads = [(a, None) for a in (grads, grads_near, grads_far, grads_near_far)]
    one_left = [
        (normed_two, None),
        (normed_two_near, None),
        (act_other, (4 * quarter, wide)),
    ]

    def unit(slot):
        return [(act_near, (slot * quarter, quarter)), (act_other, (slot * quarter, quarter))]

    two_recv = across(grad(unit(3), all_grads, "grad_fc2_send"))
    one_recv = across(grad(one_left, unit(1), "grad_fc1_send"))
    grad_middle, branch, gmix_own, gmix_send, sums_two = run(
        middle_back_kernel,
        [gtwo_own, gtwo_recv, middle, grads, vec, *all_qkv],
        [VM] * 5 + [ANY] * 2,
        [
            shape((rows, wide), F32),
            shape((rows, wide), BF),
            shape((rows, half), BF),
            shape((rows, half), BF),
            shape((4, wide), F32),
        ],
        [pltpu.VMEM((wide, wide), BF), pltpu.VMEM((rows, wide), BF), sems(4)],
        "middle_back",
    )
    gmix_recv = near(gmix_send)
    branch_far = core(branch)
    result_own, result_send = run(
        result_kernel,
        [act_near, act_far, *all_two],
        [VM] * 2 + [ANY] * 2,
        [shape((rows, wide), F32), shape((rows, wide), BF)],
        [
            pltpu.VMEM((part_hidden, wide), BF),
            pltpu.VMEM((two, wide), F32),
            sems(4),
        ],
        "result",
    )
    result_recv = near(result_send)
    total = middle[:real] + (
        result_own[:real] + result_recv[:real].astype(F32) + vec[7:8, :]
    )
    output = (total * keep).astype(BF)[None]

    gj_far, sums_far = attend_back(
        clock[0], saved, mixed_parts, (gmix_own, gmix_recv), totals, rows, real, 1
    )
    tick(gj_far)
    gj_other = core(gj_far)
    two_part = scatter_rows(grad(unit(2), all_grads, "grad_fc2_keep", [two_recv]))
    gj_near, sums_near = attend_back(
        clock[0], saved, mixed_parts, (gmix_own, gmix_recv), totals, rows, real, 0
    )
    tick(gj_near)
    joined_sums = jnp.concatenate([sums_near, sums_far], axis=0)
    one_part = scatter_rows(grad(one_left, unit(0), "grad_fc1_keep", [one_recv]))
    qkv_left = [(normed, None), (normed_far, None)]
    qkv_recv = across(grad(qkv_left, [(gj_near, 1), (gj_other, 1)], "grad_qkv_send"))
    gone_own, gone_send = run(
        qkv_back_kernel,
        [gj_near, gj_far, *all_qkv],
        [ANY] * 4,
        [shape((rows, wide), F32), shape((rows, wide), BF)],
        [
            pltpu.VMEM((wide, 3 * half), BF),
            pltpu.VMEM((two, 3 * half), BF),
            sems(8),
        ],
        "qkv_back",
    )
    gone_recv = near(gone_send)
    out_send, out_keep = run(
        out_grad_kernel,
        [mixed, mixed_far, branch, branch_far],
        [ANY] * 4,
        [shape((wide, 2 * LANES), BF), shape((wide, 2 * LANES), F32)],
        [pltpu.VMEM((two, wide), BF), pltpu.VMEM((two, 4 * LANES), BF), sems(10)],
        "grad_out",
    )
    out_recv = near(out_send)
    two_pairs = spread(two_part)
    qkv_part = scatter_rows(
        grad(qkv_left, [(gj_near, 0), (gj_other, 0)], "grad_qkv_keep", [qkv_recv])
    )
    tick(one_part)
    grad_tokens, sums_one = run(
        tokens_back_kernel,
        [gone_own, gone_recv, tok, grad_middle, vec],
        [VM] * 5,
        [shape((real, wide), BF), shape((2, wide), F32)],
        [],
        "tokens_back",
    )
    grad_tokens = grad_tokens[None]
    out_sum = out_keep + out_recv.astype(F32)
    out_cross = across(out_sum[:, :LANES].astype(BF))
    kinds = [F32] + [BF] * (blocks - 1) if blocks > 1 else [BF]
    out_part = scatter_rows(
        run(
            combine_kernel,
            [out_sum[:, LANES:], out_cross],
            [VM] * 2,
            [shape((wide // blocks, LANES), kind) for kind in kinds],
            [],
            "combine",
        )
    )
    grad_fc2 = land(two_pairs, w_fc2.shape, "rows")
    grad_fc1 = land(spread(one_part), w_fc1.shape, "hidden")
    grad_out = land(spread(out_part), w_out.shape, "columns")
    grad_qkv = land(spread(qkv_part), w_qkv.shape, "columns")

    wanted = jnp.bitwise_xor(jnp.arange(4), r)
    slots = ((wanted & 1) << 1) | (wanted >> 1)
    chosen = (slots[:, None] == jnp.arange(4)[None, :]).astype(F32)
    joined_sums = jnp.sum(chosen[:, :, None] * joined_sums[None, :, 0, :], axis=1)
    here = (jnp.arange(2) == y).astype(F32)

    def spread_half(row):
        return (here[:, None] * row.reshape(1, half)).reshape(1, wide)

    query_sums = spread_half(joined_sums[:, :LANES])
    value_sums = spread_half(joined_sums[:, 2 * LANES :])
    hidden_sums = hidden_sums.reshape(4, n, h).transpose(1, 0, 2).reshape(n, 1, 4 * h)
    hidden_sums = (hidden_sums * here[None, :, None]).reshape(n, hidden // wide, wide // n)
    rows_of = jnp.concatenate(
        [
            sums_one[0:1],
            sums_two[0:1],
            sums_one[1:2],
            query_sums,
            value_sums,
            sums_two[2:3],
            sums_two[1:2],
            sums_two[3:4],
        ],
        axis=0,
    )
    block = jnp.concatenate(
        [rows_of.reshape(8, n, wide // n).transpose(1, 0, 2), hidden_sums], axis=1
    )
    if direct:
        total = lax.dynamic_index_in_dim(block, z, axis=0, keepdims=False)
        for k in range(1, n):
            part = lax.dynamic_index_in_dim(block, lax.rem(z + k, n), axis=0, keepdims=False)
            total = total + shift(part, k)
        block = total
    else:
        block = lax.psum_scatter(block, "fsdp", scatter_dimension=0)
    block = block + core(block)
    block = block + near(block)
    block = block + across(block)
    return (
        output,
        grad_tokens,
        grad_qkv,
        grad_out,
        grad_fc1,
        grad_fc2,
        block[:2],
        block[2:8],
        block[8:].reshape(-1),
    )


def solution(mesh):
    reps, n, seqs = (mesh.shape[axis] for axis in ("rep", "fsdp", "seq"))
    assert reps == 4 and seqs == 2
    fine = Mesh(mesh.devices.reshape(reps // 2, 2, n, seqs), ("x", "core", "fsdp", "seq"))
    slots = P(("x", "core", "fsdp"), "seq", None)
    first, second = P("fsdp", None), P(None, "fsdp")
    return jax.shard_map(
        functools.partial(on_device, n),
        mesh=fine,
        in_specs=(
            slots,
            P(("x", "core", "fsdp")),
            slots,
            first,
            first,
            first,
            first,
            second,
            second,
            P("fsdp"),
        ),
        out_specs=(slots, slots, first, first, first, first, second, second, P("fsdp")),
        check_vma=False,
    )
```

time: 515 us -> 388 us (0.75); the launches traced: 508 us -> 387 us
  waiting for transfers between devices: 183 us -> 123 us
  starting transfers between devices: 120 us -> 87.4 us
  local copies, waits for them, and re-layouts: 44.6 us -> 17.5 us
  other arithmetic: 10.5 us -> 3.82 us
  Pallas kernels: 147 us -> 153 us
    ppermute x90 -> x54, waiting for transfers between devices: 126 us -> 65 us  [the longest x21 39.9 us: across(): return lax.ppermute(v, 'x', swap)]
    ppermute x30 -> x24, starting transfers between devices: 74.3 us -> 42.8 us  [shift(): return lax.ppermute(v, 'fsdp', [(i, (i + k) % n) for i in range(n)])]
    pallas_call x0 -> x6, Pallas kernels: none -> 17 us  [the longest x4 11.6 us: place(): pl.pallas_call(functools.partial(place_kernel, kind), grid_spec=pltpu.Pre...]
    unnamed x252 -> x127, local copies, waits for them, and re-layouts: 25.2 us -> 9.71 us
    pallas_call x22 -> x18, Pallas kernels: 118 us -> 106 us  [call(): pl.pallas_call(body, out_shape=outs, in_specs=specs, out_specs=out_specs...]
    convert_element_type x7 -> x0, local copies, waits for them, and re-layouts: 11 us -> none  [the longest x1 2.81 us: on_device(): lax.dynamic_slice_in_dim(w_fc2, y * 4 * h, 4 * h, axis=0).astype(BF)]
    pallas_call x1 -> x2, Pallas kernels: 19.7 us -> 18.2 us  [attend_back(): pl.pallas_call(functools.partial(attend_back_kernel, rows, real), grid_sp...]
    ppermute x30 -> x24, waiting for transfers between devices: 56.9 us -> 58 us  [shift(): return lax.ppermute(v, 'fsdp', [(i, (i + k) % n) for i in range(n)])]
  transfers between devices with their start and end apart: 120 -> 78, of which waited for: 28 -> 25; matrix products, arithmetic and copies ran while one was open for 9% -> 3% of each run, Pallas kernels for 25% -> 33%
where the time goes in v2:
time: 388 us; the launch traced here: 387 us
  Pallas kernels  153 us (39%)
  waiting for transfers between devices  123 us (32%)
  starting transfers between devices  87.4 us (23%)
  local copies, waits for them, and re-layouts  17.5 us (5%)
    pallas_call x18, Pallas kernels, call(): pl.pallas_call(body, out_shape=outs, in_specs=specs, out_specs=out_specs...  106 us
    ppermute x24, waiting for transfers between devices, shift(): return lax.ppermute(v, 'fsdp', [(i, (i + k) % n) for i in range(n)])  58 us
    ppermute x24, starting transfers between devices, shift(): return lax.ppermute(v, 'fsdp', [(i, (i + k) % n) for i in range(n)])  42.8 us
    ppermute x21, waiting for transfers between devices, across(): return lax.ppermute(v, 'x', swap)  39.9 us
    ppermute x21, starting transfers between devices, across(): return lax.ppermute(v, 'x', swap)  21.3 us
    ppermute x14, starting transfers between devices, near(): return lax.ppermute(v, 'seq', swap)  20.5 us
    pallas_call x2, Pallas kernels, attend_back(): pl.pallas_call(functools.partial(attend_back_kernel, rows, real), grid_sp...  18.2 us
    ppermute x14, waiting for transfers between devices, near(): return lax.ppermute(v, 'seq', swap)  16.8 us
  transfers between devices with their start and end apart: 78, of which 25 were waited for; matrix products, arithmetic and copies ran while one was open for 3% of the time, Pallas kernels for 33%

profile of v2, /device:TPU:0, one launch (start us, length us, event | category | flops | bytes accessed | tf_op | source)
XLA Modules:
  0.0 387.1 jit_solution(10020538193954084492)
XLA Ops:
  15.7 6.2 %collective-permute-done.refs_1_ = bf16[272,640]{1,0:T(8,128)(2,1)S(1)} collective-permute-done((bf16[272,640]{1,0:T(8,128)(2,1)}, bf16[272,640]{1,0:T(8,128)(2,1)S(1)}, u32[]{:S(2)}, u32[]{:S(2)}) %collective-permute-start) | collective-permute-done | bytes 348192 | tf_op jit(solution)/shard_map/ppermute | solution.py:633
  23.4 12.0 %collective-permute-done.1.refs_2_ = bf16[272,640]{1,0:T(8,128)(2,1)S(1)} collective-permute-done((bf16[272,640]{1,0:T(8,128)(2,1)}, bf16[272,640]{1,0:T(8,128)(2,1)S(1)}, u32[]{:S(2)}, u32[]{:S(2)}) %collective-permute-start.1) | collective-permute-done | bytes 348192 | tf_op jit(solution)/shard_map/ppermute | solution.py:633
  40.4 6.0 %collective-permute-done.5.refs_6_ = bf16[272,640]{1,0:T(8,128)(2,1)S(1)} collective-permute-done((bf16[272,640]{1,0:T(8,128)(2,1)S(1)}, bf16[272,640]{1,0:T(8,128)(2,1)S(1)}, u32[]{:S(2)}, u32[]{:S(2)}) %collective-permute-start.5) | collective-permute-done | bytes 348192 | tf_op jit(solution)/shard_map/ppermute | solution.py:627
  46.4 6.4 %collective-permute-done.7.refs_7_ = bf16[272,640]{1,0:T(8,128)(2,1)S(1)} collective-permute-done((bf16[272,640]{1,0:T(8,128)(2,1)S(1)}, bf16[272,640]{1,0:T(8,128)(2,1)S(1)}, u32[]{:S(2)}, u32[]{:S(2)}) %collective-permute-start.7) | collective-permute-done | bytes 348192 | tf_op jit(solution)/shard_map/ppermute | solution.py:627
  68.3 7.7 %qkv.1 = (bf16[608,1024]{1,0:T(8,128)(2,1)}, bf16[608,512]{1,0:T(8,128)(2,1)}, bf16[608,512]{1,0:T(8,128)(2,1)}, bf16[608,512]{1,0:T(8,128)(2,1)}) custom-call(s32[3]{0:T(128)} %pad_add_fusion.ids, bf16[304,1024]{1,0:T(8,128)(2,1)} %copy-done.4, bf16[304,1024]{1,0:T(8,128)(2,1)} %copy-done.26, f32[16,1024]{1,0:T(8,128)} %get-tuple-element.105.vec, ...), custom_call_target="tpu_custom_call" | custom-call | flops 8589934592 | bytes 262144 | tf_op jit(solution)/shard_map/qkv/pallas_call | solution.py:79
  76.0 11.5 %attend.1 = (bf16[304,512]{1,0:T(8,128)(2,1)}, bf16[304,512]{1,0:T(8,128)(2,1)}, f32[4,4,304]{2,1,0:T(4,128)}) custom-call(s32[3]{0:T(128)} %pad_add_fusion.ids, bf16[608,512]{1,0:T(8,128)(2,1)} %get-tuple-element.108.queries, bf16[608,512]{1,0:T(8,128)(2,1)} %get-tuple-element.109.keys, bf16[608,512]{1,0:T(8,128)(2,1)} %get-tuple-element.110.values), custom_call_target="tpu_custom_call" | custom-call | flops 8589934592 | bytes 262144 | tf_op jit(solution)/shard_map/attend/pallas_call | solution.py:203
  99.4 10.2 %collective-permute-done.20.refs_2_ = bf16[128,1024]{1,0:T(8,128)(2,1)S(1)} collective-permute-done((bf16[128,1024]{1,0:T(8,128)(2,1)S(1)}, bf16[128,1024]{1,0:T(8,128)(2,1)S(1)}, u32[]{:S(2)}, u32[]{:S(2)}) %collective-permute-start.20) | collective-permute-done | bytes 262176 | tf_op jit(solution)/shard_map/ppermute | solution.py:633
  128.4 8.0 %collective-permute-done.18.n_near.refs_1_ = bf16[304,1024]{1,0:T(8,128)(2,1)S(1)} collective-permute-done((bf16[304,1024]{1,0:T(8,128)(2,1)}, bf16[304,1024]{1,0:T(8,128)(2,1)S(1)}, u32[]{:S(2)}, u32[]{:S(2)}) %collective-permute-start.18) | collective-permute-done | bytes 622624 | tf_op jit(solution)/shard_map/ppermute | solution.py:630
  151.3 18.4 %mlp.1 = (bf16[608,2048]{1,0:T(8,128)(2,1)}, bf16[608,3072]{1,0:T(8,128)(2,1)}, f32[304,1024]{1,0:T(8,128)}, bf16[304,1024]{1,0:T(8,128)(2,1)}, f32[1,2048]{1,0:T(1,128)}) custom-call(s32[3]{0:T(128)} %pad_add_fusion.ids, bf16[304,1024]{1,0:T(8,128)(2,1)} %get-tuple-element.124.n_own.refs_0_, bf16[304,1024]{1,0:T(8,128)(2,1)} %copy-done.25, ...), custom_call_target="tpu_custom_call" | custom-call | flops 8589934592 | bytes 262144 | tf_op jit(solution)/shard_map/mlp/pallas_call | solution.py:79
  180.2 5.5 %grad_fc2_send.1 = bf16[512,1024]{1,0:T(8,128)(2,1)} custom-call(s32[3]{0:T(128)} %pad_add_fusion.ids, bf16[608,2048]{1,0:T(8,128)(2,1)} %get-tuple-element.136.refs_0_.refs_3_.near, bf16[608,3072]{1,0:T(8,128)(2,1)} %collective-permute-done.28.refs_1_.refs_2_.refs_4_, bf16[304,1024]{1,0:T(8,128)(2,1)} %copy-done.5, bf16[304,1024]{1,0:T(8,128)(2,1)} %copy-done.23, ...), custom_call_target="tpu_custom_call" | custom-call | flops 8589934592 | bytes 262144 | tf_op jit(solution)/shard_map/grad_fc2_send/pallas_call | solution.py:79
  186.3 5.9 %grad_fc1_send.1 = bf16[1024,512]{1,0:T(8,128)(2,1)} custom-call(s32[3]{0:T(128)} %pad_add_fusion.ids, bf16[304,1024]{1,0:T(8,128)(2,1)} %get-tuple-element.124.n_own.refs_0_, bf16[304,1024]{1,0:T(8,128)(2,1)} %copy-done.25, bf16[608,3072]{1,0:T(8,128)(2,1)} %collective-permute-done.28.refs_1_.refs_2_.refs_4_, ...), custom_call_target="tpu_custom_call" | custom-call | flops 8589934592 | bytes 262144 | tf_op jit(solution)/shard_map/grad_fc1_send/pallas_call | solution.py:79
  202.2 8.9 %result.1 = (f32[304,1024]{1,0:T(8,128)}, bf16[304,1024]{1,0:T(8,128)(2,1)}) custom-call(s32[3]{0:T(128)} %pad_add_fusion.ids, bf16[608,2048]{1,0:T(8,128)(2,1)} %get-tuple-element.136.refs_0_.refs_3_.near, bf16[608,3072]{1,0:T(8,128)(2,1)} %get-tuple-element.138.far, bf16[1024,1024]{1,0:T(8,128)(2,1)} %bitcast.84, bf16[1024,1024]{1,0:T(8,128)(2,1)} %copy-done.18), custom_call_target="tpu_custom_call" | custom-call | flops 8589934592 | bytes 262144 | tf_op jit(solution)/shard_map/result/pallas_call | solution.py:79
  211.9 9.1 %attend_back.2 = (bf16[2,608,384]{2,1,0:T(8,128)(2,1)}, f32[2,1,384]{2,1,0:T(1,128)}) custom-call(s32[3]{0:T(128)} %pad_add_fusion.ids, bf16[608,512]{1,0:T(8,128)(2,1)} %get-tuple-element.108.queries, bf16[608,512]{1,0:T(8,128)(2,1)} %get-tuple-element.109.keys, bf16[608,512]{1,0:T(8,128)(2,1)} %get-tuple-element.110.values, ...), custom_call_target="tpu_custom_call" | custom-call | flops 8589934592 | bytes 262144 | tf_op jit(solution)/shard_map/attend_back/pallas_call | solution.py:266
  222.0 5.6 %grad_fc2_keep.1 = (f32[128,1024]{1,0:T(8,128)}, bf16[128,1024]{1,0:T(8,128)(2,1)}, bf16[128,1024]{1,0:T(8,128)(2,1)}, bf16[128,1024]{1,0:T(8,128)(2,1)}) custom-call(s32[3]{0:T(128)} %pad_add_fusion.ids, bf16[608,2048]{1,0:T(8,128)(2,1)} %get-tuple-element.136.refs_0_.refs_3_.near, bf16[608,3072]{1,0:T(8,128)(2,1)} %collective-permute-done.28.refs_1_.refs_2_.refs_4_, ...), custom_call_target="tpu_custom_call" | custom-call | flops 8589934592 | bytes 262144 | tf_op jit(solution)/shard_map/grad_fc2_keep/pallas_call | solution.py:79
  227.7 9.1 %attend_back.3 = (bf16[2,608,384]{2,1,0:T(8,128)(2,1)}, f32[2,1,384]{2,1,0:T(1,128)}) custom-call(s32[3]{0:T(128)} %pad_add_fusion.ids, bf16[608,512]{1,0:T(8,128)(2,1)} %get-tuple-element.108.queries, bf16[608,512]{1,0:T(8,128)(2,1)} %get-tuple-element.109.keys, bf16[608,512]{1,0:T(8,128)(2,1)} %get-tuple-element.110.values, ...), custom_call_target="tpu_custom_call" | custom-call | flops 8589934592 | bytes 262144 | tf_op jit(solution)/shard_map/attend_back/pallas_call | solution.py:266
  237.7 5.7 %grad_fc1_keep.1 = (f32[256,512]{1,0:T(8,128)}, bf16[256,512]{1,0:T(8,128)(2,1)}, bf16[256,512]{1,0:T(8,128)(2,1)}, bf16[256,512]{1,0:T(8,128)(2,1)}) custom-call(s32[3]{0:T(128)} %pad_add_fusion.ids, bf16[304,1024]{1,0:T(8,128)(2,1)} %get-tuple-element.124.n_own.refs_0_, bf16[304,1024]{1,0:T(8,128)(2,1)} %copy-done.25, ...), custom_call_target="tpu_custom_call" | custom-call | flops 8589934592 | bytes 262144 | tf_op jit(solution)/shard_map/grad_fc1_keep/pallas_call | solution.py:79
  245.5 5.7 %grad_qkv_send.1 = bf16[1024,384]{1,0:T(8,128)(2,1)} custom-call(s32[3]{0:T(128)} %pad_add_fusion.ids, bf16[608,1024]{1,0:T(8,128)(2,1)} %get-tuple-element.106.refs_0_, bf16[608,1024]{1,0:T(8,128)(2,1)} %copy-done.19, bf16[2,608,384]{2,1,0:T(8,128)(2,1)} %get-tuple-element.155.refs_2_.near, bf16[2,608,384]{2,1,0:T(8,128)(2,1)} %collective-permute-done.40.refs_3_), custom_call_target="tpu_custom_call" | custom-call | flops 8589934592 | bytes 262144 | tf_op jit(solution)/shard_map/grad_qkv_send/pallas_call | solution.py:79
  251.2 7.1 %qkv_back.1 = (f32[304,1024]{1,0:T(8,128)}, bf16[304,1024]{1,0:T(8,128)(2,1)}) custom-call(s32[3]{0:T(128)} %pad_add_fusion.ids, bf16[2,608,384]{2,1,0:T(8,128)(2,1)} %get-tuple-element.155.refs_2_.near, bf16[2,608,384]{2,1,0:T(8,128)(2,1)} %get-tuple-element.151.far, bf16[2048,640]{1,0:T(8,128)(2,1)} %bitcast.81, bf16[2048,640]{1,0:T(8,128)(2,1)} %copy-done.17), custom_call_target="tpu_custom_call" | custom-call | flops 8589934592 | bytes 262144 | tf_op jit(solution)/shard_map/qkv_back/pallas_call | solution.py:79
  272.6 6.0 %collective-permute-done.65 = bf16[128,1024]{1,0:T(8,128)(2,1)S(1)} collective-permute-done((bf16[128,1024]{1,0:T(8,128)(2,1)S(1)}, bf16[128,1024]{1,0:T(8,128)(2,1)S(1)}, u32[]{:S(2)}, u32[]{:S(2)}) %collective-permute-start.65) | collective-permute-done | bytes 262176 | tf_op jit(solution)/shard_map/ppermute | solution.py:633
  278.7 8.9 %collective-permute-done.66 = bf16[128,1024]{1,0:T(8,128)(2,1)S(1)} collective-permute-done((bf16[128,1024]{1,0:T(8,128)(2,1)S(1)}, bf16[128,1024]{1,0:T(8,128)(2,1)S(1)}, u32[]{:S(2)}, u32[]{:S(2)}) %collective-permute-start.66) | collective-permute-done | bytes 262176 | tf_op jit(solution)/shard_map/ppermute | solution.py:633
  310.0 5.8 %collective-permute-done.76 = f32[12,256]{1,0:T(8,128)S(1)} collective-permute-done((f32[12,256]{1,0:T(8,128)S(1)}, f32[12,256]{1,0:T(8,128)S(1)}, u32[]{:S(2)}, u32[]{:S(2)}) %collective-permute-start.76) | collective-permute-done | bytes 12320 | tf_op jit(solution)/shard_map/ppermute | solution.py:630
  329.9 5.4 %grad_qkv_keep.1 = (f32[256,384]{1,0:T(8,128)}, bf16[256,384]{1,0:T(8,128)(2,1)}, bf16[256,384]{1,0:T(8,128)(2,1)}, bf16[256,384]{1,0:T(8,128)(2,1)}) custom-call(s32[3]{0:T(128)} %pad_add_fusion.ids, bf16[608,1024]{1,0:T(8,128)(2,1)} %get-tuple-element.106.refs_0_, bf16[608,1024]{1,0:T(8,128)(2,1)} %copy-done.19, ...), custom_call_target="tpu_custom_call" | custom-call | flops 8589934592 | bytes 262144 | tf_op jit(solution)/shard_map/grad_qkv_keep/pallas_call | solution.py:79
  345.8 6.2 %collective-permute-done.46 = bf16[256,384]{1,0:T(8,128)(2,1)S(1)} collective-permute-done((bf16[256,384]{1,0:T(8,128)(2,1)}, bf16[256,384]{1,0:T(8,128)(2,1)S(1)}, u32[]{:S(2)}, u32[]{:S(2)}) %collective-permute-start.46) | collective-permute-done | bytes 196640 | tf_op jit(solution)/shard_map/ppermute | solution.py:633
  352.8 13.6 %collective-permute-done.59.refs_2_ = bf16[2,256,128]{2,1,0:T(8,128)(2,1)S(1)} collective-permute-done((bf16[2,256,128]{2,1,0:T(8,128)(2,1)S(1)}, bf16[2,256,128]{2,1,0:T(8,128)(2,1)S(1)}, u32[]{:S(2)}, u32[]{:S(2)}) %collective-permute-start.59) | collective-permute-done | bytes 131104 | tf_op jit(solution)/shard_map/ppermute | solution.py:627
  (344 shorter events, 189.8 us)
Async XLA Ops:
  1.8 35.1 %collective-permute-start.6 = (bf16[304,1024]{1,0:T(8,128)(2,1)S(1)}, bf16[304,1024]{1,0:T(8,128)(2,1)S(1)}, u32[]{:S(2)}, u32[]{:S(2)}) collective-permute-start(bf16[304,1024]{1,0:T(8,128)(2,1)S(1)} %pad.7.own.tokens), channel_id=1, source_target_pairs={{0,1},{1,0},{2,3},{3,2},{4,5},{5,4},{6,7},{7,6},{8,9},{9,8},{10,11... | collective-permute-start | bytes 1867784 | tf_op jit(solution)/shard_map/ppermute | solution.py:630
  10.2 25.2 %collective-permute-start.1 = (bf16[272,640]{1,0:T(8,128)(2,1)}, bf16[272,640]{1,0:T(8,128)(2,1)S(1)}, u32[]{:S(2)}, u32[]{:S(2)}) collective-permute-start(bf16[272,640]{1,0:T(8,128)(2,1)} %cast_qkv.1.refs_0_), channel_id=1, source_target_pairs={{0,4},{2,6},{4,0},{6,2},{1,5},{3,7},{5,1},{7,3},{8,12},{10,14},{12... | collective-permute-start | bytes 1044488 | tf_op jit(solution)/shard_map/ppermute | solution.py:633
  12.8 24.1 %collective-permute-start.2 = (bf16[272,640]{1,0:T(8,128)(2,1)}, bf16[272,640]{1,0:T(8,128)(2,1)S(1)}, u32[]{:S(2)}, u32[]{:S(2)}) collective-permute-start(bf16[272,640]{1,0:T(8,128)(2,1)} %cast_qkv.1.refs_0_), channel_id=1, source_target_pairs={{0,6},{2,0},{4,2},{6,4},{1,7},{3,1},{5,3},{7,5},{8,14},{10,8},{12,... | collective-permute-start | bytes 1044488 | tf_op jit(solution)/shard_map/ppermute | solution.py:633
  14.2 26.2 %collective-permute-start.3 = (bf16[272,640]{1,0:T(8,128)(2,1)}, bf16[272,640]{1,0:T(8,128)(2,1)S(1)}, u32[]{:S(2)}, u32[]{:S(2)}) collective-permute-start(bf16[272,640]{1,0:T(8,128)(2,1)} %cast_qkv.1.refs_0_), channel_id=1, source_target_pairs={{0,16},{16,0},{1,17},{17,1},{2,18},{18,2},{3,19},{19,3},{4,20},{20... | collective-permute-start | bytes 1044488 | tf_op jit(solution)/shard_map/ppermute | solution.py:627
  58.0 29.5 %collective-permute-start.10 = (bf16[256,512]{1,0:T(8,128)(2,1)}, bf16[256,512]{1,0:T(8,128)(2,1)S(1)}, u32[]{:S(2)}, u32[]{:S(2)}) collective-permute-start(bf16[256,512]{1,0:T(8,128)(2,1)} %get-tuple-element.117.refs_0_), channel_id=1, source_target_pairs={{0,2},{2,4},{4,6},{6,0},{1,3},{3,5},{5,7},{7,1},{8,10},{10,12},{12... | collective-permute-start | bytes 786440 | tf_op jit(solution)/shard_map/ppermute | solution.py:633
  63.0 24.5 %collective-permute-start.11 = (bf16[256,512]{1,0:T(8,128)(2,1)}, bf16[256,512]{1,0:T(8,128)(2,1)S(1)}, u32[]{:S(2)}, u32[]{:S(2)}) collective-permute-start(bf16[256,512]{1,0:T(8,128)(2,1)} %get-tuple-element.117.refs_0_), channel_id=1, source_target_pairs={{0,4},{2,6},{4,0},{6,2},{1,5},{3,7},{5,1},{7,3},{8,12},{10,14},{12... | collective-permute-start | bytes 786440 | tf_op jit(solution)/shard_map/ppermute | solution.py:633
  87.6 23.5 %collective-permute-start.13 = (bf16[304,512]{1,0:T(8,128)(2,1)}, bf16[304,512]{1,0:T(8,128)(2,1)S(1)}, u32[]{:S(2)}, u32[]{:S(2)}) collective-permute-start(bf16[304,512]{1,0:T(8,128)(2,1)} %get-tuple-element.118.mixed_near), channel_id=1, source_target_pairs={{0,1},{1,0},{2,3},{3,2},{4,5},{5,4},{6,7},{7,6},{8,9},{9,8},{10,11... | collective-permute-start | bytes 933896 | tf_op jit(solution)/shard_map/ppermute | solution.py:630
  92.6 27.3 %collective-permute-start.14 = (bf16[256,512]{1,0:T(8,128)(2,1)}, bf16[256,512]{1,0:T(8,128)(2,1)S(1)}, u32[]{:S(2)}, u32[]{:S(2)}) collective-permute-start(bf16[256,512]{1,0:T(8,128)(2,1)} %get-tuple-element.117.refs_0_), channel_id=1, source_target_pairs={{0,16},{16,0},{1,17},{17,1},{2,18},{18,2},{3,19},{19,3},{4,20},{20... | collective-permute-start | bytes 786440 | tf_op jit(solution)/shard_map/ppermute | solution.py:627
  94.1 27.4 %collective-permute-start.15 = (bf16[256,512]{1,0:T(8,128)(2,1)S(1)}, bf16[256,512]{1,0:T(8,128)(2,1)S(1)}, u32[]{:S(2)}, u32[]{:S(2)}) collective-permute-start(bf16[256,512]{1,0:T(8,128)(2,1)S(1)} %collective-permute-done.10.refs_1_), channel_id=1, source_target_pairs={{0,16},{16,0},{1,17},{17,1},{2,18},{18,2},{3,19},{19,3},{4,20},{20... | collective-permute-start | bytes 786440 | tf_op jit(solution)/shard_map/ppermute | solution.py:627
  97.9 24.2 %collective-permute-start.16 = (bf16[256,512]{1,0:T(8,128)(2,1)S(1)}, bf16[256,512]{1,0:T(8,128)(2,1)S(1)}, u32[]{:S(2)}, u32[]{:S(2)}) collective-permute-start(bf16[256,512]{1,0:T(8,128)(2,1)S(1)} %collective-permute-done.11.refs_2_), channel_id=1, source_target_pairs={{0,16},{16,0},{1,17},{17,1},{2,18},{18,2},{3,19},{19,3},{4,20},{20... | collective-permute-start | bytes 786440 | tf_op jit(solution)/shard_map/ppermute | solution.py:627
  171.5 72.0 %collective-permute-start.39 = (bf16[608,1024]{1,0:T(8,128)(2,1)}, bf16[608,1024]{1,0:T(8,128)(2,1)S(1)}, u32[]{:S(2)}, u32[]{:S(2)}) collective-permute-start(bf16[608,1024]{1,0:T(8,128)(2,1)} %get-tuple-element.106.refs_0_), channel_id=1, source_target_pairs={{0,8},{8,0},{1,9},{9,1},{2,10},{10,2},{3,11},{11,3},{4,12},{12,4},... | collective-permute-start | bytes 3735560 | tf_op jit(solution)/shard_map/ppermute | solution.py:624
  171.8 86.5 %collective-permute-start.42 = (bf16[304,1024]{1,0:T(8,128)(2,1)}, bf16[304,1024]{1,0:T(8,128)(2,1)}, u32[]{:S(2)}, u32[]{:S(2)}) collective-permute-start(bf16[304,1024]{1,0:T(8,128)(2,1)} %get-tuple-element.130.mixed), channel_id=1, source_target_pairs={{0,8},{8,0},{1,9},{9,1},{2,10},{10,2},{3,11},{11,3},{4,12},{12,4},... | collective-permute-start | bytes 1867784 | tf_op jit(solution)/shard_map/ppermute | solution.py:624
  185.7 35.3 %collective-permute-start.34 = (bf16[512,1024]{1,0:T(8,128)(2,1)}, bf16[512,1024]{1,0:T(8,128)(2,1)S(1)}, u32[]{:S(2)}, u32[]{:S(2)}) collective-permute-start(bf16[512,1024]{1,0:T(8,128)(2,1)} %grad_fc2_send.1), channel_id=1, source_target_pairs={{0,16},{16,0},{1,17},{17,1},{2,18},{18,2},{3,19},{19,3},{4,20},{20... | collective-permute-start | bytes 3145736 | tf_op jit(solution)/shard_map/ppermute | solution.py:627
  192.2 45.4 %collective-permute-start.35 = (bf16[1024,512]{1,0:T(8,128)(2,1)}, bf16[1024,512]{1,0:T(8,128)(2,1)}, u32[]{:S(2)}, u32[]{:S(2)}) collective-permute-start(bf16[1024,512]{1,0:T(8,128)(2,1)} %grad_fc1_send.1), channel_id=1, source_target_pairs={{0,16},{16,0},{1,17},{17,1},{2,18},{18,2},{3,19},{19,3},{4,20},{20... | collective-permute-start | bytes 3145736 | tf_op jit(solution)/shard_map/ppermute | solution.py:627
  211.2 49.1 %collective-permute-start.43 = (bf16[304,1024]{1,0:T(8,128)(2,1)}, bf16[304,1024]{1,0:T(8,128)(2,1)}, u32[]{:S(2)}, u32[]{:S(2)}) collective-permute-start(bf16[304,1024]{1,0:T(8,128)(2,1)} %get-tuple-element.168.branch), channel_id=1, source_target_pairs={{0,8},{8,0},{1,9},{9,1},{2,10},{10,2},{3,11},{11,3},{4,12},{12,4},... | collective-permute-start | bytes 1867784 | tf_op jit(solution)/shard_map/ppermute | solution.py:624
  221.0 22.5 %collective-permute-start.40 = (bf16[2,608,384]{2,1,0:T(8,128)(2,1)}, bf16[2,608,384]{2,1,0:T(8,128)(2,1)}, u32[]{:S(2)}, u32[]{:S(2)}) collective-permute-start(bf16[2,608,384]{2,1,0:T(8,128)(2,1)} %get-tuple-element.151.far), channel_id=1, source_target_pairs={{0,8},{8,0},{1,9},{9,1},{2,10},{10,2},{3,11},{11,3},{4,12},{12,4},... | collective-permute-start | bytes 2801672 | tf_op jit(solution)/shard_map/ppermute | solution.py:624
  237.6 67.7 %collective-permute-start.32 = (bf16[304,1024]{1,0:T(8,128)(2,1)}, bf16[304,1024]{1,0:T(8,128)(2,1)S(1)}, u32[]{:S(2)}, u32[]{:S(2)}) collective-permute-start(bf16[304,1024]{1,0:T(8,128)(2,1)} %get-tuple-element.146), channel_id=1, source_target_pairs={{0,1},{1,0},{2,3},{3,2},{4,5},{5,4},{6,7},{7,6},{8,9},{9,8},{10,11... | collective-permute-start | bytes 1867784 | tf_op jit(solution)/shard_map/ppermute | solution.py:630
  243.5 23.9 %collective-permute-start.36 = (bf16[256,512]{1,0:T(8,128)(2,1)}, bf16[256,512]{1,0:T(8,128)(2,1)S(1)}, u32[]{:S(2)}, u32[]{:S(2)}) collective-permute-start(bf16[256,512]{1,0:T(8,128)(2,1)} %get-tuple-element.158), channel_id=1, source_target_pairs={{0,2},{2,4},{4,6},{6,0},{1,3},{3,5},{5,7},{7,1},{8,10},{10,12},{12... | collective-permute-start | bytes 786440 | tf_op jit(solution)/shard_map/ppermute | solution.py:633
  243.6 24.5 %collective-permute-start.37 = (bf16[256,512]{1,0:T(8,128)(2,1)}, bf16[256,512]{1,0:T(8,128)(2,1)S(1)}, u32[]{:S(2)}, u32[]{:S(2)}) collective-permute-start(bf16[256,512]{1,0:T(8,128)(2,1)} %get-tuple-element.159), channel_id=1, source_target_pairs={{0,4},{2,6},{4,0},{6,2},{1,5},{3,7},{5,1},{7,3},{8,12},{10,14},{12... | collective-permute-start | bytes 786440 | tf_op jit(solution)/shard_map/ppermute | solution.py:633
  260.4 31.0 %collective-permute-start.41 = (bf16[304,1024]{1,0:T(8,128)(2,1)}, bf16[304,1024]{1,0:T(8,128)(2,1)S(1)}, u32[]{:S(2)}, u32[]{:S(2)}) collective-permute-start(bf16[304,1024]{1,0:T(8,128)(2,1)} %get-tuple-element.165), channel_id=1, source_target_pairs={{0,1},{1,0},{2,3},{3,2},{4,5},{5,4},{6,7},{7,6},{8,9},{9,8},{10,11... | collective-permute-start | bytes 1867784 | tf_op jit(solution)/shard_map/ppermute | solution.py:630
  307.0 32.2 %collective-permute-start.61 = (bf16[256,512]{1,0:T(8,128)(2,1)S(1)}, bf16[256,512]{1,0:T(8,128)(2,1)S(1)}, u32[]{:S(2)}, u32[]{:S(2)}) collective-permute-start(bf16[256,512]{1,0:T(8,128)(2,1)S(1)} %add_convert_fusion.1), channel_id=1, source_target_pairs={{0,1},{1,0},{2,3},{3,2},{4,5},{5,4},{6,7},{7,6},{8,9},{9,8},{10,11... | collective-permute-start | bytes 786440 | tf_op jit(solution)/shard_map/ppermute | solution.py:630
  315.8 24.2 %collective-permute-start.77 = (f32[12,256]{1,0:T(8,128)S(1)}, f32[12,256]{1,0:T(8,128)S(1)}, u32[]{:S(2)}, u32[]{:S(2)}) collective-permute-start(f32[12,256]{1,0:T(8,128)S(1)} %add.149), channel_id=1, source_target_pairs={{0,16},{16,0},{1,17},{17,1},{2,18},{18,2},{3,19},{19,3},{4,20},{20... | collective-permute-start | bytes 36872 | tf_op jit(solution)/shard_map/ppermute | solution.py:627
  340.0 28.7 %collective-permute-start.70 = (bf16[2,128,1024]{2,1,0:T(8,128)(2,1)S(1)}, bf16[2,128,1024]{2,1,0:T(8,128)(2,1)S(1)}, u32[]{:S(2)}, u32[]{:S(2)}) collective-permute-start(bf16[2,128,1024]{2,1,0:T(8,128)(2,1)S(1)} %pad_maximum_fusion.1.refs_0_), channel_id=1, source_target_pairs={{0,16},{16,0},{1,17},{17,1},{2,18},{18,2},{3,19},{19,3},{4,20},{20... | collective-permute-start | bytes 1572872 | tf_op jit(solution)/shard_map/ppermute | solution.py:627
  343.6 25.2 %collective-permute-start.63 = (bf16[2,256,512]{2,1,0:T(8,128)(2,1)S(1)}, bf16[2,256,512]{2,1,0:T(8,128)(2,1)S(1)}, u32[]{:S(2)}, u32[]{:S(2)}) collective-permute-start(bf16[2,256,512]{2,1,0:T(8,128)(2,1)S(1)} %pad_maximum_fusion.refs_0_), channel_id=1, source_target_pairs={{0,16},{16,0},{1,17},{17,1},{2,18},{18,2},{3,19},{19,3},{4,20},{20... | collective-permute-start | bytes 1572872 | tf_op jit(solution)/shard_map/ppermute | solution.py:627
  (112 other events, 1223.6 us)

commit v3 on v2

v3 whole, which is shorter than its diff:
```python
import functools

import jax
import jax.numpy as jnp
from jax import lax
from jax.experimental import pallas as pl
from jax.experimental.pallas import tpu as pltpu
from jax.sharding import Mesh
from jax.sharding import PartitionSpec as P

HEADS = 16
HEAD_DIM = 64
IMG_TOK = 577
EPSILON = 1e-05
NEGATIVE = -1e30
LANES = 128
BF = jnp.bfloat16
F32 = jnp.float32

ANY = pl.BlockSpec(memory_space=pl.ANY)
VM = pl.BlockSpec(memory_space=pltpu.VMEM)
SM = pl.BlockSpec(memory_space=pltpu.SMEM)

ORDER = (0, 2, 1, 3)
OUT_LANE = 3 * LANES
PEERS = ((0, 0), (1, 0), (0, 2), (1, 2))


def mm(a, b):
    return lax.dot_general(a, b, (((1,), (0,)), ((), ())), preferred_element_type=F32)


def mmt(a, b):
    return lax.dot_general(a, b, (((1,), (1,)), ((), ())), preferred_element_type=F32)


def tmm(a, b):
    return lax.dot_general(a, b, (((0,), (0,)), ((), ())), preferred_element_type=F32)


def normalize(inputs):
    center = inputs - jnp.mean(inputs, axis=-1, keepdims=True)
    inverse = lax.rsqrt(jnp.mean(center * center, axis=-1, keepdims=True) + EPSILON)
    return center * inverse, inverse


def norm_back(grad_in, scaled, inverse, gain_row):
    weighted = grad_in * gain_row
    return inverse * (
        weighted
        - jnp.mean(weighted, axis=-1, keepdims=True)
        - scaled * jnp.mean(weighted * scaled, axis=-1, keepdims=True)
    )


def at(index, size):
    return pl.ds(pl.multiple_of(index * size, size), size)


def flip(r, d):
    return jnp.bitwise_xor(r, d) if d else r


def fetch(copies, sems):
    handles = [pltpu.make_async_copy(s, t, sems.at[i]) for i, (s, t) in enumerate(copies)]
    for handle in handles:
        handle.start()
    return handles


def finish(handles):
    for handle in handles:
        handle.wait()


KNOBS = {"places": 1, "factor": 1.0, "floor": 8.0, "gnear": 1, "n2": 0, "x2": 0, "place": 0.3, "grad_out": 1.0, "ago": 0, "a1": 1, "a3": 0}
TIMES = {
    "qkv": 7.7, "attend": 11.3, "project": 4.9, "mlp": 18.6, "grad_fc2": 6.9,
    "middle_back": 5.4, "grad_fc1_send": 5.9, "grad_out": 4.9, "attend_back": 16.9,
    "grad_qkv_send": 5.7, "qkv_back": 7.1, "grad_fc1_keep": 5.7, "grad_qkv_keep": 5.3,
    "tokens_back": 3.8, "combine": 2.1, "small": 1.5, "place": 3.2, "stack_qkv": 3.4,
    "stack_rest": 4.5, "cast_qkv": 2.7, "cast_rest": 2.7,
}


def on(name, default=1):
    return KNOBS.get(name, default)


def cost(name):
    value = max(TIMES[name], KNOBS.get("floor", 0.0)) * KNOBS.get("factor", 0.25)
    flops = int(value * KNOBS.get(name, 1.0) * 1.15e9)
    return pl.CostEstimate(flops=flops, bytes_accessed=1 << 18, transcendentals=0)


def skipping(body, count, extra):
    def kernel(*refs):
        body(*refs[:count], *refs[count + extra :])

    return kernel if extra else body


def call(body, ins, specs, outs, scratch, name, out_specs=None, first=()):
    return pl.pallas_call(
        skipping(body, len(ins), len(first)),
        out_shape=outs,
        in_specs=specs + [ANY] * len(first),
        out_specs=out_specs or [VM] * len(outs),
        scratch_shapes=scratch,
        compiler_params=pltpu.CompilerParams(vmem_limit_bytes=56 << 20),
        cost_estimate=cost(name),
        name=name,
    )(*ins, *first)


def grid_call(body, ids, ins, specs, outs, out_specs, steps, name, scratch=(), first=()):
    return pl.pallas_call(
        skipping(body, len(ins) + 1, len(first)),
        grid_spec=pltpu.PrefetchScalarGridSpec(
            num_scalar_prefetch=1,
            grid=(steps,),
            in_specs=specs + [ANY] * len(first),
            out_specs=out_specs,
            scratch_shapes=list(scratch),
        ),
        out_shape=outs,
        compiler_params=pltpu.CompilerParams(vmem_limit_bytes=56 << 20),
        cost_estimate=cost(name),
        name=name,
    )(ids, *ins, *first)


def shape(dims, dtype):
    return jax.ShapeDtypeStruct(dims, dtype)


def column_copies(refs, w, ids, lane=0, relative=False):
    rows, q = w.shape[0], w.shape[1] // 4
    copies = []
    for d in range(4):
        slot = pl.ds(ORDER.index(d) * q, q) if relative else at(flip(ids[0], d), q)
        source = refs[d & 1].at[pl.ds((d >> 1) * rows, rows), pl.ds(lane, q)]
        copies.append((source, w.at[:, slot]))
    return copies


def rest_copies(refs, w1, w2, ids, n, sems):
    rows, wide = w1.shape[0], w1.shape[1] // 4
    half, h = w2.shape[1] // 2, w2.shape[0] // (4 * n)
    for d in range(4):
        q = flip(ids[0], d)
        x = jnp.bitwise_xor(ids[0] >> 1, d >> 1)
        source = refs[d & 1].at[at(x, rows), pl.ds(0, wide)]
        pltpu.make_async_copy(source, w1.at[:, at(q, wide)], sems.at[d]).start()
        for i in range(n):
            for side in range(2):
                first = pl.multiple_of(x * rows + (i * 2 + side) * h, h)
                source = refs[d & 1].at[pl.ds(first, h), pl.ds(wide, half)]
                target = w2.at[at(q * n + i, h), pl.ds(side * half, half)]
                pltpu.make_async_copy(source, target, sems.at[4 + d]).start()


def row_copies(refs, w, ids):
    q = w.shape[0] // 4
    return [
        (refs[d & 1].at[pl.ds((d >> 1) * q, q), :], w.at[at(flip(ids[0], d), q), :])
        for d in range(4)
    ]


def split(refs, *counts):
    refs = list(refs)
    out = []
    for count in counts:
        out.append(refs[:count])
        refs = refs[count:]
    return out + [refs]


def qkv_kernel(ids, own, near, vec, *refs):
    weights, (normed, queries, keys, values), (w, sems) = split(refs, 2, 4)
    handles = fetch(column_copies(weights, w, ids), sems)
    rows = own.shape[0]
    for i, part in enumerate((own, near)):
        scaled, _ = normalize(part[...].astype(F32))
        normed[i * rows : (i + 1) * rows, :] = (scaled * vec[0:1, :] + vec[2:3, :]).astype(BF)
    finish(handles)
    scale = HEAD_DIM ** (-0.5)
    first = ids[1] * (queries.shape[1] // LANES)

    def step(i, carry):
        joined = mm(normed[...], w[:, at(i, 3 * LANES)])
        here = at(i, LANES)
        there = at(first + i, LANES)
        queries[:, here] = ((joined[:, :LANES] + vec[3:4, there]) * scale).astype(BF)
        keys[:, here] = joined[:, LANES : 2 * LANES].astype(BF)
        values[:, here] = (joined[:, 2 * LANES :] + vec[4:5, there]).astype(BF)
        return carry

    lax.fori_loop(0, 4, step, 0)


def valid_keys(ids, rows, real):
    index = lax.broadcasted_iota(jnp.int32, (2 * rows, 1), 0)
    second = (index >= rows).astype(jnp.int32)
    local = index - second * rows
    position = jnp.bitwise_xor(second, ids[1]) * real + local
    return (local < real) & (position < IMG_TOK)


def head_half(value, half):
    lane = lax.broadcasted_iota(jnp.int32, value.shape, 1)
    keep = (lane < HEAD_DIM) if half == 0 else (lane >= HEAD_DIM)
    return jnp.where(keep, value, jnp.zeros_like(value))


def with_lanes(value, half, columns):
    lane = lax.broadcasted_iota(jnp.int32, value.shape, 1)
    out = head_half(value, half)
    for i, column in enumerate(columns):
        out = jnp.where(lane == (1 - half) * HEAD_DIM + i, column, out)
    return out


def three_parts(column):
    high = column.astype(BF)
    rest = column - high.astype(F32)
    middle = rest.astype(BF)
    return [high, middle, (rest - middle.astype(F32)).astype(BF)]


def key_shift(ids, rows, real):
    shift = jnp.where(valid_keys(ids, rows, real), 0.0, NEGATIVE)
    return shift.astype(BF)


def attend_kernel(rows, real, ids, queries, keys, values, mixed_own, mixed_near, totals):
    one = jnp.ones((1, 1), BF)
    shift = key_shift(ids, rows, real)
    keys_of = [with_lanes(keys[...], half, [shift]) for half in range(2)]
    values_of = [head_half(values[...], half) for half in range(2)]
    for i, target in enumerate((mixed_own, mixed_near)):
        block = queries[i * rows : (i + 1) * rows, :]
        total = None
        for half in range(2):
            scores = mmt(keys_of[half], with_lanes(block, half, [one]))
            highest = jnp.max(scores, axis=0, keepdims=True)
            exponent = jnp.exp(scores - highest)
            sums = jnp.sum(exponent, axis=0, keepdims=True)
            totals[2 * half + i : 2 * half + i + 1, :] = highest + jnp.log(sums)
            part = tmm(values_of[half], exponent.astype(BF)) * (1.0 / sums)
            total = part if total is None else total + part
        target[...] = total.T.astype(BF)


def attend(ids, queries, keys, values, rows, real, first):
    wide = queries.shape[1]
    steps = wide // LANES
    block = pl.BlockSpec((2 * rows, LANES), lambda i, ids: (0, i))
    half = pl.BlockSpec((rows, LANES), lambda i, ids: (0, i))
    return grid_call(
        functools.partial(attend_kernel, rows, real),
        ids,
        [queries, keys, values],
        [block] * 3,
        [shape((rows, wide), BF)] * 2 + [shape((steps, 4, rows), F32)],
        [half] * 2 + [pl.BlockSpec((None, 4, rows), lambda i, ids: (i, 0, 0))],
        steps,
        "attend",
        first=first,
    )


def attend_back_kernel(
    rows, real, ids, queries, keys, values, mixed_own, mixed_near, grad_own, grad_near,
    totals, near, far, sums,
):
    step = pl.program_id(0)
    one = jnp.ones((1, 1), BF)
    shift = key_shift(ids, rows, real)
    keys_of = [head_half(keys[...], half) for half in range(2)]
    wide_keys = [with_lanes(keys[...], half, [shift, one, one, one]) for half in range(2)]
    wide_values = [with_lanes(values[...], half, [one, one, one]) for half in range(2)]
    lines = jnp.concatenate([totals[...], jnp.zeros_like(totals[...])], axis=0).T
    grad_k = grad_v = None
    grad_q = []
    for part, (mixed, grad_ref) in enumerate(((mixed_own, grad_own), (mixed_near, grad_near))):
        block = queries[part * rows : (part + 1) * rows, :]
        grad = grad_ref[...]
        product = grad.astype(F32) * mixed[...].astype(F32)
        total = None
        for half in range(2):
            line = three_parts(-lines[:, 2 * half + part : 2 * half + part + 1])
            probs = jnp.exp(mmt(wide_keys[half], with_lanes(block, half, [one, *line])))
            inner = jnp.sum(head_half(product, half), axis=1, keepdims=True)
            wide_grad = with_lanes(grad, half, three_parts(-inner))
            grad_scores = (probs * mmt(wide_values[half], wide_grad)).astype(BF)
            first = tmm(keys_of[half], grad_scores)
            total = first if total is None else total + first
            second = mm(grad_scores, head_half(block, half))
            third = mm(probs.astype(BF), head_half(grad, half))
            grad_k = second if grad_k is None else grad_k + second
            grad_v = third if grad_v is None else grad_v + third
        grad_q.append(total.T)
    scale = HEAD_DIM ** (-0.5)
    grad_q = jnp.concatenate(grad_q, axis=0).astype(BF).astype(F32) * scale
    pieces = [grad_q.astype(BF), grad_k.astype(BF), grad_v.astype(BF)]
    for kind, piece in enumerate(pieces):
        columns = slice(kind * LANES, (kind + 1) * LANES)
        sums[:, columns] = jnp.sum(piece.astype(F32), axis=0, keepdims=True)

        @pl.when(step < 2)
        def _():
            near[:, columns] = piece

        @pl.when(step >= 2)
        def _():
            far[:, columns] = piece


def attend_back(ids, saved, mixed, grads, totals, rows, real, first):
    def index(i, ids):
        return jnp.bitwise_xor(ids[0], ((i & 1) << 1) | (i >> 1))

    block = pl.BlockSpec((2 * rows, LANES), lambda i, ids: (0, index(i, ids)))
    half = pl.BlockSpec((rows, LANES), lambda i, ids: (0, index(i, ids)))
    lines = pl.BlockSpec((None, 4, rows), lambda i, ids: (index(i, ids), 0, 0))
    line = pl.BlockSpec((None, 1, 3 * LANES), lambda i, ids: (i, 0, 0))
    pair = (2, 2 * rows, 3 * LANES)
    near = pl.BlockSpec((None,) + pair[1:], lambda i, ids: (jnp.minimum(i, 1), 0, 0))
    far = pl.BlockSpec((None,) + pair[1:], lambda i, ids: (jnp.maximum(i - 2, 0), 0, 0))
    return grid_call(
        functools.partial(attend_back_kernel, rows, real),
        ids,
        [*saved, *mixed, *grads, totals],
        [block] * 3 + [half] * 4 + [lines],
        [shape(pair, BF), shape(pair, BF), shape((4, 1, 3 * LANES), F32)],
        [near, far, line],
        4,
        "attend_back",
        first=first,
    )


def project_kernel(ids, tokens, mixed_own, mixed_near, vec, *refs):
    weights, (mixed, middle, normed), (w, sems) = split(refs, 2, 3)
    handles = fetch(column_copies(weights, w, ids, OUT_LANE), sems)
    y = ids[1]
    half = mixed_own.shape[1]
    mixed[:, at(y, half)] = mixed_own[...]
    mixed[:, at(1 - y, half)] = mixed_near[...]
    finish(handles)
    total = tokens[...].astype(F32) + (mm(mixed[...], w[...]) + vec[5:6, :])
    middle[...] = total
    scaled, _ = normalize(total)
    normed[...] = (scaled * vec[1:2, :] + vec[6:7, :]).astype(BF)


def mlp_kernel(n, joint, ids, n_own, n_near, g_own, g_near, fb, *refs):
    ones, twos, outs, scratch = split(refs, 2, 0 if joint else 2, 7)
    near, far, grad_own, grad_near, result_own, result_near, sums = outs
    w1, w2, normed, grads, total, result, stage, sems, out_sems = scratch
    r = ids[0]
    rows = n_own.shape[0]
    if joint:
        rest_copies(ones, w1, w2, ids, n, sems)
    else:
        fetch(column_copies(ones, w1, ids) + row_copies(twos, w2, ids), sems)
    normed[:rows, :] = n_own[...]
    normed[rows:, :] = n_near[...]
    wide = w1.shape[1] // 4
    grads[:rows, :] = g_own[...]
    grads[rows:, :] = g_near[...]
    total[...] = jnp.zeros_like(total)
    result[...] = jnp.zeros_like(result)

    def out_copy(target, d, kind):
        place = at(2 * kind + (d >> 1), wide)
        return pltpu.make_async_copy(
            stage.at[2 * d + kind], target.at[:, place], out_sems.at[2 * d + kind]
        )

    def step(d, carry):
        here = at(jnp.bitwise_xor(r, d), wide)
        pltpu.make_async_copy(w1.at[:, here], w1.at[:, here], sems.at[d]).wait()
        pltpu.make_async_copy(w2.at[here, :], w2.at[here, :], sems.at[4 + d]).wait()
        hidden = mm(normed[...], w1[:, here]) + fb[:, here]
        gate = 1.0 / (1.0 + jnp.exp(-1.702 * hidden))
        active = (hidden * gate).astype(BF)
        stage[2 * d + 1] = active
        result[...] += mm(active, w2[here, :])
        grad_active = mmt(grads[...], w2[here, :])
        grad_hidden = (
            grad_active * (gate + 1.702 * hidden * gate * (1.0 - gate))
        ).astype(BF)
        stage[2 * d] = grad_hidden
        sums[:, here] = jnp.sum(grad_hidden.astype(F32), axis=0, keepdims=True)
        total[...] += mmt(grad_hidden, w1[:, here])
        for kind in range(2):

            @pl.when((d & 1) == 0)
            def _():
                out_copy(near, d, kind).start()

            @pl.when((d & 1) == 1)
            def _():
                out_copy(far, d, kind).start()

        return carry

    lax.fori_loop(0, 4, step, 0)
    grad_own[...] = total[:rows, :]
    grad_near[...] = total[rows:, :].astype(BF)
    result_own[...] = result[:rows, :]
    result_near[...] = result[rows:, :].astype(BF)
    for d in range(4):
        for kind in range(2):
            out_copy(far if d & 1 else near, d, kind).wait()


def middle_back_kernel(ids, grad_own, grad_recv, middle, incoming, vec, *refs):
    weights, outs, (w, work, sems) = split(refs, 2, 5)
    grad_middle, branch, mixed_own, mixed_near, sums = outs
    handles = fetch(column_copies(weights, w, ids, OUT_LANE), sems)
    y = ids[1]
    grad = grad_own[...] + grad_recv[...].astype(F32)
    scaled, inverse = normalize(middle[...])
    sums[0:1, :] = jnp.sum(grad * scaled, axis=0, keepdims=True)
    sums[1:2, :] = jnp.sum(grad, axis=0, keepdims=True)
    arriving = incoming[...].astype(F32)
    sums[3:4, :] = jnp.sum(arriving, axis=0, keepdims=True)
    total = arriving + norm_back(grad, scaled, inverse, vec[1:2, :])
    grad_middle[...] = total
    low = total.astype(BF)
    branch[...] = low
    sums[2:3, :] = jnp.sum(low.astype(F32), axis=0, keepdims=True)
    finish(handles)
    work[...] = mmt(branch[...], w[...]).astype(BF)
    half = work.shape[1] // 2
    mixed_own[...] = work[:, at(y, half)]
    mixed_near[...] = work[:, at(1 - y, half)]


def qkv_back_kernel(ids, near, far, *refs):
    weights, (own, other), (w, grads, sems) = split(refs, 2, 2)
    wide = near.shape[2]
    copies = column_copies(weights, w, ids, relative=True)
    for s in range(4):
        source = (near if s < 2 else far).at[s % 2]
        copies.append((source, grads.at[:, pl.ds(s * wide, wide)]))
    finish(fetch(copies, sems))
    rows = own.shape[0]
    step_rows = 256

    def step(i, carry):
        here = at(i, step_rows)
        value = mmt(grads[...], w[here, :])
        own[:, here] = value[:rows, :]
        other[:, here] = value[rows:, :].astype(BF)
        return carry

    lax.fori_loop(0, w.shape[0] // step_rows, step, 0)


def tokens_back_kernel(ids, grad_own, grad_recv, tokens, grad_middle, vec, out, sums):
    grad = grad_own[...] + grad_recv[...].astype(F32)
    scaled, inverse = normalize(tokens[...].astype(F32))
    sums[0:1, :] = jnp.sum(grad * scaled, axis=0, keepdims=True)
    sums[1:2, :] = jnp.sum(grad, axis=0, keepdims=True)
    total = grad_middle[...] + norm_back(grad, scaled, inverse, vec[0:1, :])
    out[...] = total.astype(BF)[: out.shape[0], :]


def window(ref, pick):
    if pick is None:
        return ref
    if len(ref.shape) == 3:
        return ref.at[pick]
    return ref.at[:, pl.ds(*pick)]


def extent(array, pick):
    if pick is None:
        return array.shape
    if array.ndim == 3:
        return array.shape[1:]
    return (array.shape[0], pick[1])


def weight_kernel(left_picks, right_picks, more, slots, ids, *refs):
    left_refs, right_refs, extra, rest = split(refs, len(left_picks), len(right_picks), more)
    *outs, a, b, sems = rest
    copies = []
    for parts, target, picks in ((left_refs, a, left_picks), (right_refs, b, right_picks)):
        start = 0
        for part, pick in zip(parts, picks):
            source = window(part, pick)
            count = source.shape[0]
            copies.append((source, target.at[pl.ds(start, count), :]))
            start += count
    finish(fetch(copies, sems))
    if len(outs) == 1 and slots > 1:
        size = outs[0].shape[0] // 4
        for i in range(4):
            block = jnp.bitwise_xor(ids[0] >> 1, i // 2) * 2 + i % 2
            value = tmm(a[:, i * size : (i + 1) * size], b[...])
            outs[0][at(block, size), :] = value.astype(outs[0].dtype)
        return
    if len(outs) > 1:
        rows = outs[0].shape[0]
        for k, out in enumerate(outs):
            for slot in range(slots):
                size = rows // slots
                here = at(slot * len(outs) + lax.rem(ids[2] + k, len(outs)), size)
                value = tmm(a[:, here], b[...])
                if more:
                    value = value + extra[0][here, :].astype(F32)
                out[slot * size : (slot + 1) * size, :] = value.astype(out.dtype)
        return
    (out,) = outs
    step_rows = 256

    def step(i, carry):
        here = at(i, step_rows)
        value = tmm(a[:, here], b[...])
        if more:
            value = value + extra[0][here, :].astype(F32)
        out[here, :] = value.astype(out.dtype)
        return carry

    lax.fori_loop(0, out.shape[0] // step_rows, step, 0)


def weight_grad(ids, left, right, name, extra=(), blocks=1, slots=1, first=()):
    def span(parts):
        dims = [extent(*p) for p in parts]
        return sum(d[0] for d in dims), dims[0][1]

    depth, rows = span(left)
    _, columns = span(right)
    kinds = [F32] + [BF] * (blocks - 1) if blocks > 1 else [BF]
    return call(
        functools.partial(
            weight_kernel, [p for _, p in left], [p for _, p in right], len(extra), slots
        ),
        [ids] + [a for a, _ in left] + [a for a, _ in right] + list(extra),
        [SM] + [ANY] * (len(left) + len(right)) + [VM] * len(extra),
        [shape((rows // blocks, columns), kind) for kind in kinds],
        [
            pltpu.VMEM((depth, rows), BF),
            pltpu.VMEM((depth, columns), BF),
            pltpu.SemaphoreType.DMA((len(left) + len(right),)),
        ],
        name,
        first=first,
    )


def out_grad_kernel(ids, mixed, mixed_far, branch, branch_far, *refs):
    *outs, a, b, sems = refs
    r, y = ids[0], ids[1]
    rows = mixed.shape[0]
    quarters = branch.shape[1] // 2 // LANES
    copies = []
    for i, (left, right) in enumerate(((mixed, branch), (mixed_far, branch_far))):
        here = pl.ds(i * rows, rows)
        copies.append((left, a.at[here, :]))
        for s, (dy, d) in enumerate(PEERS):
            block = flip(y, dy) * quarters + flip(r, d)
            copies.append((right.at[:, at(block, LANES)], b.at[here, pl.ds(s * LANES, LANES)]))
    finish(fetch(copies, sems))
    step_rows = 256

    def step(i, carry):
        here = at(i, step_rows)
        value = tmm(a[:, here], b[...])
        for s, out in enumerate(outs):
            out[here, :] = value[:, s * LANES : (s + 1) * LANES].astype(out.dtype)
        return carry

    lax.fori_loop(0, a.shape[1] // step_rows, step, 0)


def combine_kernel(ids, keep, *refs):
    recvs, outs = refs[:3], refs[3:]
    rows = outs[0].shape[0]
    for k, out in enumerate(outs):
        here = at(lax.rem(ids[2] + k, len(outs)), rows)
        value = keep[here, :]
        for recv in recvs:
            value = value + recv[here, :].astype(F32)
        out[...] = value.astype(out.dtype)


def join(parts):
    return parts[0] if len(parts) == 1 else jnp.concatenate(parts, axis=1)


def cast_qkv_kernel(ids, first, second, third, fourth, gains, biases, shift, out, low):
    rows = first.shape[0]
    out[:rows, :] = join([part[...].astype(BF) for part in (first, second, third, fourth)])
    low[...] = jnp.zeros_like(low)
    width = gains.shape[1]
    low[0:2, :width] = gains[...]
    low[2:8, :width] = biases[...]
    low[8:12, :width] = shift[...]
    out[rows:, :] = low[...].astype(BF)


def cast_rest_kernel(n, ids, *refs):
    ones, (two_part,), (out,) = split(refs, n, 1)
    wide = out.shape[1] // 2
    rows = two_part.shape[0]
    out[:, :wide] = join([part[...].astype(BF) for part in ones])
    out[:rows, wide:] = two_part[:, :wide].astype(BF)
    out[rows:, wide:] = two_part[:, wide:].astype(BF)


def cast(body, ids, blocks, outs, scratch, name, first=()):
    return grid_call(
        body,
        ids,
        [array for array, _, _ in blocks],
        [pl.BlockSpec(block, lambda i, ids, at=at: at(ids)) for _, block, at in blocks],
        outs,
        [pl.BlockSpec(o.shape, lambda i, ids: (0, 0)) for o in outs],
        1,
        name,
        scratch,
        first,
    )


def stack_kernel(n, ids, *refs):
    parts, (out, low) = split(refs, 2 * n)[0], refs[2 * n :]
    rows = out.shape[1]
    width = low.shape[1] // n
    for i, part in enumerate(parts):
        there = lax.rem(ids[2] - i % n + n, n)
        out[(i // n) * n + there] = part[:rows, :]
        if i < n:
            low[:, at(there, width)] = part[rows:, :width].astype(F32)


def stack_rest_kernel(n, ids, *refs):
    parts, (one, two) = split(refs, 2 * n)[0], refs[2 * n :]
    wide, rows = one.shape[2], two.shape[1]
    for i, part in enumerate(parts):
        there = (i // n) * n + lax.rem(ids[2] - i % n + n, n)
        one[there] = part[:, :wide]
        two[there, :, :wide] = part[:rows, wide:]
        two[there, :, wide:] = part[rows:, wide:]


def place_kernel(kind, ids, *refs):
    sources, (out,), _ = split(refs, 8, 1)
    for i, source in enumerate(sources):
        dy, d = PEERS[i % 4]
        block = flip(ids[1], dy) * 4 + flip(ids[0], d + i // 4)
        piece = source[...].astype(F32)
        if kind == "rows":
            out[at(block, piece.shape[0]), :] = piece
            continue
        for g in range(piece.shape[1] // LANES):
            columns = at(block + g * 8, LANES)
            out[:, columns] = piece[:, g * LANES : (g + 1) * LANES]


def place(ids, sources, dims, kind, first):
    rows, columns = sources[0].shape
    steps = 4
    if kind == "rows":
        inside = pl.BlockSpec((rows, columns // steps), lambda i, ids: (0, i))
        outside = pl.BlockSpec((dims[0], dims[1] // steps), lambda i, ids: (0, i))
    else:
        inside = pl.BlockSpec((rows // steps, columns), lambda i, ids: (i, 0))
        outside = pl.BlockSpec((dims[0] // steps, dims[1]), lambda i, ids: (i, 0))
    return grid_call(
        functools.partial(place_kernel, kind),
        ids,
        sources,
        [inside] * 8,
        [shape(dims, F32)],
        [outside],
        steps,
        "place",
        first=first,
    )[0]


def small_kernel(ids, one, two, joined, hidden, *refs):
    *outs, full = refs
    r, y, z = ids[0], ids[1], ids[2]
    n, width = full.shape[0], full.shape[2]
    full[...] = jnp.zeros_like(full)
    for row, (source, line) in {
        0: (one, 0), 1: (two, 0), 2: (one, 1), 5: (two, 2), 6: (two, 1), 7: (two, 3),
    }.items():
        for i in range(n):
            full[i, row : row + 1, :] = source[line : line + 1, i * width : (i + 1) * width]
    slots = [joined[slot] for slot in range(4)]
    for q in range(4):
        value = sum(
            jnp.where(jnp.bitwise_xor(r, d) == q, slots[slot], 0.0) for slot, d in enumerate(ORDER)
        )
        here = slice((q % 2) * LANES, (q % 2 + 1) * LANES)
        for half in range(2):
            mine = jnp.where(y == half, 1.0, 0.0)
            for row, kind in ((3, 0), (4, 2)):
                line = value[:, kind * LANES : (kind + 1) * LANES]
                full[2 * half + q // 2, row : row + 1, here] = line * mine
            row = 8 + 2 * half + q // 2
            for i in range(n):
                line = hidden[:, (q * n + i) * LANES : (q * n + i + 1) * LANES]
                full[i, row : row + 1, here] = line * mine
    for k, out in enumerate(outs):
        out[...] = full[lax.rem(z + k, n)]


def on_device(n, tokens, slot_mask, cotangent, w_qkv, w_out, w_fc1, w_fc2, ln_gains, biases, fc1_bias):
    slot_count, real, wide = tokens.shape
    assert slot_count == 1
    direct = n == 4
    joint = direct and bool(on("scf"))
    whole_two = direct and bool(on("sc2"))
    rows = -(-real // 16) * 16
    hidden = fc1_bias.shape[0] * n
    half, part_hidden = wide // 2, hidden // 2
    h = hidden // n // 8
    x, c = lax.axis_index("x"), lax.axis_index("core")
    y, z = lax.axis_index("seq"), lax.axis_index("fsdp")
    r = 2 * x + c
    ids = jnp.stack([r, y, z]).astype(jnp.int32)
    swap = [(0, 1), (1, 0)]

    def core(v):
        return lax.ppermute(v, "core", swap)

    def across(v):
        return lax.ppermute(v, "x", swap)

    def near(v):
        return lax.ppermute(v, "seq", swap)

    def diagonal(v):
        return lax.ppermute(v, ("x", "seq"), [(i, i ^ 3) for i in range(4)])

    def shift(v, k):
        return lax.ppermute(v, "fsdp", [(i, (i + k) % n) for i in range(n)])

    def scatter_rows(outs, *gate):
        if len(outs) == 1:
            value = lax.psum_scatter(outs[0], "fsdp", scatter_dimension=0, tiled=True).astype(F32)
        else:
            moved = [shift(outs[k], k) for k in range(1, n)]
            value = after("sums", outs[0], *gate) if gate else outs[0]
            for part in moved:
                value = value + part.astype(F32)
        return value

    waiting = []

    def tick(name, *values):
        if on(name):
            waiting.extend(values)

    def take():
        values = tuple(waiting) if direct else ()
        waiting.clear()
        return values

    def after(name, value, *others):
        if not direct or not others or not on(name):
            return value
        value, *others = lax.optimization_barrier((value, *others))
        waiting.extend(others)
        return value

    def run(body, ins, specs, outs, scratch, name, out_specs=None):
        results = call(
            body, [ids, *ins], [SM] + specs, outs, scratch, name, out_specs, take()
        )
        tick("chain", results[0])
        return results

    def make_rows():
        pad = ((0, rows - real), (0, 0))
        tok = jnp.pad(tokens[0], pad)
        tok_near = near(tok)
        positions = y * real + jnp.arange(real)
        keep = slot_mask.astype(F32)[0] * (positions < IMG_TOK).astype(F32)
        keep = keep[:, None]
        grads = jnp.pad((cotangent[0].astype(F32) * keep).astype(BF), pad)
        grads_near = near(grads)
        return tok, tok_near, keep, grads, grads_near

    sems = lambda c: pltpu.SemaphoreType.DMA((c,))
    few = hidden // wide
    shift_rows = fc1_bias.reshape(few, wide // n)
    quarter = part_hidden // 4
    own_rows = wide // n

    def both_cores(v):
        return [v, core(v)]

    if direct:
        q = lambda ids: ids[1] * 4 + ids[0]
        blocks = [(w_qkv, (own_rows, LANES), lambda ids, k=k: (0, k * 8 + q(ids))) for k in range(3)]
        blocks += [(w_out, (own_rows, wide // 4), lambda ids: (0, ids[0]))]
        blocks += [(v, v.shape, lambda ids: (0, 0)) for v in (ln_gains, biases, shift_rows)]
        across_lanes = OUT_LANE + wide // 4
        (qkv_piece,) = cast(
            cast_qkv_kernel,
            ids,
            blocks,
            [shape((own_rows + 16, across_lanes), BF)],
            [pltpu.VMEM((16, across_lanes), F32)],
            "cast_qkv",
            take(),
        )
        tick("c_cast", qkv_piece)
        qkv_own = across(qkv_piece)
        tok, tok_near, keep, grads, grads_near = make_rows()
        blocks = [(w_fc1, (own_rows, LANES), lambda ids, k=k: (0, k * 8 + q(ids))) for k in range(n)]
        blocks += [(w_fc2, (h, wide), lambda ids: (q(ids), 0))]
        def over_z(piece, before=None, gate=()):
            parts = [piece]
            for k in range(1, n):
                ready = piece if before is None else after("zf", piece, before[k], *gate)
                parts.append(shift(ready, k))
            return parts

        qkv_parts = over_z(qkv_piece)
        tick("a1", qkv_parts[1])
        tick("a3", *qkv_parts[2:])
        (rest_piece,) = cast(
            functools.partial(cast_rest_kernel, n),
            ids,
            blocks,
            [shape((own_rows, 2 * quarter), BF)],
            [],
            "cast_rest",
            first=take(),
        )
        tick("c_rest", rest_piece)

        def over_x(parts, own, *gates):
            others = [own]
            for k in range(1, n):
                gate = gates[min(k, len(gates)) - 1] if gates else ()
                others.append(across(after("xf", parts[k], *gate)))
            return others

        def stack(body, parts, others, outs, name):
            values = run(
                functools.partial(body, n),
                parts + others,
                [VM] * (2 * n),
                outs,
                [],
                name,
            )
            flat = [v.reshape(-1, v.shape[2]) if v.ndim == 3 else v for v in values]
            return flat

        if joint:
            rest_all = lax.all_gather(rest_piece, ("x", "fsdp"), axis=0, tiled=True)
        else:
            rest_own = across(rest_piece)
            rest_parts = over_z(rest_piece, qkv_parts)
        tick("tok", tok_near)
        qkv_stack, vec = stack(
            stack_kernel,
            qkv_parts,
            over_x(qkv_parts, qkv_own),
            [shape((2 * n, own_rows, across_lanes), BF), shape((16, wide), F32)],
            "stack_qkv",
        )
        all_qkv = both_cores(qkv_stack)
    else:
        cut = lambda v, start, size, axis: lax.dynamic_slice_in_dim(v, start, size, axis).astype(BF)
        qkv_piece = jnp.concatenate(
            [cut(w_qkv, k * wide + y * half + r * LANES, LANES, 1) for k in range(3)]
            + [cut(w_out, r * (wide // 4), wide // 4, 1)],
            axis=1,
        )
        grid = w_fc1.reshape(w_fc1.shape[0], n, 8, h)
        one_piece = cut(grid, y * 4 + r, 1, 2).reshape(w_fc1.shape[0], n * h)
        two_piece = cut(w_fc2, (y * 4 + r) * h, h, 0)

        def whole(v):
            v = lax.all_gather(v, "fsdp", axis=0, tiled=True)
            return both_cores(jnp.concatenate([v, across(v)], axis=0))

        all_qkv, all_one, all_two = map(whole, (qkv_piece, one_piece, two_piece))
        tok, tok_near, keep, grads, grads_near = make_rows()
        small = jnp.concatenate([ln_gains, biases, shift_rows], axis=0).astype(BF)
        vec = lax.all_gather(small, "fsdp", axis=0).astype(F32).transpose(1, 0, 2)
        vec = jnp.pad(vec.reshape(-1, wide), ((0, 4), (0, 0)))

    two = 2 * rows
    tick("gnear", grads_near)
    normed, queries, keys, values = run(
        qkv_kernel,
        [tok, tok_near, vec, *all_qkv],
        [VM] * 3 + [ANY] * 2,
        [shape((two, wide), BF)] + [shape((two, half), BF)] * 3,
        [pltpu.VMEM((wide, 3 * half), BF), sems(4)],
        "qkv",
    )
    hidden_shift = vec[8:12].reshape(few, n, wide // n).transpose(1, 0, 2).reshape(n, 2, 4, h)
    hidden_shift = lax.dynamic_index_in_dim(hidden_shift, y, axis=1, keepdims=False)
    hidden_shift = hidden_shift.transpose(1, 0, 2).reshape(1, part_hidden)
    normed_far = core(normed)
    saved = (queries, keys, values)
    mixed_own, mixed_send, totals = attend(ids, *saved, rows, real, take())
    mixed_parts = (mixed_own, mixed_send)
    tick("chain", mixed_own)
    mixed_recv = near(mixed_send)
    grads_far, grads_near_far = core(grads), core(grads_near)
    mixed, middle, normed_two = run(
        project_kernel,
        [tok, mixed_own, mixed_recv, vec, *all_qkv],
        [VM] * 4 + [ANY] * 2,
        [shape((rows, wide), BF), shape((rows, wide), F32), shape((rows, wide), BF)],
        [pltpu.VMEM((wide, wide), BF), sems(4)],
        "project",
    )
    normed_two_near = near(normed_two)
    mixed_far, normed_two_far = core(mixed), core(normed_two)
    tick("n2", normed_two_near)
    tick("fars", normed_far, mixed_far, grads_far, grads_near_far, normed_two_far)
    if direct:
        if joint:
            all_one, all_two = both_cores(after("cf", rest_all, normed_two)), []
        else:
            rest_others = over_x(rest_parts, rest_own, (mixed_own,))
            one_stack, two_stack = stack(
                stack_rest_kernel,
                rest_parts,
                rest_others,
                [shape((2 * n, own_rows, quarter), BF), shape((2 * n, h, wide), BF)],
                "stack_rest",
            )
            all_one, all_two = both_cores(one_stack), both_cores(two_stack)
    normed_two_near_far = core(normed_two_near)
    tick("n2f", normed_two_near_far)
    act_near, act_far, gtwo_own, gtwo_send, result_own, result_send, hidden_sums = run(
        functools.partial(mlp_kernel, n, joint),
        [normed_two, normed_two_near, grads, grads_near, hidden_shift, *all_one, *all_two],
        [VM] * 5 + [ANY] * (len(all_one) + len(all_two)),
        [
            shape((two, 4 * quarter), BF),
            shape((two, 4 * quarter), BF),
            shape((rows, wide), F32),
            shape((rows, wide), BF),
            shape((rows, wide), F32),
            shape((rows, wide), BF),
            shape((1, part_hidden), F32),
        ],
        [
            pltpu.VMEM((wide, part_hidden), BF),
            pltpu.VMEM((part_hidden, wide), BF),
            pltpu.VMEM((two, wide), BF),
            pltpu.VMEM((two, wide), BF),
            pltpu.VMEM((two, wide), F32),
            pltpu.VMEM((two, wide), F32),
            pltpu.VMEM((8, two, quarter), BF),
            sems(8),
            sems(8),
        ],
        "mlp",
        [ANY] * 2 + [VM] * 5,
    )
    gtwo_recv = near(gtwo_send)
    act_other = core(act_far)

    def spread(part):
        return [part, near(part), across(part), diagonal(part)]

    def land(parts, dims, kind):
        parts = parts + [core(v) for v in parts]
        if direct:
            value = place(ids, parts, dims, kind, take())
            tick("places", value)
            return value
        order = [flip(y, dy) * 4 + flip(r, d + j) for j in range(2) for dy, d in PEERS]
        stack = jnp.zeros((8,) + parts[0].shape, F32)
        for index, v in zip(order, parts):
            stack = lax.dynamic_update_slice_in_dim(stack, v.astype(F32)[None], index, 0)
        if kind == "rows":
            return stack.reshape(dims)
        groups = dims[1] // (8 * (h if kind == "hidden" else LANES))
        stack = stack.reshape(8, dims[0], groups, -1)
        return stack.transpose(1, 2, 0, 3).reshape(dims)

    blocks = n if direct else 1

    def grad(left, right, name, extra=()):
        values = weight_grad(
            ids, left, right, name, extra, blocks if extra else 1, first=take()
        )
        tick("chain", values[0])
        return values if extra else values[0]

    all_grads = [(a, None) for a in (grads, grads_near, grads_far, grads_near_far)]
    one_left = [
        (a, None) for a in (normed_two, normed_two_near, normed_two_far, normed_two_near_far)
    ]

    def unit(slot):
        return [(act_near, (slot * quarter, quarter)), (act_other, (slot * quarter, quarter))]

    two_left = [(v, (2 * quarter, 2 * quarter)) for v in (act_near, act_other)]
    two_sums = weight_grad(
        ids,
        two_left,
        all_grads,
        "grad_fc2",
        blocks=1 if whole_two else blocks,
        slots=2 if direct else 1,
        first=take(),
    )
    tick("chain", two_sums[0])
    if not direct:
        two_sums = [
            v.reshape(2, n, h, wide).transpose(1, 0, 2, 3).reshape(-1, wide) for v in two_sums
        ]
    grad_middle, branch, gmix_own, gmix_send, sums_two = run(
        middle_back_kernel,
        [gtwo_own, gtwo_recv, middle, grads, vec, *all_qkv],
        [VM] * 5 + [ANY] * 2,
        [
            shape((rows, wide), F32),
            shape((rows, wide), BF),
            shape((rows, half), BF),
            shape((rows, half), BF),
            shape((4, wide), F32),
        ],
        [pltpu.VMEM((wide, wide), BF), pltpu.VMEM((rows, wide), BF), sems(4)],
        "middle_back",
    )
    gmix_recv = near(gmix_send)
    branch_far = core(branch)
    one_recv = across(grad(one_left, unit(1), "grad_fc1_send"))
    out_keep, *out_sends = run(
        out_grad_kernel,
        [mixed, mixed_far, branch, branch_far],
        [ANY] * 4,
        [shape((wide, LANES), F32)] + [shape((wide, LANES), BF)] * 3,
        [pltpu.VMEM((two, wide), BF), pltpu.VMEM((two, 4 * LANES), BF), sems(10)],
        "grad_out",
    )
    gj_near, gj_far, joined_sums = attend_back(
        ids, saved, mixed_parts, (gmix_own, gmix_recv), totals, rows, real, take()
    )
    tick("chain", gj_near)
    gj_other = core(gj_far)
    result_recv = near(result_send)
    total = middle[:real] + (
        result_own[:real] + result_recv[:real].astype(F32) + vec[7:8, :]
    )
    output = (total * keep).astype(BF)[None]
    out_recvs = [near(out_sends[0]), across(out_sends[1]), diagonal(out_sends[2])]
    tick("res", result_recv)
    one_sums = grad(one_left, unit(0), "grad_fc1_keep", [one_recv])
    qkv_left = [(normed, None), (normed_far, None)]
    qkv_send = grad(qkv_left, [(gj_near, 1), (gj_other, 1)], "grad_qkv_send")
    qkv_recv = across(qkv_send)
    gone_own, gone_send = run(
        qkv_back_kernel,
        [gj_near, gj_far, *all_qkv],
        [ANY] * 4,
        [shape((rows, wide), F32), shape((rows, wide), BF)],
        [
            pltpu.VMEM((wide, 3 * half), BF),
            pltpu.VMEM((two, 3 * half), BF),
            sems(8),
        ],
        "qkv_back",
    )
    gone_recv = near(gone_send)
    if whole_two:
        two_part = lax.psum_scatter(two_sums[0], ("x", "fsdp"), scatter_dimension=0, tiled=True)
        two_all = lax.all_gather(two_part, ("x", "core", "seq"), axis=0)
        two_all = two_all.reshape((2, 2, 2) + two_part.shape).transpose(2, 0, 1, 3, 4)
        grad_fc2 = two_all.reshape(w_fc2.shape).astype(F32)
    two_total = two_cross = None if whole_two else scatter_rows(two_sums, *([gone_own] if on("s2") else []))
    if not whole_two:
        two_cross = across(two_total[h:].astype(BF))
    kinds = [F32] + [BF] * (blocks - 1) if blocks > 1 else [BF]
    out_sums = run(
        combine_kernel,
        [out_keep, *out_recvs],
        [VM] * 4,
        [shape((wide // blocks, LANES), kind) for kind in kinds],
        [],
        "combine",
    )
    out_part = scatter_rows(out_sums).astype(BF)
    qkv_sums = grad(qkv_left, [(gj_near, 0), (gj_other, 0)], "grad_qkv_keep", [qkv_recv])
    if not whole_two:
        tick("x2", two_cross)
    else:
        tick("rs2", two_part)
    tick("zo", out_part)
    grad_tokens, sums_one = run(
        tokens_back_kernel,
        [gone_own, gone_recv, tok, grad_middle, vec],
        [VM] * 5,
        [shape((real, wide), BF), shape((2, wide), F32)],
        [],
        "tokens_back",
    )
    grad_tokens = grad_tokens[None]
    qkv_part = scatter_rows(qkv_sums).astype(BF)
    if not whole_two:
        two_parts = spread((two_total[:h] + two_cross.astype(F32)).astype(BF))
    one_part = scatter_rows(one_sums, *([sums_one] if on("s1") else [])).astype(BF)
    out_parts = spread(out_part)
    tick("ago", *out_parts)
    if not whole_two:
        tick("ag2", *two_parts)
    tick("z1", one_part)
    if direct:
        parts = run(
            small_kernel,
            [sums_one, sums_two, joined_sums, hidden_sums],
            [VM] * 4,
            [shape((16, wide // n), F32)] * n,
            [pltpu.VMEM((n, 16, wide // n), F32)],
            "small",
        )
        block = parts[0]
        for k in range(1, n):
            block = block + shift(parts[k], k)
    else:
        wanted = jnp.bitwise_xor(jnp.arange(4), r)
        slots = ((wanted & 1) << 1) | (wanted >> 1)
        chosen = (slots[:, None] == jnp.arange(4)[None, :]).astype(F32)
        joined_sums = jnp.sum(chosen[:, :, None] * joined_sums[None, :, 0, :], axis=1)
        here = (jnp.arange(2) == y).astype(F32)

        def spread_half(row):
            return (here[:, None] * row.reshape(1, half)).reshape(1, wide)

        query_sums = spread_half(joined_sums[:, :LANES])
        value_sums = spread_half(joined_sums[:, 2 * LANES :])
        hidden_sums = hidden_sums.reshape(4, n, h).transpose(1, 0, 2).reshape(n, 1, 4 * h)
        hidden_sums = (hidden_sums * here[None, :, None]).reshape(n, hidden // wide, wide // n)
        rows_of = jnp.concatenate(
            [
                sums_one[0:1],
                sums_two[0:1],
                sums_one[1:2],
                query_sums,
                value_sums,
                sums_two[2:3],
                sums_two[1:2],
                sums_two[3:4],
            ],
            axis=0,
        )
        block = jnp.concatenate(
            [rows_of.reshape(8, n, wide // n).transpose(1, 0, 2), hidden_sums], axis=1
        )
        block = lax.psum_scatter(block, "fsdp", scatter_dimension=0)
    block = block + near(block) + across(block) + diagonal(block)
    block = block + core(block)

    tick("zq", qkv_part)
    qkv_parts = spread(qkv_part)
    one_parts = spread(one_part)
    tick("ag1", *one_parts)
    if not whole_two:
        grad_fc2 = land(two_parts, w_fc2.shape, "rows")
    grad_fc1 = land(one_parts, w_fc1.shape, "hidden")
    tick("agq", *qkv_parts)
    grad_out = land(out_parts, w_out.shape, "columns")
    grad_qkv = land(qkv_parts, w_qkv.shape, "columns")
    return (
        output,
        grad_tokens,
        grad_qkv,
        grad_out,
        grad_fc1,
        grad_fc2,
        block[:2],
        block[2:8],
        block[8 : 8 + few].reshape(-1),
    )


def solution(mesh):
    reps, n, seqs = (mesh.shape[axis] for axis in ("rep", "fsdp", "seq"))
    assert reps == 4 and seqs == 2
    fine = Mesh(mesh.devices.reshape(reps // 2, 2, n, seqs), ("x", "core", "fsdp", "seq"))
    slots = P(("x", "core", "fsdp"), "seq", None)
    first, second = P("fsdp", None), P(None, "fsdp")
    return jax.shard_map(
        functools.partial(on_device, n),
        mesh=fine,
        in_specs=(
            slots,
            P(("x", "core", "fsdp")),
            slots,
            first,
            first,
            first,
            first,
            second,
            second,
            P("fsdp"),
        ),
        out_specs=(slots, slots, first, first, first, first, second, second, P("fsdp")),
        check_vma=False,
    )
```

time: 388 us -> 375 us (0.966)
  Pallas kernels: 153 us -> 136 us
  starting transfers between devices: 87.4 us -> 72.1 us
  between operations: 2.24 us -> 15.3 us
  local copies, waits for them, and re-layouts: 17.5 us -> 22.8 us
    ppermute x24 -> x15, waiting for transfers between devices: 58 us -> 30.6 us  [shift(): return lax.ppermute(v, 'fsdp', [(i, (i + k) % n) for i in range(n)])]
    pallas_call x27 -> x22, Pallas kernels: 153 us -> 136 us  [the longest x15 88.9 us: call(): pl.pallas_call(skipping(body, len(ins), len(first)), out_shape=outs, in_s...]
    ppermute x14 -> x13, waiting for transfers between devices: 16.8 us -> 33.1 us  [near(): return lax.ppermute(v, 'seq', swap)]
    ppermute x21 -> x11, waiting for transfers between devices: 39.9 us -> 24 us  [across(): return lax.ppermute(v, 'x', swap)]
    reduce_scatter x0 -> x1, waiting for transfers between devices: none -> 15.4 us  [on_device(): lax.psum_scatter(two_sums[0], ('x', 'fsdp'), scatter_dimension=0, tiled=T...]
    ppermute x24 -> x15, starting transfers between devices: 42.8 us -> 32.5 us  [shift(): return lax.ppermute(v, 'fsdp', [(i, (i + k) % n) for i in range(n)])]
    ppermute x0 -> x5, starting transfers between devices: none -> 9.31 us  [diagonal(): return lax.ppermute(v, ('x', 'seq'), [(i, i ^ 3) for i in range(4)])]
    ppermute x21 -> x11, starting transfers between devices: 21.3 us -> 12.2 us  [across(): return lax.ppermute(v, 'x', swap)]
  transfers between devices with their start and end apart: 78 -> 71, of which waited for: 25 -> 23; matrix products, arithmetic and copies ran while one was open for 3% -> 2% of each run, Pallas kernels for 33% -> 31%
where the time goes in v3:
time: 375 us; the launch traced here: 373 us
  Pallas kernels  136 us (36%)
  waiting for transfers between devices  120 us (32%)
  starting transfers between devices  72.1 us (19%)
  local copies, waits for them, and re-layouts  22.8 us (6%)
  between operations  15.3 us (4%)
  other arithmetic  7.11 us (2%)
    pallas_call x15, Pallas kernels, call(): pl.pallas_call(skipping(body, len(ins), len(first)), out_shape=outs, in_s...  88.9 us
    pallas_call x7, Pallas kernels, grid_call(): pl.pallas_call(skipping(body, len(ins) + 1, len(first)), grid_spec=pltpu....  47 us
    ppermute x13, waiting for transfers between devices, near(): return lax.ppermute(v, 'seq', swap)  33.1 us
    ppermute x15, starting transfers between devices, shift(): return lax.ppermute(v, 'fsdp', [(i, (i + k) % n) for i in range(n)])  32.5 us
    ppermute x15, waiting for transfers between devices, shift(): return lax.ppermute(v, 'fsdp', [(i, (i + k) % n) for i in range(n)])  30.6 us
    ppermute x11, waiting for transfers between devices, across(): return lax.ppermute(v, 'x', swap)  24 us
    unnamed x142, local copies, waits for them, and re-layouts  15.8 us
    reduce_scatter x1, waiting for transfers between devices, on_device(): lax.psum_scatter(two_sums[0], ('x', 'fsdp'), scatter_dimension=0, tiled=T...  15.4 us
  transfers between devices with their start and end apart: 71, of which 23 were waited for; matrix products, arithmetic and copies ran while one was open for 2% of the time, Pallas kernels for 31%

profile of v3, /device:TPU:0, one launch (start us, length us, event | category | flops | bytes accessed | tf_op | source)
XLA Modules:
  0.0 373.0 jit_solution(14424123742090759380)
XLA Ops:
  20.5 5.8 %collective-permute-done.1.refs_7_.refs_2_ = bf16[272,640]{1,0:T(8,128)(2,1)S(1)} collective-permute-done((bf16[272,640]{1,0:T(8,128)(2,1)}, bf16[272,640]{1,0:T(8,128)(2,1)S(1)}, u32[]{:S(2)}, u32[]{:S(2)}) %collective-permute-start.1) | collective-permute-done | bytes 348192 | tf_op jit(solution)/shard_map/ppermute | solution.py:749
  32.0 8.3 %collective-permute-done.2.refs_3_ = bf16[272,640]{1,0:T(8,128)(2,1)S(1)} collective-permute-done((bf16[272,640]{1,0:T(8,128)(2,1)}, bf16[272,640]{1,0:T(8,128)(2,1)S(1)}, u32[]{:S(2)}, u32[]{:S(2)}) %collective-permute-start.2) | collective-permute-done | bytes 348192 | tf_op jit(solution)/shard_map/ppermute | solution.py:749
  42.4 6.1 %collective-permute-done.5.refs_6_ = bf16[272,640]{1,0:T(8,128)(2,1)S(1)} collective-permute-done((bf16[272,640]{1,0:T(8,128)(2,1)}, bf16[272,640]{1,0:T(8,128)(2,1)S(1)}, u32[]{:S(2)}, u32[]{:S(2)}) %collective-permute-start.5) | collective-permute-done | bytes 348192 | tf_op jit(solution)/shard_map/ppermute | solution.py:740
  48.5 9.1 %collective-permute-done.6.refs_7_ = bf16[272,640]{1,0:T(8,128)(2,1)S(1)} collective-permute-done((bf16[272,640]{1,0:T(8,128)(2,1)S(1)}, bf16[272,640]{1,0:T(8,128)(2,1)S(1)}, u32[]{:S(2)}, u32[]{:S(2)}) %collective-permute-start.6) | collective-permute-done | bytes 348192 | tf_op jit(solution)/shard_map/ppermute | solution.py:740
  57.6 8.8 %collective-permute-done.7.refs_8_ = bf16[272,640]{1,0:T(8,128)(2,1)S(1)} collective-permute-done((bf16[272,640]{1,0:T(8,128)(2,1)S(1)}, bf16[272,640]{1,0:T(8,128)(2,1)S(1)}, u32[]{:S(2)}, u32[]{:S(2)}) %collective-permute-start.7) | collective-permute-done | bytes 348192 | tf_op jit(solution)/shard_map/ppermute | solution.py:740
  72.9 15.3 %collective-permute-done.9.refs_7_.refs_4_ = bf16[304,1024]{1,0:T(8,128)(2,1)} collective-permute-done((bf16[304,1024]{1,0:T(8,128)(2,1)S(1)}, bf16[304,1024]{1,0:T(8,128)(2,1)}, u32[]{:S(2)}, u32[]{:S(2)}) %collective-permute-start.9) | collective-permute-done | bytes 622624 | tf_op jit(solution)/shard_map/ppermute | solution.py:743
  88.2 7.7 %qkv.1 = (bf16[608,1024]{1,0:T(8,128)(2,1)}, bf16[608,512]{1,0:T(8,128)(2,1)}, bf16[608,512]{1,0:T(8,128)(2,1)}, bf16[608,512]{1,0:T(8,128)(2,1)}) custom-call(s32[3]{0:T(128)} %pad_add_fusion.ids.refs_0_, bf16[304,1024]{1,0:T(8,128)(2,1)} %copy-done.2, bf16[304,1024]{1,0:T(8,128)(2,1)} %copy-done.22, f32[16,1024]{1,0:T(8,128)} %get-tuple-element.64.refs_3_.refs_4_.refs_5_, ...), custom_call_target="tpu_custom_call" | custom-call | flops 9200000000 | bytes 262144 | tf_op jit(solution)/shard_map/qkv/pallas_call | solution.py:104
  95.9 11.3 %attend.1 = (bf16[304,512]{1,0:T(8,128)(2,1)}, bf16[304,512]{1,0:T(8,128)(2,1)}, f32[4,4,304]{2,1,0:T(4,128)}) custom-call(s32[3]{0:T(128)} %pad_add_fusion.ids.refs_0_, bf16[608,512]{1,0:T(8,128)(2,1)} %get-tuple-element.66.refs_1_, bf16[608,512]{1,0:T(8,128)(2,1)} %get-tuple-element.67.refs_2_, bf16[608,512]{1,0:T(8,128)(2,1)} %get-tuple-element.68.refs_3_, ...), custom_call_target="tpu_custom_call" | custom-call | flops 12995000320 | bytes 262144 | tf_op jit(solution)/shard_map/attend/pallas_call | solution.py:117
  108.5 7.9 %collective-permute-done.10.refs_3_ = bf16[304,512]{1,0:T(8,128)(2,1)S(1)} collective-permute-done((bf16[304,512]{1,0:T(8,128)(2,1)}, bf16[304,512]{1,0:T(8,128)(2,1)S(1)}, u32[]{:S(2)}, u32[]{:S(2)}) %collective-permute-start.10) | collective-permute-done | bytes 311328 | tf_op jit(solution)/shard_map/ppermute | solution.py:743
  124.3 5.6 %collective-permute-done.15.refs_11_.refs_5_ = bf16[304,1024]{1,0:T(8,128)(2,1)S(1)} collective-permute-done((bf16[304,1024]{1,0:T(8,128)(2,1)S(1)}, bf16[304,1024]{1,0:T(8,128)(2,1)S(1)}, u32[]{:S(2)}, u32[]{:S(2)}) %collective-permute-start.15) | collective-permute-done | bytes 622624 | tf_op jit(solution)/shard_map/ppermute | solution.py:737
  133.5 6.1 %collective-permute-done.11.refs_2_ = bf16[304,1024]{1,0:T(8,128)(2,1)} collective-permute-done((bf16[304,1024]{1,0:T(8,128)(2,1)}, bf16[304,1024]{1,0:T(8,128)(2,1)}, u32[]{:S(2)}, u32[]{:S(2)}) %collective-permute-start.11) | collective-permute-done | bytes 622624 | tf_op jit(solution)/shard_map/ppermute | solution.py:743
  142.1 17.9 %mlp.1 = (bf16[608,2048]{1,0:T(8,128)(2,1)}, bf16[608,2048]{1,0:T(8,128)(2,1)}, f32[304,1024]{1,0:T(8,128)}, bf16[304,1024]{1,0:T(8,128)(2,1)}, f32[304,1024]{1,...) custom-call(s32[3]{0:T(128)} %pad_add_fusion.ids.refs_0_, ...), custom_call_target="tpu_custom_call" | custom-call | flops 21390000128 | bytes 262144 | tf_op jit(solution)/shard_map/mlp/pallas_call | solution.py:104
  166.6 7.3 %grad_fc2.1.refs_8_ = bf16[1024,1024]{1,0:T(8,128)(2,1)} custom-call(s32[3]{0:T(128)} %pad_add_fusion.ids.refs_0_, bf16[608,2048]{1,0:T(8,128)(2,1)} %get-tuple-element.81.refs_1_.refs_7_.refs_5_, bf16[608,2048]{1,0:T(8,128)(2,1)} %copy-done.15, bf16[304,1024]{1,0:T(8,128)(2,1)} %copy-done.3, bf16[304,1024]{1,0:T(8,128)(2,1)} %collective-permute-done.9.refs_7_.refs_4_, ...), custom_call_target="tpu_custom_call" | custom-call | flops 9200000000 | bytes 262144 | tf_op jit(solution)/shard_map/grad_fc2/pallas_call | solution.py:104
  178.5 5.4 %middle_back.1 = (f32[304,1024]{1,0:T(8,128)}, bf16[304,1024]{1,0:T(8,128)(2,1)}, bf16[304,512]{1,0:T(8,128)(2,1)}, bf16[304,512]{1,0:T(8,128)(2,1)}, f32[4,1024]{1,0:T(4,128)}) custom-call(s32[3]{0:T(128)} %pad_add_fusion.ids.refs_0_, f32[304,1024]{1,0:T(8,128)} %get-tuple-element.79.refs_1_, bf16[304,1024]{1,0:T(8,128)(2,1)} %copy-done.25, ...), custom_call_target="tpu_custom_call" | custom-call | flops 9200000000 | bytes 262144 | tf_op jit(solution)/shard_map/middle_back/pallas_call | solution.py:104
  185.3 6.0 %grad_fc1_send.1.refs_5_ = bf16[1024,512]{1,0:T(8,128)(2,1)} custom-call(s32[3]{0:T(128)} %pad_add_fusion.ids.refs_0_, bf16[304,1024]{1,0:T(8,128)(2,1)} %get-tuple-element.76.refs_1_.refs_14_, bf16[304,1024]{1,0:T(8,128)(2,1)} %collective-permute-done.11.refs_2_, bf16[304,1024]{1,0:T(8,128)(2,1)} %collective-permute-done.17.refs_13_.refs_3_, ...), custom_call_target="tpu_custom_call" | custom-call | flops 9200000000 | bytes 262144 | tf_op jit(solution)/shard_map/grad_fc1_send/pallas_call | solution.py:104
  199.3 16.7 %attend_back.1 = (bf16[2,608,384]{2,1,0:T(8,128)(2,1)}, bf16[2,608,384]{2,1,0:T(8,128)(2,1)}, f32[4,1,384]{2,1,0:T(1,128)}) custom-call(s32[3]{0:T(128)} %pad_add_fusion.ids.refs_0_, bf16[608,512]{1,0:T(8,128)(2,1)} %get-tuple-element.66.refs_1_, bf16[608,512]{1,0:T(8,128)(2,1)} %get-tuple-element.67.refs_2_, bf16[608,512]{1,0:T(8,128)(2,1)} %get-tuple-element.68.refs_3_, ...), custom_call_target="tpu_custom_call" | custom-call | flops 19434999808 | bytes 262144 | tf_op jit(solution)/shard_map/attend_back/pallas_call | solution.py:117
  221.5 5.6 %grad_fc1_keep.1 = (f32[256,512]{1,0:T(8,128)}, bf16[256,512]{1,0:T(8,128)(2,1)}, bf16[256,512]{1,0:T(8,128)(2,1)}, bf16[256,512]{1,0:T(8,128)(2,1)}) custom-call(s32[3]{0:T(128)} %pad_add_fusion.ids.refs_0_, bf16[304,1024]{1,0:T(8,128)(2,1)} %get-tuple-element.76.refs_1_.refs_14_, bf16[304,1024]{1,0:T(8,128)(2,1)} %collective-permute-done.11.refs_2_, ...), custom_call_target="tpu_custom_call" | custom-call | flops 9200000000 | bytes 262144 | tf_op jit(solution)/shard_map/grad_fc1_keep/pallas_call | solution.py:104
  228.1 5.7 %grad_qkv_send.1.refs_5_ = bf16[1024,384]{1,0:T(8,128)(2,1)} custom-call(s32[3]{0:T(128)} %pad_add_fusion.ids.refs_0_, bf16[608,1024]{1,0:T(8,128)(2,1)} %get-tuple-element.69.refs_4_.refs_1_, bf16[608,1024]{1,0:T(8,128)(2,1)} %copy-done.17, bf16[2,608,384]{2,1,0:T(8,128)(2,1)} %get-tuple-element.89.refs_8_.refs_3_.refs_1_, bf16[2,608,384]{2,1,0:T(8,128)(2,1)} %copy-done.19, ...), custom_call_target="tpu_custom_call" | custom-call | flops 9200000000 | bytes 262144 | tf_op jit(solution)/shard_map/grad_qkv_send/pallas_call | solution.py:104
  234.5 7.0 %qkv_back.1 = (f32[304,1024]{1,0:T(8,128)}, bf16[304,1024]{1,0:T(8,128)(2,1)}) custom-call(s32[3]{0:T(128)} %pad_add_fusion.ids.refs_0_, bf16[2,608,384]{2,1,0:T(8,128)(2,1)} %get-tuple-element.89.refs_8_.refs_3_.refs_1_, bf16[2,608,384]{2,1,0:T(8,128)(2,1)} %get-tuple-element.90.refs_2_, bf16[2048,640]{1,0:T(8,128)(2,1)} %bitcast.40, ...), custom_call_target="tpu_custom_call" | custom-call | flops 9200000000 | bytes 262144 | tf_op jit(solution)/shard_map/qkv_back/pallas_call | solution.py:104
  244.6 9.3 %collective-permute-start.31 = (bf16[256,128]{1,0:T(8,128)(2,1)}, bf16[256,128]{1,0:T(8,128)(2,1)S(1)}, u32[]{:S(2)}, u32[]{:S(2)}) collective-permute-start(bf16[256,128]{1,0:T(8,128)(2,1)} %get-tuple-element.99), channel_id=1, source_target_pairs={{0,2},{2,4},{4,6},{6,0},{1,3},{3,5},{5,7},{7,1},{8,10},{10,12},{12... | collective-permute-start | bytes 196616 | tf_op jit(solution)/shard_map/ppermute | solution.py:749
  260.5 9.6 %collective-permute-done.32 = bf16[256,128]{1,0:T(8,128)(2,1)S(1)} collective-permute-done((bf16[256,128]{1,0:T(8,128)(2,1)}, bf16[256,128]{1,0:T(8,128)(2,1)S(1)}, u32[]{:S(2)}, u32[]{:S(2)}) %collective-permute-start.32) | collective-permute-done | bytes 65568 | tf_op jit(solution)/shard_map/ppermute | solution.py:749
  273.5 5.4 %grad_qkv_keep.1 = (f32[256,384]{1,0:T(8,128)}, bf16[256,384]{1,0:T(8,128)(2,1)}, bf16[256,384]{1,0:T(8,128)(2,1)}, bf16[256,384]{1,0:T(8,128)(2,1)}) custom-call(s32[3]{0:T(128)} %pad_add_fusion.ids.refs_0_, bf16[608,1024]{1,0:T(8,128)(2,1)} %get-tuple-element.69.refs_4_.refs_1_, bf16[608,1024]{1,0:T(8,128)(2,1)} %copy-done.17, ...), custom_call_target="tpu_custom_call" | custom-call | flops 9200000000 | bytes 262144 | tf_op jit(solution)/shard_map/grad_qkv_keep/pallas_call | solution.py:104
  278.9 15.4 %reduce-scatter.2.cloned.1.call-done.refs_7_ = bf16[128,1024]{1,0:T(8,128)(2,1)} async-done(((bf16[1024,1024]{1,0:T(8,128)(2,1)}), bf16[128,1024]{1,0:T(8,128)(2,1)}) %reduce-scatter.2.cloned.1.call-update) | async-done | bytes 262160 | tf_op jit(solution)/shard_map/reduce_scatter | solution.py:1084
  342.1 5.0 %place.3.refs_9_ = f32[256,4096]{1,0:T(8,128)} custom-call(s32[3]{0:T(128)} %pad_add_fusion.ids.refs_0_, bf16[256,512]{1,0:T(8,128)(2,1)} %add_convert_fusion.refs_7_.refs_1_.refs_11_, bf16[256,512]{1,0:T(8,128)(2,1)} %copy-done.40, bf16[256,512]{1,0:T(8,128)(2,1)} %copy-done.41, bf16[256,512]{1,0:T(8,128)(2,1)} %copy-done.42, bf16[256,512]{1,0:T(8,128)(2,1)} %copy-done.46, ...), custom_call_target="tpu_custom_call" | custom-call | flops 2760000000 | bytes 262144 | tf_op jit(solution)/shard_map/place/pallas_call | solution.py:117
  (306 shorter events, 149.4 us)
Async XLA Ops:
  7.2 115.0 %all-gather.4.cloned.1.call-start = ((), (), s32[]{:S(2)}) async-start(), calls=%async_computation.1 | async-start | bytes 4718592 | tf_op jit(solution)/shard_map/all_gather | solution.py:867
  14.9 25.4 %collective-permute-start.2 = (bf16[272,640]{1,0:T(8,128)(2,1)}, bf16[272,640]{1,0:T(8,128)(2,1)S(1)}, u32[]{:S(2)}, u32[]{:S(2)}) collective-permute-start(bf16[272,640]{1,0:T(8,128)(2,1)} %cast_qkv.1.refs_6_.refs_1_), channel_id=1, source_target_pairs={{0,4},{2,6},{4,0},{6,2},{1,5},{3,7},{5,1},{7,3},{8,12},{10,14},{12... | collective-permute-start | bytes 1044488 | tf_op jit(solution)/shard_map/ppermute | solution.py:749
  17.4 24.3 %collective-permute-start.3 = (bf16[272,640]{1,0:T(8,128)(2,1)}, bf16[272,640]{1,0:T(8,128)(2,1)S(1)}, u32[]{:S(2)}, u32[]{:S(2)}) collective-permute-start(bf16[272,640]{1,0:T(8,128)(2,1)} %cast_qkv.1.refs_6_.refs_1_), channel_id=1, source_target_pairs={{0,6},{2,0},{4,2},{6,4},{1,7},{3,1},{5,3},{7,5},{8,14},{10,8},{12,... | collective-permute-start | bytes 1044488 | tf_op jit(solution)/shard_map/ppermute | solution.py:749
  18.9 23.5 %collective-permute-start = (bf16[304,1024]{1,0:T(8,128)(2,1)S(1)}, bf16[304,1024]{1,0:T(8,128)(2,1)S(1)}, u32[]{:S(2)}, u32[]{:S(2)}) collective-permute-start(bf16[304,1024]{1,0:T(8,128)(2,1)S(1)} %pad.7.refs_1_.refs_3_), channel_id=1, source_target_pairs={{0,1},{1,0},{2,3},{3,2},{4,5},{5,4},{6,7},{7,6},{8,9},{9,8},{10,11... | collective-permute-start | bytes 1867784 | tf_op jit(solution)/shard_map/ppermute | solution.py:743
  29.8 264.4 %reduce-scatter.2.cloned.1.call-start = ((), (), s32[]{:S(2)}) async-start(), calls=%async_computation.2 | async-start | bytes 2359296 | tf_op jit(solution)/shard_map/reduce_scatter | solution.py:1084
  31.7 16.8 %collective-permute-start.5 = (bf16[272,640]{1,0:T(8,128)(2,1)}, bf16[272,640]{1,0:T(8,128)(2,1)S(1)}, u32[]{:S(2)}, u32[]{:S(2)}) collective-permute-start(bf16[272,640]{1,0:T(8,128)(2,1)} %copy-done.28), channel_id=1, source_target_pairs={{0,16},{16,0},{1,17},{17,1},{2,18},{18,2},{3,19},{19,3},{4,20},{20... | collective-permute-start | bytes 1044488 | tf_op jit(solution)/shard_map/ppermute | solution.py:740
  40.3 17.3 %collective-permute-start.6 = (bf16[272,640]{1,0:T(8,128)(2,1)S(1)}, bf16[272,640]{1,0:T(8,128)(2,1)S(1)}, u32[]{:S(2)}, u32[]{:S(2)}) collective-permute-start(bf16[272,640]{1,0:T(8,128)(2,1)S(1)} %collective-permute-done.2.refs_3_), channel_id=1, source_target_pairs={{0,16},{16,0},{1,17},{17,1},{2,18},{18,2},{3,19},{19,3},{4,20},{20... | collective-permute-start | bytes 1044488 | tf_op jit(solution)/shard_map/ppermute | solution.py:740
  41.8 24.6 %collective-permute-start.7 = (bf16[272,640]{1,0:T(8,128)(2,1)S(1)}, bf16[272,640]{1,0:T(8,128)(2,1)S(1)}, u32[]{:S(2)}, u32[]{:S(2)}) collective-permute-start(bf16[272,640]{1,0:T(8,128)(2,1)S(1)} %collective-permute-done.3.refs_4_), channel_id=1, source_target_pairs={{0,16},{16,0},{1,17},{17,1},{2,18},{18,2},{3,19},{19,3},{4,20},{20... | collective-permute-start | bytes 1044488 | tf_op jit(solution)/shard_map/ppermute | solution.py:740
  70.7 17.5 %collective-permute-start.8 = (bf16[2048,640]{1,0:T(8,128)(2,1)}, bf16[2048,640]{1,0:T(8,128)(2,1)}, u32[]{:S(2)}, u32[]{:S(2)}) collective-permute-start(bf16[2048,640]{1,0:T(8,128)(2,1)} %bitcast.36), channel_id=1, source_target_pairs={{0,8},{8,0},{1,9},{9,1},{2,10},{10,2},{3,11},{11,3},{4,12},{12,4},... | collective-permute-start | bytes 7864328 | tf_op jit(solution)/shard_map/ppermute | solution.py:737
  122.2 19.8 %collective-permute-start.12 = (bf16[2048,1024]{1,0:T(8,128)(2,1)}, bf16[2048,1024]{1,0:T(8,128)(2,1)}, u32[]{:S(2)}, u32[]{:S(2)}) collective-permute-start(bf16[2048,1024]{1,0:T(8,128)(2,1)} %all-gather.4.cloned.1.call-done.refs_6_), channel_id=1, source_target_pairs={{0,8},{8,0},{1,9},{9,1},{2,10},{10,2},{3,11},{11,3},{4,12},{12,4},... | collective-permute-start | bytes 12582920 | tf_op jit(solution)/shard_map/ppermute | solution.py:737
  122.9 16.7 %collective-permute-start.11 = (bf16[304,1024]{1,0:T(8,128)(2,1)}, bf16[304,1024]{1,0:T(8,128)(2,1)}, u32[]{:S(2)}, u32[]{:S(2)}) collective-permute-start(bf16[304,1024]{1,0:T(8,128)(2,1)} %get-tuple-element.76.refs_1_.refs_14_), channel_id=1, source_target_pairs={{0,1},{1,0},{2,3},{3,2},{4,5},{5,4},{6,7},{7,6},{8,9},{9,8},{10,11... | collective-permute-start | bytes 1867784 | tf_op jit(solution)/shard_map/ppermute | solution.py:743
  124.2 16.8 %collective-permute-start.13 = (bf16[608,1024]{1,0:T(8,128)(2,1)S(1)}, bf16[608,1024]{1,0:T(8,128)(2,1)S(1)}, u32[]{:S(2)}, u32[]{:S(2)}) collective-permute-start(bf16[608,1024]{1,0:T(8,128)(2,1)S(1)} %copy-done.16), channel_id=1, source_target_pairs={{0,8},{8,0},{1,9},{9,1},{2,10},{10,2},{3,11},{11,3},{4,12},{12,4},... | collective-permute-start | bytes 3735560 | tf_op jit(solution)/shard_map/ppermute | solution.py:737
  160.6 17.1 %collective-permute-start.20 = (bf16[304,1024]{1,0:T(8,128)(2,1)}, bf16[304,1024]{1,0:T(8,128)(2,1)S(1)}, u32[]{:S(2)}, u32[]{:S(2)}) collective-permute-start(bf16[304,1024]{1,0:T(8,128)(2,1)} %get-tuple-element.80), channel_id=1, source_target_pairs={{0,1},{1,0},{2,3},{3,2},{4,5},{5,4},{6,7},{7,6},{8,9},{9,8},{10,11... | collective-permute-start | bytes 1867784 | tf_op jit(solution)/shard_map/ppermute | solution.py:743
  161.8 56.4 %collective-permute-start.19 = (bf16[304,1024]{1,0:T(8,128)(2,1)}, bf16[304,1024]{1,0:T(8,128)(2,1)S(1)}, u32[]{:S(2)}, u32[]{:S(2)}) collective-permute-start(bf16[304,1024]{1,0:T(8,128)(2,1)} %get-tuple-element.78), channel_id=1, source_target_pairs={{0,1},{1,0},{2,3},{3,2},{4,5},{5,4},{6,7},{7,6},{8,9},{9,8},{10,11... | collective-permute-start | bytes 1867784 | tf_op jit(solution)/shard_map/ppermute | solution.py:743
  191.3 29.2 %collective-permute-start.25 = (bf16[1024,512]{1,0:T(8,128)(2,1)}, bf16[1024,512]{1,0:T(8,128)(2,1)S(1)}, u32[]{:S(2)}, u32[]{:S(2)}) collective-permute-start(bf16[1024,512]{1,0:T(8,128)(2,1)} %grad_fc1_send.1.refs_5_), channel_id=1, source_target_pairs={{0,16},{16,0},{1,17},{17,1},{2,18},{18,2},{3,19},{19,3},{4,20},{20... | collective-permute-start | bytes 3145736 | tf_op jit(solution)/shard_map/ppermute | solution.py:740
  216.1 145.9 %all-gather.6.cloned.1.call-start = ((), (), s32[]{:S(2)}) async-start(), calls=%async_computation.3 | async-start | bytes 2359296 | tf_op jit(solution)/shard_map/all_gather | solution.py:1085
  217.0 24.6 %collective-permute-start.28 = (bf16[1024,128]{1,0:T(8,128)(2,1)S(1)}, bf16[1024,128]{1,0:T(8,128)(2,1)S(1)}, u32[]{:S(2)}, u32[]{:S(2)}) collective-permute-start(bf16[1024,128]{1,0:T(8,128)(2,1)S(1)} %copy-done.45), channel_id=1, source_target_pairs={{0,1},{1,0},{2,3},{3,2},{4,5},{5,4},{6,7},{7,6},{8,9},{9,8},{10,11... | collective-permute-start | bytes 786440 | tf_op jit(solution)/shard_map/ppermute | solution.py:743
  217.5 24.1 %collective-permute-start.29 = (bf16[1024,128]{1,0:T(8,128)(2,1)S(1)}, bf16[1024,128]{1,0:T(8,128)(2,1)S(1)}, u32[]{:S(2)}, u32[]{:S(2)}) collective-permute-start(bf16[1024,128]{1,0:T(8,128)(2,1)S(1)} %copy-done.44), channel_id=1, source_target_pairs={{0,16},{16,0},{1,17},{17,1},{2,18},{18,2},{3,19},{19,3},{4,20},{20... | collective-permute-start | bytes 786440 | tf_op jit(solution)/shard_map/ppermute | solution.py:740
  218.3 23.3 %collective-permute-start.30 = (bf16[1024,128]{1,0:T(8,128)(2,1)S(1)}, bf16[1024,128]{1,0:T(8,128)(2,1)S(1)}, u32[]{:S(2)}, u32[]{:S(2)}) collective-permute-start(bf16[1024,128]{1,0:T(8,128)(2,1)S(1)} %copy-done.43), channel_id=1, source_target_pairs={{0,17},{1,16},{16,1},{17,0},{2,19},{3,18},{18,3},{19,2},{4,21},{5,... | collective-permute-start | bytes 786440 | tf_op jit(solution)/shard_map/ppermute | solution.py:746
  233.8 38.9 %collective-permute-start.27 = (bf16[1024,384]{1,0:T(8,128)(2,1)}, bf16[1024,384]{1,0:T(8,128)(2,1)S(1)}, u32[]{:S(2)}, u32[]{:S(2)}) collective-permute-start(bf16[1024,384]{1,0:T(8,128)(2,1)} %grad_qkv_send.1.refs_5_), channel_id=1, source_target_pairs={{0,16},{16,0},{1,17},{17,1},{2,18},{18,2},{3,19},{19,3},{4,20},{20... | collective-permute-start | bytes 2359304 | tf_op jit(solution)/shard_map/ppermute | solution.py:740
  256.3 42.7 %collective-permute-start.51 = (bf16[256,512]{1,0:T(8,128)(2,1)S(1)}, bf16[256,512]{1,0:T(8,128)(2,1)S(1)}, u32[]{:S(2)}, u32[]{:S(2)}) collective-permute-start(bf16[256,512]{1,0:T(8,128)(2,1)S(1)} %copy-done.39), channel_id=1, source_target_pairs={{0,2},{2,4},{4,6},{6,0},{1,3},{3,5},{5,7},{7,1},{8,10},{10,12},{12... | collective-permute-start | bytes 786440 | tf_op jit(solution)/shard_map/ppermute | solution.py:749
  256.7 42.3 %collective-permute-start.52 = (bf16[256,512]{1,0:T(8,128)(2,1)S(1)}, bf16[256,512]{1,0:T(8,128)(2,1)S(1)}, u32[]{:S(2)}, u32[]{:S(2)}) collective-permute-start(bf16[256,512]{1,0:T(8,128)(2,1)S(1)} %copy-done.38), channel_id=1, source_target_pairs={{0,4},{2,6},{4,0},{6,2},{1,5},{3,7},{5,1},{7,3},{8,12},{10,14},{12... | collective-permute-start | bytes 786440 | tf_op jit(solution)/shard_map/ppermute | solution.py:749
  270.2 28.8 %collective-permute-start.53 = (bf16[256,512]{1,0:T(8,128)(2,1)S(1)}, bf16[256,512]{1,0:T(8,128)(2,1)S(1)}, u32[]{:S(2)}, u32[]{:S(2)}) collective-permute-start(bf16[256,512]{1,0:T(8,128)(2,1)S(1)} %copy-done.37), channel_id=1, source_target_pairs={{0,6},{2,0},{4,2},{6,4},{1,7},{3,1},{5,3},{7,5},{8,14},{10,8},{12,... | collective-permute-start | bytes 786440 | tf_op jit(solution)/shard_map/ppermute | solution.py:749
  270.2 24.1 %collective-permute-start.26 = (bf16[304,1024]{1,0:T(8,128)(2,1)S(1)}, bf16[304,1024]{1,0:T(8,128)(2,1)S(1)}, u32[]{:S(2)}, u32[]{:S(2)}) collective-permute-start(bf16[304,1024]{1,0:T(8,128)(2,1)S(1)} %copy-done.21), channel_id=1, source_target_pairs={{0,1},{1,0},{2,3},{3,2},{4,5},{5,4},{6,7},{7,6},{8,9},{9,8},{10,11... | collective-permute-start | bytes 1867784 | tf_op jit(solution)/shard_map/ppermute | solution.py:743
  (117 other events, 1134.9 us)
Sparse Core Ops, SparseCore 0:
  29.9 90.0 all-gather.3
  216.3 77.9 reduce-scatter.1
  296.1 31.0 all-gather.5

commit v4 on v3

--- a/solution.py
+++ b/solution.py
@@ -73,7 +73,7 @@
         handle.wait()
 
 
-KNOBS = {"places": 1, "factor": 1.0, "floor": 8.0, "gnear": 1, "n2": 0, "x2": 0, "place": 0.3, "grad_out": 1.0, "ago": 0, "a1": 1, "a3": 0}
+KNOBS = {"places": 1, "factor": 1.0, "floor": 8.0, "gnear": 0, "n2": 0, "x2": 0, "place": 0.3, "grad_out": 1.0, "ago": 0, "a1": 1, "a3": 0, "rs3": 0, "zq2": 0, "tokens_back": 0.02, "small": 0.02}
 TIMES = {
     "qkv": 7.7, "attend": 11.3, "project": 4.9, "mlp": 18.6, "grad_fc2": 6.9,
     "middle_back": 5.4, "grad_fc1_send": 5.9, "grad_out": 4.9, "attend_back": 16.9,
@@ -869,6 +869,7 @@
             rest_own = across(rest_piece)
             rest_parts = over_z(rest_piece, qkv_parts)
         tick("tok", tok_near)
+        tick("gn2", grads_near)
         qkv_stack, vec = stack(
             stack_kernel,
             qkv_parts,
@@ -1104,6 +1105,8 @@
     else:
         tick("rs2", two_part)
     tick("zo", out_part)
+    qkv_part = scatter_rows(qkv_sums).astype(BF)
+    tick("zq2", qkv_part)
     grad_tokens, sums_one = run(
         tokens_back_kernel,
         [gone_own, gone_recv, tok, grad_middle, vec],
@@ -1113,12 +1116,13 @@
         "tokens_back",
     )
     grad_tokens = grad_tokens[None]
-    qkv_part = scatter_rows(qkv_sums).astype(BF)
     if not whole_two:
         two_parts = spread((two_total[:h] + two_cross.astype(F32)).astype(BF))
     one_part = scatter_rows(one_sums, *([sums_one] if on("s1") else [])).astype(BF)
     out_parts = spread(out_part)
     tick("ago", *out_parts)
+    if whole_two:
+        tick("rs3", two_part)
     if not whole_two:
         tick("ag2", *two_parts)
     tick("z1", one_part)

time: 375 us -> 369 us (0.984)
  starting transfers between devices: 72.1 us -> 66.7 us
    reduce_scatter x1, waiting for transfers between devices: 15.4 us -> 2.11 us  [on_device(): lax.psum_scatter(two_sums[0], ('x', 'fsdp'), scatter_dimension=0, tiled=T...]
    ppermute x15, starting transfers between devices: 32.5 us -> 27.1 us  [shift(): return lax.ppermute(v, 'fsdp', [(i, (i + k) % n) for i in range(n)])]
    ppermute x11, waiting for transfers between devices: 24 us -> 28.7 us  [across(): return lax.ppermute(v, 'x', swap)]
    ppermute x24, waiting for transfers between devices: 11.4 us -> 15.4 us  [core(): return lax.ppermute(v, 'core', swap)]
    ppermute x15, waiting for transfers between devices: 30.6 us -> 34.5 us  [shift(): return lax.ppermute(v, 'fsdp', [(i, (i + k) % n) for i in range(n)])]
    ppermute x13, waiting for transfers between devices: 33.1 us -> 29.2 us  [near(): return lax.ppermute(v, 'seq', swap)]
  transfers between devices with their start and end apart: 71 -> 71, of which waited for: 23 -> 25; matrix products, arithmetic and copies ran while one was open for 2% -> 2% of each run, Pallas kernels for 31% -> 32%
where the time goes in v4:
time: 369 us; the launch traced here: 365 us
  Pallas kernels  136 us (37%)
  waiting for transfers between devices  117 us (32%)
  starting transfers between devices  66.7 us (18%)
  local copies, waits for them, and re-layouts  22.7 us (6%)
  between operations  15.2 us (4%)
  other arithmetic  7.07 us (2%)
    pallas_call x15, Pallas kernels, call(): pl.pallas_call(skipping(body, len(ins), len(first)), out_shape=outs, in_s...  88.9 us
    pallas_call x7, Pallas kernels, grid_call(): pl.pallas_call(skipping(body, len(ins) + 1, len(first)), grid_spec=pltpu....  47.2 us
    ppermute x15, waiting for transfers between devices, shift(): return lax.ppermute(v, 'fsdp', [(i, (i + k) % n) for i in range(n)])  34.5 us
    ppermute x13, waiting for transfers between devices, near(): return lax.ppermute(v, 'seq', swap)  29.2 us
    ppermute x11, waiting for transfers between devices, across(): return lax.ppermute(v, 'x', swap)  28.7 us
    ppermute x15, starting transfers between devices, shift(): return lax.ppermute(v, 'fsdp', [(i, (i + k) % n) for i in range(n)])  27.1 us
    unnamed x142, local copies, waits for them, and re-layouts  15.7 us
    ppermute x24, waiting for transfers between devices, core(): return lax.ppermute(v, 'core', swap)  15.4 us
  transfers between devices with their start and end apart: 71, of which 25 were waited for; matrix products, arithmetic and copies ran while one was open for 2% of the time, Pallas kernels for 32%

profile of v4, /device:TPU:0, one launch (start us, length us, event | category | flops | bytes accessed | tf_op | source)
XLA Modules:
  0.0 364.9 jit_solution(16870730996146323351)
XLA Ops:
  30.9 9.4 %collective-permute-done.2.refs_3_ = bf16[272,640]{1,0:T(8,128)(2,1)S(1)} collective-permute-done((bf16[272,640]{1,0:T(8,128)(2,1)}, bf16[272,640]{1,0:T(8,128)(2,1)S(1)}, u32[]{:S(2)}, u32[]{:S(2)}) %collective-permute-start.2) | collective-permute-done | bytes 348192 | tf_op jit(solution)/shard_map/ppermute | solution.py:749
  43.8 5.4 %collective-permute-done.refs_10_.refs_2_ = bf16[304,1024]{1,0:T(8,128)(2,1)S(1)} collective-permute-done((bf16[304,1024]{1,0:T(8,128)(2,1)S(1)}, bf16[304,1024]{1,0:T(8,128)(2,1)S(1)}, u32[]{:S(2)}, u32[]{:S(2)}) %collective-permute-start) | collective-permute-done | bytes 622624 | tf_op jit(solution)/shard_map/ppermute | solution.py:743
  51.5 12.1 %collective-permute-done.6.refs_7_ = bf16[272,640]{1,0:T(8,128)(2,1)S(1)} collective-permute-done((bf16[272,640]{1,0:T(8,128)(2,1)S(1)}, bf16[272,640]{1,0:T(8,128)(2,1)S(1)}, u32[]{:S(2)}, u32[]{:S(2)}) %collective-permute-start.6) | collective-permute-done | bytes 348192 | tf_op jit(solution)/shard_map/ppermute | solution.py:740
  63.6 7.4 %collective-permute-done.7.refs_8_ = bf16[272,640]{1,0:T(8,128)(2,1)S(1)} collective-permute-done((bf16[272,640]{1,0:T(8,128)(2,1)S(1)}, bf16[272,640]{1,0:T(8,128)(2,1)S(1)}, u32[]{:S(2)}, u32[]{:S(2)}) %collective-permute-start.7) | collective-permute-done | bytes 348192 | tf_op jit(solution)/shard_map/ppermute | solution.py:740
  75.2 5.1 %collective-permute-done.9.refs_5_.refs_6_.refs_7_.refs_4_ = bf16[2048,640]{1,0:T(8,128)(2,1)S(1)} collective-permute-done((bf16[2048,640]{1,0:T(8,128)(2,1)}, bf16[2048,640]{1,0:T(8,128)(2,1)S(1)}, u32[]{:S(2)}, u32[]{:S(2)}) %collective-permute-start.9) | collective-permute-done | bytes 2621472 | tf_op jit(solution)/shard_map/ppermute | solution.py:737
  81.8 7.7 %qkv.1 = (bf16[608,1024]{1,0:T(8,128)(2,1)}, bf16[608,512]{1,0:T(8,128)(2,1)}, bf16[608,512]{1,0:T(8,128)(2,1)}, bf16[608,512]{1,0:T(8,128)(2,1)}) custom-call(s32[3]{0:T(128)} %pad_add_fusion.ids.refs_0_, bf16[304,1024]{1,0:T(8,128)(2,1)} %copy-done, bf16[304,1024]{1,0:T(8,128)(2,1)} %copy-done.25, f32[16,1024]{1,0:T(8,128)} %get-tuple-element.64.refs_3_.refs_4_.refs_5_, ...), custom_call_target="tpu_custom_call" | custom-call | flops 9200000000 | bytes 262144 | tf_op jit(solution)/shard_map/qkv/pallas_call | solution.py:104
  89.5 11.3 %attend.1 = (bf16[304,512]{1,0:T(8,128)(2,1)}, bf16[304,512]{1,0:T(8,128)(2,1)}, f32[4,4,304]{2,1,0:T(4,128)}) custom-call(s32[3]{0:T(128)} %pad_add_fusion.ids.refs_0_, bf16[608,512]{1,0:T(8,128)(2,1)} %get-tuple-element.66.refs_1_, bf16[608,512]{1,0:T(8,128)(2,1)} %get-tuple-element.67.refs_2_, bf16[608,512]{1,0:T(8,128)(2,1)} %get-tuple-element.68.refs_3_, ...), custom_call_target="tpu_custom_call" | custom-call | flops 12995000320 | bytes 262144 | tf_op jit(solution)/shard_map/attend/pallas_call | solution.py:117
  102.4 8.1 %collective-permute-done.10.refs_3_ = bf16[304,512]{1,0:T(8,128)(2,1)S(1)} collective-permute-done((bf16[304,512]{1,0:T(8,128)(2,1)}, bf16[304,512]{1,0:T(8,128)(2,1)S(1)}, u32[]{:S(2)}, u32[]{:S(2)}) %collective-permute-start.10) | collective-permute-done | bytes 311328 | tf_op jit(solution)/shard_map/ppermute | solution.py:743
  122.2 5.4 %collective-permute-done.15.refs_11_.refs_5_ = bf16[304,1024]{1,0:T(8,128)(2,1)S(1)} collective-permute-done((bf16[304,1024]{1,0:T(8,128)(2,1)S(1)}, bf16[304,1024]{1,0:T(8,128)(2,1)S(1)}, u32[]{:S(2)}, u32[]{:S(2)}) %collective-permute-start.15) | collective-permute-done | bytes 622624 | tf_op jit(solution)/shard_map/ppermute | solution.py:737
  130.2 7.0 %collective-permute-done.11.refs_2_ = bf16[304,1024]{1,0:T(8,128)(2,1)} collective-permute-done((bf16[304,1024]{1,0:T(8,128)(2,1)}, bf16[304,1024]{1,0:T(8,128)(2,1)}, u32[]{:S(2)}, u32[]{:S(2)}) %collective-permute-start.11) | collective-permute-done | bytes 622624 | tf_op jit(solution)/shard_map/ppermute | solution.py:743
  139.7 17.8 %mlp.1 = (bf16[608,2048]{1,0:T(8,128)(2,1)}, bf16[608,2048]{1,0:T(8,128)(2,1)}, f32[304,1024]{1,0:T(8,128)}, bf16[304,1024]{1,0:T(8,128)(2,1)}, f32[304,1024]{1,...) custom-call(s32[3]{0:T(128)} %pad_add_fusion.ids.refs_0_, ...), custom_call_target="tpu_custom_call" | custom-call | flops 21390000128 | bytes 262144 | tf_op jit(solution)/shard_map/mlp/pallas_call | solution.py:104
  164.1 7.4 %grad_fc2.1.refs_8_ = bf16[1024,1024]{1,0:T(8,128)(2,1)} custom-call(s32[3]{0:T(128)} %pad_add_fusion.ids.refs_0_, bf16[608,2048]{1,0:T(8,128)(2,1)} %get-tuple-element.81.refs_1_.refs_7_.refs_5_, bf16[608,2048]{1,0:T(8,128)(2,1)} %copy-done.17, bf16[304,1024]{1,0:T(8,128)(2,1)} %copy-done.5, bf16[304,1024]{1,0:T(8,128)(2,1)} %collective-permute-done.8.refs_11_.refs_4_, ...), custom_call_target="tpu_custom_call" | custom-call | flops 9200000000 | bytes 262144 | tf_op jit(solution)/shard_map/grad_fc2/pallas_call | solution.py:104
  176.0 5.4 %middle_back.1 = (f32[304,1024]{1,0:T(8,128)}, bf16[304,1024]{1,0:T(8,128)(2,1)}, bf16[304,512]{1,0:T(8,128)(2,1)}, bf16[304,512]{1,0:T(8,128)(2,1)}, f32[4,1024]{1,0:T(4,128)}) custom-call(s32[3]{0:T(128)} %pad_add_fusion.ids.refs_0_, f32[304,1024]{1,0:T(8,128)} %get-tuple-element.79.refs_1_, bf16[304,1024]{1,0:T(8,128)(2,1)} %copy-done.26, ...), custom_call_target="tpu_custom_call" | custom-call | flops 9200000000 | bytes 262144 | tf_op jit(solution)/shard_map/middle_back/pallas_call | solution.py:104
  183.0 5.9 %grad_fc1_send.1.refs_5_ = bf16[1024,512]{1,0:T(8,128)(2,1)} custom-call(s32[3]{0:T(128)} %pad_add_fusion.ids.refs_0_, bf16[304,1024]{1,0:T(8,128)(2,1)} %get-tuple-element.76.refs_1_.refs_14_, bf16[304,1024]{1,0:T(8,128)(2,1)} %collective-permute-done.11.refs_2_, bf16[304,1024]{1,0:T(8,128)(2,1)} %collective-permute-done.17.refs_13_.refs_3_, ...), custom_call_target="tpu_custom_call" | custom-call | flops 9200000000 | bytes 262144 | tf_op jit(solution)/shard_map/grad_fc1_send/pallas_call | solution.py:104
  196.1 16.9 %attend_back.1 = (bf16[2,608,384]{2,1,0:T(8,128)(2,1)}, bf16[2,608,384]{2,1,0:T(8,128)(2,1)}, f32[4,1,384]{2,1,0:T(1,128)}) custom-call(s32[3]{0:T(128)} %pad_add_fusion.ids.refs_0_, bf16[608,512]{1,0:T(8,128)(2,1)} %get-tuple-element.66.refs_1_, bf16[608,512]{1,0:T(8,128)(2,1)} %get-tuple-element.67.refs_2_, bf16[608,512]{1,0:T(8,128)(2,1)} %get-tuple-element.68.refs_3_, ...), custom_call_target="tpu_custom_call" | custom-call | flops 19434999808 | bytes 262144 | tf_op jit(solution)/shard_map/attend_back/pallas_call | solution.py:117
  216.7 7.0 %collective-permute-done.25.refs_7_ = bf16[1024,512]{1,0:T(8,128)(2,1)S(1)} collective-permute-done((bf16[1024,512]{1,0:T(8,128)(2,1)}, bf16[1024,512]{1,0:T(8,128)(2,1)S(1)}, u32[]{:S(2)}, u32[]{:S(2)}) %collective-permute-start.25) | collective-permute-done | bytes 1048608 | tf_op jit(solution)/shard_map/ppermute | solution.py:740
  224.6 5.6 %grad_fc1_keep.1 = (f32[256,512]{1,0:T(8,128)}, bf16[256,512]{1,0:T(8,128)(2,1)}, bf16[256,512]{1,0:T(8,128)(2,1)}, bf16[256,512]{1,0:T(8,128)(2,1)}) custom-call(s32[3]{0:T(128)} %pad_add_fusion.ids.refs_0_, bf16[304,1024]{1,0:T(8,128)(2,1)} %get-tuple-element.76.refs_1_.refs_14_, bf16[304,1024]{1,0:T(8,128)(2,1)} %collective-permute-done.11.refs_2_, ...), custom_call_target="tpu_custom_call" | custom-call | flops 9200000000 | bytes 262144 | tf_op jit(solution)/shard_map/grad_fc1_keep/pallas_call | solution.py:104
  231.2 5.7 %grad_qkv_send.1.refs_5_ = bf16[1024,384]{1,0:T(8,128)(2,1)} custom-call(s32[3]{0:T(128)} %pad_add_fusion.ids.refs_0_, bf16[608,1024]{1,0:T(8,128)(2,1)} %get-tuple-element.69.refs_4_.refs_1_, bf16[608,1024]{1,0:T(8,128)(2,1)} %copy-done.19, bf16[2,608,384]{2,1,0:T(8,128)(2,1)} %get-tuple-element.89.refs_8_.refs_3_.refs_1_, bf16[2,608,384]{2,1,0:T(8,128)(2,1)} %copy-done.21, ...), custom_call_target="tpu_custom_call" | custom-call | flops 9200000000 | bytes 262144 | tf_op jit(solution)/shard_map/grad_qkv_send/pallas_call | solution.py:104
  237.6 7.1 %qkv_back.1 = (f32[304,1024]{1,0:T(8,128)}, bf16[304,1024]{1,0:T(8,128)(2,1)}) custom-call(s32[3]{0:T(128)} %pad_add_fusion.ids.refs_0_, bf16[2,608,384]{2,1,0:T(8,128)(2,1)} %get-tuple-element.89.refs_8_.refs_3_.refs_1_, bf16[2,608,384]{2,1,0:T(8,128)(2,1)} %get-tuple-element.90.refs_2_, bf16[2048,640]{1,0:T(8,128)(2,1)} %bitcast.41, ...), custom_call_target="tpu_custom_call" | custom-call | flops 9200000000 | bytes 262144 | tf_op jit(solution)/shard_map/qkv_back/pallas_call | solution.py:104
  256.6 11.4 %collective-permute-done.32 = bf16[256,128]{1,0:T(8,128)(2,1)S(1)} collective-permute-done((bf16[256,128]{1,0:T(8,128)(2,1)}, bf16[256,128]{1,0:T(8,128)(2,1)S(1)}, u32[]{:S(2)}, u32[]{:S(2)}) %collective-permute-start.32) | collective-permute-done | bytes 65568 | tf_op jit(solution)/shard_map/ppermute | solution.py:749
  271.4 5.4 %grad_qkv_keep.1 = (f32[256,384]{1,0:T(8,128)}, bf16[256,384]{1,0:T(8,128)(2,1)}, bf16[256,384]{1,0:T(8,128)(2,1)}, bf16[256,384]{1,0:T(8,128)(2,1)}) custom-call(s32[3]{0:T(128)} %pad_add_fusion.ids.refs_0_, bf16[608,1024]{1,0:T(8,128)(2,1)} %get-tuple-element.69.refs_4_.refs_1_, bf16[608,1024]{1,0:T(8,128)(2,1)} %copy-done.19, ...), custom_call_target="tpu_custom_call" | custom-call | flops 9200000000 | bytes 262144 | tf_op jit(solution)/shard_map/grad_qkv_keep/pallas_call | solution.py:104
  276.8 5.3 %collective-permute-done.26.refs_2_ = bf16[304,1024]{1,0:T(8,128)(2,1)S(1)} collective-permute-done((bf16[304,1024]{1,0:T(8,128)(2,1)S(1)}, bf16[304,1024]{1,0:T(8,128)(2,1)S(1)}, u32[]{:S(2)}, u32[]{:S(2)}) %collective-permute-start.26) | collective-permute-done | bytes 622624 | tf_op jit(solution)/shard_map/ppermute | solution.py:743
  289.2 8.2 %collective-permute-start.61 = (f32[16,256]{1,0:T(8,128)}, f32[16,256]{1,0:T(8,128)S(1)}, u32[]{:S(2)}, u32[]{:S(2)}) collective-permute-start(f32[16,256]{1,0:T(8,128)} %get-tuple-element.116), channel_id=1, source_target_pairs={{0,2},{2,4},{4,6},{6,0},{1,3},{3,5},{5,7},{7,1},{8,10},{10,12},{12... | collective-permute-start | bytes 49160 | tf_op jit(solution)/shard_map/ppermute | solution.py:749
  334.0 5.0 %place.3.refs_9_ = f32[256,4096]{1,0:T(8,128)} custom-call(s32[3]{0:T(128)} %pad_add_fusion.ids.refs_0_, bf16[256,512]{1,0:T(8,128)(2,1)} %add_convert_fusion.refs_7_.refs_1_.refs_11_, bf16[256,512]{1,0:T(8,128)(2,1)} %copy-done.40, bf16[256,512]{1,0:T(8,128)(2,1)} %copy-done.41, bf16[256,512]{1,0:T(8,128)(2,1)} %copy-done.42, bf16[256,512]{1,0:T(8,128)(2,1)} %copy-done.46, ...), custom_call_target="tpu_custom_call" | custom-call | flops 2760000000 | bytes 262144 | tf_op jit(solution)/shard_map/place/pallas_call | solution.py:117
  (306 shorter events, 156.8 us)
Async XLA Ops:
  7.2 112.8 %all-gather.4.cloned.1.call-start = ((), (), s32[]{:S(2)}) async-start(), calls=%async_computation.1 | async-start | bytes 4718592 | tf_op jit(solution)/shard_map/all_gather | solution.py:867
  14.8 25.4 %collective-permute-start.2 = (bf16[272,640]{1,0:T(8,128)(2,1)}, bf16[272,640]{1,0:T(8,128)(2,1)S(1)}, u32[]{:S(2)}, u32[]{:S(2)}) collective-permute-start(bf16[272,640]{1,0:T(8,128)(2,1)} %cast_qkv.1.refs_6_.refs_1_), channel_id=1, source_target_pairs={{0,4},{2,6},{4,0},{6,2},{1,5},{3,7},{5,1},{7,3},{8,12},{10,14},{12... | collective-permute-start | bytes 1044488 | tf_op jit(solution)/shard_map/ppermute | solution.py:749
  17.4 24.3 %collective-permute-start.3 = (bf16[272,640]{1,0:T(8,128)(2,1)}, bf16[272,640]{1,0:T(8,128)(2,1)S(1)}, u32[]{:S(2)}, u32[]{:S(2)}) collective-permute-start(bf16[272,640]{1,0:T(8,128)(2,1)} %cast_qkv.1.refs_6_.refs_1_), channel_id=1, source_target_pairs={{0,6},{2,0},{4,2},{6,4},{1,7},{3,1},{5,3},{7,5},{8,14},{10,8},{12,... | collective-permute-start | bytes 1044488 | tf_op jit(solution)/shard_map/ppermute | solution.py:749
  18.8 23.5 %collective-permute-start.4 = (bf16[272,640]{1,0:T(8,128)(2,1)}, bf16[272,640]{1,0:T(8,128)(2,1)S(1)}, u32[]{:S(2)}, u32[]{:S(2)}) collective-permute-start(bf16[272,640]{1,0:T(8,128)(2,1)} %cast_qkv.1.refs_6_.refs_1_), channel_id=1, source_target_pairs={{0,16},{16,0},{1,17},{17,1},{2,18},{18,2},{3,19},{19,3},{4,20},{20... | collective-permute-start | bytes 1044488 | tf_op jit(solution)/shard_map/ppermute | solution.py:740
  21.2 22.6 %collective-permute-start.8 = (bf16[304,1024]{1,0:T(8,128)(2,1)S(1)}, bf16[304,1024]{1,0:T(8,128)(2,1)}, u32[]{:S(2)}, u32[]{:S(2)}) collective-permute-start(bf16[304,1024]{1,0:T(8,128)(2,1)S(1)} %pad.8.refs_3_.refs_4_), channel_id=1, source_target_pairs={{0,1},{1,0},{2,3},{3,2},{4,5},{5,4},{6,7},{7,6},{8,9},{9,8},{10,11... | collective-permute-start | bytes 1867784 | tf_op jit(solution)/shard_map/ppermute | solution.py:743
  26.2 23.1 %collective-permute-start = (bf16[304,1024]{1,0:T(8,128)(2,1)S(1)}, bf16[304,1024]{1,0:T(8,128)(2,1)S(1)}, u32[]{:S(2)}, u32[]{:S(2)}) collective-permute-start(bf16[304,1024]{1,0:T(8,128)(2,1)S(1)} %pad.7.refs_1_.refs_3_), channel_id=1, source_target_pairs={{0,1},{1,0},{2,3},{3,2},{4,5},{5,4},{6,7},{7,6},{8,9},{9,8},{10,11... | collective-permute-start | bytes 1867784 | tf_op jit(solution)/shard_map/ppermute | solution.py:743
  30.8 216.0 %reduce-scatter.2.cloned.1.call-start = ((), (), s32[]{:S(2)}) async-start(), calls=%async_computation.2 | async-start | bytes 2359296 | tf_op jit(solution)/shard_map/reduce_scatter | solution.py:1085
  41.8 21.9 %collective-permute-start.6 = (bf16[272,640]{1,0:T(8,128)(2,1)S(1)}, bf16[272,640]{1,0:T(8,128)(2,1)S(1)}, u32[]{:S(2)}, u32[]{:S(2)}) collective-permute-start(bf16[272,640]{1,0:T(8,128)(2,1)S(1)} %collective-permute-done.2.refs_3_), channel_id=1, source_target_pairs={{0,16},{16,0},{1,17},{17,1},{2,18},{18,2},{3,19},{19,3},{4,20},{20... | collective-permute-start | bytes 1044488 | tf_op jit(solution)/shard_map/ppermute | solution.py:740
  42.3 28.7 %collective-permute-start.7 = (bf16[272,640]{1,0:T(8,128)(2,1)S(1)}, bf16[272,640]{1,0:T(8,128)(2,1)S(1)}, u32[]{:S(2)}, u32[]{:S(2)}) collective-permute-start(bf16[272,640]{1,0:T(8,128)(2,1)S(1)} %collective-permute-done.3.refs_4_), channel_id=1, source_target_pairs={{0,16},{16,0},{1,17},{17,1},{2,18},{18,2},{3,19},{19,3},{4,20},{20... | collective-permute-start | bytes 1044488 | tf_op jit(solution)/shard_map/ppermute | solution.py:740
  119.9 19.7 %collective-permute-start.12 = (bf16[2048,1024]{1,0:T(8,128)(2,1)}, bf16[2048,1024]{1,0:T(8,128)(2,1)}, u32[]{:S(2)}, u32[]{:S(2)}) collective-permute-start(bf16[2048,1024]{1,0:T(8,128)(2,1)} %all-gather.4.cloned.1.call-done.refs_6_), channel_id=1, source_target_pairs={{0,8},{8,0},{1,9},{9,1},{2,10},{10,2},{3,11},{11,3},{4,12},{12,4},... | collective-permute-start | bytes 12582920 | tf_op jit(solution)/shard_map/ppermute | solution.py:737
  120.5 16.8 %collective-permute-start.11 = (bf16[304,1024]{1,0:T(8,128)(2,1)}, bf16[304,1024]{1,0:T(8,128)(2,1)}, u32[]{:S(2)}, u32[]{:S(2)}) collective-permute-start(bf16[304,1024]{1,0:T(8,128)(2,1)} %get-tuple-element.76.refs_1_.refs_14_), channel_id=1, source_target_pairs={{0,1},{1,0},{2,3},{3,2},{4,5},{5,4},{6,7},{7,6},{8,9},{9,8},{10,11... | collective-permute-start | bytes 1867784 | tf_op jit(solution)/shard_map/ppermute | solution.py:743
  158.1 17.1 %collective-permute-start.20 = (bf16[304,1024]{1,0:T(8,128)(2,1)}, bf16[304,1024]{1,0:T(8,128)(2,1)S(1)}, u32[]{:S(2)}, u32[]{:S(2)}) collective-permute-start(bf16[304,1024]{1,0:T(8,128)(2,1)} %get-tuple-element.80), channel_id=1, source_target_pairs={{0,1},{1,0},{2,3},{3,2},{4,5},{5,4},{6,7},{7,6},{8,9},{9,8},{10,11... | collective-permute-start | bytes 1867784 | tf_op jit(solution)/shard_map/ppermute | solution.py:743
  159.6 55.6 %collective-permute-start.19 = (bf16[304,1024]{1,0:T(8,128)(2,1)}, bf16[304,1024]{1,0:T(8,128)(2,1)S(1)}, u32[]{:S(2)}, u32[]{:S(2)}) collective-permute-start(bf16[304,1024]{1,0:T(8,128)(2,1)} %get-tuple-element.78), channel_id=1, source_target_pairs={{0,1},{1,0},{2,3},{3,2},{4,5},{5,4},{6,7},{7,6},{8,9},{9,8},{10,11... | collective-permute-start | bytes 1867784 | tf_op jit(solution)/shard_map/ppermute | solution.py:743
  171.5 182.5 %all-gather.6.cloned.1.call-start = ((), (), s32[]{:S(2)}) async-start(), calls=%async_computation.3 | async-start | bytes 2359296 | tf_op jit(solution)/shard_map/all_gather | solution.py:1086
  188.9 34.7 %collective-permute-start.25 = (bf16[1024,512]{1,0:T(8,128)(2,1)}, bf16[1024,512]{1,0:T(8,128)(2,1)S(1)}, u32[]{:S(2)}, u32[]{:S(2)}) collective-permute-start(bf16[1024,512]{1,0:T(8,128)(2,1)} %grad_fc1_send.1.refs_5_), channel_id=1, source_target_pairs={{0,16},{16,0},{1,17},{17,1},{2,18},{18,2},{3,19},{19,3},{4,20},{20... | collective-permute-start | bytes 3145736 | tf_op jit(solution)/shard_map/ppermute | solution.py:740
  213.0 17.3 %collective-permute-start.24 = (bf16[2,608,384]{2,1,0:T(8,128)(2,1)}, bf16[2,608,384]{2,1,0:T(8,128)(2,1)S(1)}, u32[]{:S(2)}, u32[]{:S(2)}) collective-permute-start(bf16[2,608,384]{2,1,0:T(8,128)(2,1)} %get-tuple-element.90.refs_2_), channel_id=1, source_target_pairs={{0,8},{8,0},{1,9},{9,1},{2,10},{10,2},{3,11},{11,3},{4,12},{12,4},... | collective-permute-start | bytes 2801672 | tf_op jit(solution)/shard_map/ppermute | solution.py:737
  213.1 33.8 %collective-permute-start.28 = (bf16[1024,128]{1,0:T(8,128)(2,1)S(1)}, bf16[1024,128]{1,0:T(8,128)(2,1)S(1)}, u32[]{:S(2)}, u32[]{:S(2)}) collective-permute-start(bf16[1024,128]{1,0:T(8,128)(2,1)S(1)} %copy-done.45), channel_id=1, source_target_pairs={{0,1},{1,0},{2,3},{3,2},{4,5},{5,4},{6,7},{7,6},{8,9},{9,8},{10,11... | collective-permute-start | bytes 786440 | tf_op jit(solution)/shard_map/ppermute | solution.py:743
  213.7 33.2 %collective-permute-start.29 = (bf16[1024,128]{1,0:T(8,128)(2,1)S(1)}, bf16[1024,128]{1,0:T(8,128)(2,1)S(1)}, u32[]{:S(2)}, u32[]{:S(2)}) collective-permute-start(bf16[1024,128]{1,0:T(8,128)(2,1)S(1)} %copy-done.44), channel_id=1, source_target_pairs={{0,16},{16,0},{1,17},{17,1},{2,18},{18,2},{3,19},{19,3},{4,20},{20... | collective-permute-start | bytes 786440 | tf_op jit(solution)/shard_map/ppermute | solution.py:740
  215.1 31.8 %collective-permute-start.30 = (bf16[1024,128]{1,0:T(8,128)(2,1)S(1)}, bf16[1024,128]{1,0:T(8,128)(2,1)S(1)}, u32[]{:S(2)}, u32[]{:S(2)}) collective-permute-start(bf16[1024,128]{1,0:T(8,128)(2,1)S(1)} %copy-done.43), channel_id=1, source_target_pairs={{0,17},{1,16},{16,1},{17,0},{2,19},{3,18},{18,3},{19,2},{4,21},{5,... | collective-permute-start | bytes 786440 | tf_op jit(solution)/shard_map/ppermute | solution.py:746
  236.9 33.6 %collective-permute-start.27 = (bf16[1024,384]{1,0:T(8,128)(2,1)}, bf16[1024,384]{1,0:T(8,128)(2,1)S(1)}, u32[]{:S(2)}, u32[]{:S(2)}) collective-permute-start(bf16[1024,384]{1,0:T(8,128)(2,1)} %grad_qkv_send.1.refs_5_), channel_id=1, source_target_pairs={{0,16},{16,0},{1,17},{17,1},{2,18},{18,2},{3,19},{19,3},{4,20},{20... | collective-permute-start | bytes 2359304 | tf_op jit(solution)/shard_map/ppermute | solution.py:740
  250.3 17.7 %collective-permute-start.32 = (bf16[256,128]{1,0:T(8,128)(2,1)}, bf16[256,128]{1,0:T(8,128)(2,1)S(1)}, u32[]{:S(2)}, u32[]{:S(2)}) collective-permute-start(bf16[256,128]{1,0:T(8,128)(2,1)} %get-tuple-element.100), channel_id=1, source_target_pairs={{0,4},{2,6},{4,0},{6,2},{1,5},{3,7},{5,1},{7,3},{8,12},{10,14},{12... | collective-permute-start | bytes 196616 | tf_op jit(solution)/shard_map/ppermute | solution.py:749
  253.7 33.1 %collective-permute-start.51 = (bf16[256,512]{1,0:T(8,128)(2,1)S(1)}, bf16[256,512]{1,0:T(8,128)(2,1)S(1)}, u32[]{:S(2)}, u32[]{:S(2)}) collective-permute-start(bf16[256,512]{1,0:T(8,128)(2,1)S(1)} %copy-done.39), channel_id=1, source_target_pairs={{0,2},{2,4},{4,6},{6,0},{1,3},{3,5},{5,7},{7,1},{8,10},{10,12},{12... | collective-permute-start | bytes 786440 | tf_op jit(solution)/shard_map/ppermute | solution.py:749
  256.6 30.3 %collective-permute-start.52 = (bf16[256,512]{1,0:T(8,128)(2,1)S(1)}, bf16[256,512]{1,0:T(8,128)(2,1)S(1)}, u32[]{:S(2)}, u32[]{:S(2)}) collective-permute-start(bf16[256,512]{1,0:T(8,128)(2,1)S(1)} %copy-done.38), channel_id=1, source_target_pairs={{0,4},{2,6},{4,0},{6,2},{1,5},{3,7},{5,1},{7,3},{8,12},{10,14},{12... | collective-permute-start | bytes 786440 | tf_op jit(solution)/shard_map/ppermute | solution.py:749
  268.0 18.9 %collective-permute-start.53 = (bf16[256,512]{1,0:T(8,128)(2,1)S(1)}, bf16[256,512]{1,0:T(8,128)(2,1)S(1)}, u32[]{:S(2)}, u32[]{:S(2)}) collective-permute-start(bf16[256,512]{1,0:T(8,128)(2,1)S(1)} %copy-done.37), channel_id=1, source_target_pairs={{0,6},{2,0},{4,2},{6,4},{1,7},{3,1},{5,3},{7,5},{8,14},{10,8},{12,... | collective-permute-start | bytes 786440 | tf_op jit(solution)/shard_map/ppermute | solution.py:749
  (117 other events, 1187.2 us)
Sparse Core Ops, SparseCore 0:
  30.9 88.9 all-gather.3
  171.7 75.1 reduce-scatter.1
  248.7 30.2 all-gather.5

commit v5 on v4

--- a/solution.py
+++ b/solution.py
@@ -73,7 +73,7 @@
         handle.wait()
 
 
-KNOBS = {"places": 1, "factor": 1.0, "floor": 8.0, "gnear": 0, "n2": 0, "x2": 0, "place": 0.3, "grad_out": 1.0, "ago": 0, "a1": 1, "a3": 0, "rs3": 0, "zq2": 0, "tokens_back": 0.02, "small": 0.02}
+KNOBS = {"places": 1, "factor": 1.0, "floor": 8.0, "gnear": 0, "n2": 0, "x2": 0, "place": 0.3, "grad_out": 1.0, "ago": 0, "a1": 1, "a3": 0, "rs3": 0, "zq2": 0, "tokens_back": 0.02, "small": 0.02, "z1": 0, "ag1": 0, "agq": 0, "zq": 0}
 TIMES = {
     "qkv": 7.7, "attend": 11.3, "project": 4.9, "mlp": 18.6, "grad_fc2": 6.9,
     "middle_back": 5.4, "grad_fc1_send": 5.9, "grad_out": 4.9, "attend_back": 16.9,

time: 369 us -> 367 us (level)
  transfers between devices with their start and end apart: 71 -> 71, of which waited for: 25 -> 28; matrix products, arithmetic and copies ran while one was open for 2% -> 2% of each run, Pallas kernels for 32% -> 32%
where the time goes in v5:
time: 367 us; the launch traced here: 363 us
  Pallas kernels  136 us (37%)
  waiting for transfers between devices  116 us (32%)
  starting transfers between devices  67.3 us (18%)
  local copies, waits for them, and re-layouts  22.1 us (6%)
  between operations  15.2 us (4%)
  other arithmetic  6.34 us (2%)
    pallas_call x15, Pallas kernels, call(): pl.pallas_call(skipping(body, len(ins), len(first)), out_shape=outs, in_s...  89 us
    pallas_call x7, Pallas kernels, grid_call(): pl.pallas_call(skipping(body, len(ins) + 1, len(first)), grid_spec=pltpu....  47.2 us
    ppermute x15, waiting for transfers between devices, shift(): return lax.ppermute(v, 'fsdp', [(i, (i + k) % n) for i in range(n)])  33.5 us
    ppermute x13, waiting for transfers between devices, near(): return lax.ppermute(v, 'seq', swap)  29.1 us
    ppermute x11, waiting for transfers between devices, across(): return lax.ppermute(v, 'x', swap)  29 us
    ppermute x15, starting transfers between devices, shift(): return lax.ppermute(v, 'fsdp', [(i, (i + k) % n) for i in range(n)])  26.7 us
    ppermute x13, starting transfers between devices, near(): return lax.ppermute(v, 'seq', swap)  16.7 us
    ppermute x24, waiting for transfers between devices, core(): return lax.ppermute(v, 'core', swap)  15.4 us
  transfers between devices with their start and end apart: 71, of which 28 were waited for; matrix products, arithmetic and copies ran while one was open for 2% of the time, Pallas kernels for 32%

profile of v5, /device:TPU:0, one launch (start us, length us, event | category | flops | bytes accessed | tf_op | source)
XLA Modules:
  0.0 363.3 jit_solution(18317001359093624851)
XLA Ops:
  30.9 9.4 %collective-permute-done.2.refs_3_ = bf16[272,640]{1,0:T(8,128)(2,1)S(1)} collective-permute-done((bf16[272,640]{1,0:T(8,128)(2,1)}, bf16[272,640]{1,0:T(8,128)(2,1)S(1)}, u32[]{:S(2)}, u32[]{:S(2)}) %collective-permute-start.2) | collective-permute-done | bytes 348192 | tf_op jit(solution)/shard_map/ppermute | solution.py:749
  43.8 5.4 %collective-permute-done.refs_10_.refs_2_ = bf16[304,1024]{1,0:T(8,128)(2,1)S(1)} collective-permute-done((bf16[304,1024]{1,0:T(8,128)(2,1)S(1)}, bf16[304,1024]{1,0:T(8,128)(2,1)S(1)}, u32[]{:S(2)}, u32[]{:S(2)}) %collective-permute-start) | collective-permute-done | bytes 622624 | tf_op jit(solution)/shard_map/ppermute | solution.py:743
  51.5 12.1 %collective-permute-done.6.refs_7_ = bf16[272,640]{1,0:T(8,128)(2,1)S(1)} collective-permute-done((bf16[272,640]{1,0:T(8,128)(2,1)S(1)}, bf16[272,640]{1,0:T(8,128)(2,1)S(1)}, u32[]{:S(2)}, u32[]{:S(2)}) %collective-permute-start.6) | collective-permute-done | bytes 348192 | tf_op jit(solution)/shard_map/ppermute | solution.py:740
  63.6 7.4 %collective-permute-done.7.refs_8_ = bf16[272,640]{1,0:T(8,128)(2,1)S(1)} collective-permute-done((bf16[272,640]{1,0:T(8,128)(2,1)S(1)}, bf16[272,640]{1,0:T(8,128)(2,1)S(1)}, u32[]{:S(2)}, u32[]{:S(2)}) %collective-permute-start.7) | collective-permute-done | bytes 348192 | tf_op jit(solution)/shard_map/ppermute | solution.py:740
  75.2 5.1 %collective-permute-done.9.refs_5_.refs_6_.refs_7_.refs_4_ = bf16[2048,640]{1,0:T(8,128)(2,1)S(1)} collective-permute-done((bf16[2048,640]{1,0:T(8,128)(2,1)}, bf16[2048,640]{1,0:T(8,128)(2,1)S(1)}, u32[]{:S(2)}, u32[]{:S(2)}) %collective-permute-start.9) | collective-permute-done | bytes 2621472 | tf_op jit(solution)/shard_map/ppermute | solution.py:737
  81.8 7.7 %qkv.1 = (bf16[608,1024]{1,0:T(8,128)(2,1)}, bf16[608,512]{1,0:T(8,128)(2,1)}, bf16[608,512]{1,0:T(8,128)(2,1)}, bf16[608,512]{1,0:T(8,128)(2,1)}) custom-call(s32[3]{0:T(128)} %pad_add_fusion.ids.refs_0_, bf16[304,1024]{1,0:T(8,128)(2,1)} %copy-done, bf16[304,1024]{1,0:T(8,128)(2,1)} %copy-done.25, f32[16,1024]{1,0:T(8,128)} %get-tuple-element.64.refs_3_.refs_4_.refs_5_, ...), custom_call_target="tpu_custom_call" | custom-call | flops 9200000000 | bytes 262144 | tf_op jit(solution)/shard_map/qkv/pallas_call | solution.py:104
  89.5 11.3 %attend.1 = (bf16[304,512]{1,0:T(8,128)(2,1)}, bf16[304,512]{1,0:T(8,128)(2,1)}, f32[4,4,304]{2,1,0:T(4,128)}) custom-call(s32[3]{0:T(128)} %pad_add_fusion.ids.refs_0_, bf16[608,512]{1,0:T(8,128)(2,1)} %get-tuple-element.66.refs_1_, bf16[608,512]{1,0:T(8,128)(2,1)} %get-tuple-element.67.refs_2_, bf16[608,512]{1,0:T(8,128)(2,1)} %get-tuple-element.68.refs_3_, ...), custom_call_target="tpu_custom_call" | custom-call | flops 12995000320 | bytes 262144 | tf_op jit(solution)/shard_map/attend/pallas_call | solution.py:117
  102.4 8.1 %collective-permute-done.10.refs_3_ = bf16[304,512]{1,0:T(8,128)(2,1)S(1)} collective-permute-done((bf16[304,512]{1,0:T(8,128)(2,1)}, bf16[304,512]{1,0:T(8,128)(2,1)S(1)}, u32[]{:S(2)}, u32[]{:S(2)}) %collective-permute-start.10) | collective-permute-done | bytes 311328 | tf_op jit(solution)/shard_map/ppermute | solution.py:743
  111.2 5.0 %project.1 = (bf16[304,1024]{1,0:T(8,128)(2,1)}, f32[304,1024]{1,0:T(8,128)}, bf16[304,1024]{1,0:T(8,128)(2,1)}) custom-call(s32[3]{0:T(128)} %pad_add_fusion.ids.refs_0_, bf16[304,1024]{1,0:T(8,128)(2,1)} %copy-done, bf16[304,512]{1,0:T(8,128)(2,1)} %get-tuple-element.70.refs_2_.refs_7_.refs_4_, bf16[304,512]{1,0:T(8,128)(2,1)} %copy-done.36, ...), custom_call_target="tpu_custom_call" | custom-call | flops 9200000000 | bytes 262144 | tf_op jit(solution)/shard_map/project/pallas_call | solution.py:104
  122.2 5.4 %collective-permute-done.15.refs_11_.refs_5_ = bf16[304,1024]{1,0:T(8,128)(2,1)S(1)} collective-permute-done((bf16[304,1024]{1,0:T(8,128)(2,1)S(1)}, bf16[304,1024]{1,0:T(8,128)(2,1)S(1)}, u32[]{:S(2)}, u32[]{:S(2)}) %collective-permute-start.15) | collective-permute-done | bytes 622624 | tf_op jit(solution)/shard_map/ppermute | solution.py:737
  130.2 7.0 %collective-permute-done.11.refs_2_ = bf16[304,1024]{1,0:T(8,128)(2,1)} collective-permute-done((bf16[304,1024]{1,0:T(8,128)(2,1)}, bf16[304,1024]{1,0:T(8,128)(2,1)}, u32[]{:S(2)}, u32[]{:S(2)}) %collective-permute-start.11) | collective-permute-done | bytes 622624 | tf_op jit(solution)/shard_map/ppermute | solution.py:743
  139.7 17.8 %mlp.1 = (bf16[608,2048]{1,0:T(8,128)(2,1)}, bf16[608,2048]{1,0:T(8,128)(2,1)}, f32[304,1024]{1,0:T(8,128)}, bf16[304,1024]{1,0:T(8,128)(2,1)}, f32[304,1024]{1,...) custom-call(s32[3]{0:T(128)} %pad_add_fusion.ids.refs_0_, ...), custom_call_target="tpu_custom_call" | custom-call | flops 21390000128 | bytes 262144 | tf_op jit(solution)/shard_map/mlp/pallas_call | solution.py:104
  164.1 7.4 %grad_fc2.1.refs_8_ = bf16[1024,1024]{1,0:T(8,128)(2,1)} custom-call(s32[3]{0:T(128)} %pad_add_fusion.ids.refs_0_, bf16[608,2048]{1,0:T(8,128)(2,1)} %get-tuple-element.81.refs_1_.refs_7_.refs_5_, bf16[608,2048]{1,0:T(8,128)(2,1)} %copy-done.17, bf16[304,1024]{1,0:T(8,128)(2,1)} %copy-done.4, bf16[304,1024]{1,0:T(8,128)(2,1)} %collective-permute-done.8.refs_11_.refs_4_, ...), custom_call_target="tpu_custom_call" | custom-call | flops 9200000000 | bytes 262144 | tf_op jit(solution)/shard_map/grad_fc2/pallas_call | solution.py:104
  176.0 5.4 %middle_back.1 = (f32[304,1024]{1,0:T(8,128)}, bf16[304,1024]{1,0:T(8,128)(2,1)}, bf16[304,512]{1,0:T(8,128)(2,1)}, bf16[304,512]{1,0:T(8,128)(2,1)}, f32[4,1024]{1,0:T(4,128)}) custom-call(s32[3]{0:T(128)} %pad_add_fusion.ids.refs_0_, f32[304,1024]{1,0:T(8,128)} %get-tuple-element.79.refs_1_, bf16[304,1024]{1,0:T(8,128)(2,1)} %copy-done.26, ...), custom_call_target="tpu_custom_call" | custom-call | flops 9200000000 | bytes 262144 | tf_op jit(solution)/shard_map/middle_back/pallas_call | solution.py:104
  183.0 5.9 %grad_fc1_send.1.refs_5_ = bf16[1024,512]{1,0:T(8,128)(2,1)} custom-call(s32[3]{0:T(128)} %pad_add_fusion.ids.refs_0_, bf16[304,1024]{1,0:T(8,128)(2,1)} %get-tuple-element.76.refs_1_.refs_14_, bf16[304,1024]{1,0:T(8,128)(2,1)} %collective-permute-done.11.refs_2_, bf16[304,1024]{1,0:T(8,128)(2,1)} %collective-permute-done.17.refs_13_.refs_3_, ...), custom_call_target="tpu_custom_call" | custom-call | flops 9200000000 | bytes 262144 | tf_op jit(solution)/shard_map/grad_fc1_send/pallas_call | solution.py:104
  196.1 16.9 %attend_back.1 = (bf16[2,608,384]{2,1,0:T(8,128)(2,1)}, bf16[2,608,384]{2,1,0:T(8,128)(2,1)}, f32[4,1,384]{2,1,0:T(1,128)}) custom-call(s32[3]{0:T(128)} %pad_add_fusion.ids.refs_0_, bf16[608,512]{1,0:T(8,128)(2,1)} %get-tuple-element.66.refs_1_, bf16[608,512]{1,0:T(8,128)(2,1)} %get-tuple-element.67.refs_2_, bf16[608,512]{1,0:T(8,128)(2,1)} %get-tuple-element.68.refs_3_, ...), custom_call_target="tpu_custom_call" | custom-call | flops 19434999808 | bytes 262144 | tf_op jit(solution)/shard_map/attend_back/pallas_call | solution.py:117
  216.7 7.0 %collective-permute-done.25.refs_7_ = bf16[1024,512]{1,0:T(8,128)(2,1)S(1)} collective-permute-done((bf16[1024,512]{1,0:T(8,128)(2,1)}, bf16[1024,512]{1,0:T(8,128)(2,1)S(1)}, u32[]{:S(2)}, u32[]{:S(2)}) %collective-permute-start.25) | collective-permute-done | bytes 1048608 | tf_op jit(solution)/shard_map/ppermute | solution.py:740
  224.6 5.6 %grad_fc1_keep.1 = (f32[256,512]{1,0:T(8,128)}, bf16[256,512]{1,0:T(8,128)(2,1)}, bf16[256,512]{1,0:T(8,128)(2,1)}, bf16[256,512]{1,0:T(8,128)(2,1)}) custom-call(s32[3]{0:T(128)} %pad_add_fusion.ids.refs_0_, bf16[304,1024]{1,0:T(8,128)(2,1)} %get-tuple-element.76.refs_1_.refs_14_, bf16[304,1024]{1,0:T(8,128)(2,1)} %collective-permute-done.11.refs_2_, ...), custom_call_target="tpu_custom_call" | custom-call | flops 9200000000 | bytes 262144 | tf_op jit(solution)/shard_map/grad_fc1_keep/pallas_call | solution.py:104
  231.2 5.7 %grad_qkv_send.1.refs_5_ = bf16[1024,384]{1,0:T(8,128)(2,1)} custom-call(s32[3]{0:T(128)} %pad_add_fusion.ids.refs_0_, bf16[608,1024]{1,0:T(8,128)(2,1)} %get-tuple-element.69.refs_4_.refs_1_, bf16[608,1024]{1,0:T(8,128)(2,1)} %copy-done.19, bf16[2,608,384]{2,1,0:T(8,128)(2,1)} %get-tuple-element.89.refs_8_.refs_3_.refs_1_, bf16[2,608,384]{2,1,0:T(8,128)(2,1)} %copy-done.21, ...), custom_call_target="tpu_custom_call" | custom-call | flops 9200000000 | bytes 262144 | tf_op jit(solution)/shard_map/grad_qkv_send/pallas_call | solution.py:104
  237.6 7.0 %qkv_back.1 = (f32[304,1024]{1,0:T(8,128)}, bf16[304,1024]{1,0:T(8,128)(2,1)}) custom-call(s32[3]{0:T(128)} %pad_add_fusion.ids.refs_0_, bf16[2,608,384]{2,1,0:T(8,128)(2,1)} %get-tuple-element.89.refs_8_.refs_3_.refs_1_, bf16[2,608,384]{2,1,0:T(8,128)(2,1)} %get-tuple-element.90.refs_2_, bf16[2048,640]{1,0:T(8,128)(2,1)} %bitcast.40, ...), custom_call_target="tpu_custom_call" | custom-call | flops 9200000000 | bytes 262144 | tf_op jit(solution)/shard_map/qkv_back/pallas_call | solution.py:104
  256.3 11.3 %collective-permute-done.32 = bf16[256,128]{1,0:T(8,128)(2,1)S(1)} collective-permute-done((bf16[256,128]{1,0:T(8,128)(2,1)}, bf16[256,128]{1,0:T(8,128)(2,1)S(1)}, u32[]{:S(2)}, u32[]{:S(2)}) %collective-permute-start.32) | collective-permute-done | bytes 65568 | tf_op jit(solution)/shard_map/ppermute | solution.py:749
  271.5 5.4 %grad_qkv_keep.1 = (f32[256,384]{1,0:T(8,128)}, bf16[256,384]{1,0:T(8,128)(2,1)}, bf16[256,384]{1,0:T(8,128)(2,1)}, bf16[256,384]{1,0:T(8,128)(2,1)}) custom-call(s32[3]{0:T(128)} %pad_add_fusion.ids.refs_0_, bf16[608,1024]{1,0:T(8,128)(2,1)} %get-tuple-element.69.refs_4_.refs_1_, bf16[608,1024]{1,0:T(8,128)(2,1)} %copy-done.19, ...), custom_call_target="tpu_custom_call" | custom-call | flops 9200000000 | bytes 262144 | tf_op jit(solution)/shard_map/grad_qkv_keep/pallas_call | solution.py:104
  288.2 8.2 %collective-permute-start.61 = (f32[16,256]{1,0:T(8,128)}, f32[16,256]{1,0:T(8,128)S(1)}, u32[]{:S(2)}, u32[]{:S(2)}) collective-permute-start(f32[16,256]{1,0:T(8,128)} %get-tuple-element.116), channel_id=1, source_target_pairs={{0,2},{2,4},{4,6},{6,0},{1,3},{3,5},{5,7},{7,1},{8,10},{10,12},{12... | collective-permute-start | bytes 49160 | tf_op jit(solution)/shard_map/ppermute | solution.py:749
  332.6 5.0 %place.3.refs_9_ = f32[256,4096]{1,0:T(8,128)} custom-call(s32[3]{0:T(128)} %pad_add_fusion.ids.refs_0_, bf16[256,512]{1,0:T(8,128)(2,1)} %copy-done.12, bf16[256,512]{1,0:T(8,128)(2,1)} %copy-done.40, bf16[256,512]{1,0:T(8,128)(2,1)} %copy-done.41, bf16[256,512]{1,0:T(8,128)(2,1)} %copy-done.42, bf16[256,512]{1,0:T(8,128)(2,1)} %copy-done.46, ...), custom_call_target="tpu_custom_call" | custom-call | flops 2760000000 | bytes 262144 | tf_op jit(solution)/shard_map/place/pallas_call | solution.py:117
  (306 shorter events, 155.6 us)
Async XLA Ops:
  7.2 112.8 %all-gather.4.cloned.1.call-start = ((), (), s32[]{:S(2)}) async-start(), calls=%async_computation.1 | async-start | bytes 4718592 | tf_op jit(solution)/shard_map/all_gather | solution.py:867
  14.8 25.4 %collective-permute-start.2 = (bf16[272,640]{1,0:T(8,128)(2,1)}, bf16[272,640]{1,0:T(8,128)(2,1)S(1)}, u32[]{:S(2)}, u32[]{:S(2)}) collective-permute-start(bf16[272,640]{1,0:T(8,128)(2,1)} %cast_qkv.1.refs_6_.refs_1_), channel_id=1, source_target_pairs={{0,4},{2,6},{4,0},{6,2},{1,5},{3,7},{5,1},{7,3},{8,12},{10,14},{12... | collective-permute-start | bytes 1044488 | tf_op jit(solution)/shard_map/ppermute | solution.py:749
  17.4 24.3 %collective-permute-start.3 = (bf16[272,640]{1,0:T(8,128)(2,1)}, bf16[272,640]{1,0:T(8,128)(2,1)S(1)}, u32[]{:S(2)}, u32[]{:S(2)}) collective-permute-start(bf16[272,640]{1,0:T(8,128)(2,1)} %cast_qkv.1.refs_6_.refs_1_), channel_id=1, source_target_pairs={{0,6},{2,0},{4,2},{6,4},{1,7},{3,1},{5,3},{7,5},{8,14},{10,8},{12,... | collective-permute-start | bytes 1044488 | tf_op jit(solution)/shard_map/ppermute | solution.py:749
  18.8 23.5 %collective-permute-start.4 = (bf16[272,640]{1,0:T(8,128)(2,1)}, bf16[272,640]{1,0:T(8,128)(2,1)S(1)}, u32[]{:S(2)}, u32[]{:S(2)}) collective-permute-start(bf16[272,640]{1,0:T(8,128)(2,1)} %cast_qkv.1.refs_6_.refs_1_), channel_id=1, source_target_pairs={{0,16},{16,0},{1,17},{17,1},{2,18},{18,2},{3,19},{19,3},{4,20},{20... | collective-permute-start | bytes 1044488 | tf_op jit(solution)/shard_map/ppermute | solution.py:740
  21.2 22.6 %collective-permute-start.8 = (bf16[304,1024]{1,0:T(8,128)(2,1)S(1)}, bf16[304,1024]{1,0:T(8,128)(2,1)}, u32[]{:S(2)}, u32[]{:S(2)}) collective-permute-start(bf16[304,1024]{1,0:T(8,128)(2,1)S(1)} %pad.8.refs_3_.refs_4_), channel_id=1, source_target_pairs={{0,1},{1,0},{2,3},{3,2},{4,5},{5,4},{6,7},{7,6},{8,9},{9,8},{10,11... | collective-permute-start | bytes 1867784 | tf_op jit(solution)/shard_map/ppermute | solution.py:743
  26.2 23.1 %collective-permute-start = (bf16[304,1024]{1,0:T(8,128)(2,1)S(1)}, bf16[304,1024]{1,0:T(8,128)(2,1)S(1)}, u32[]{:S(2)}, u32[]{:S(2)}) collective-permute-start(bf16[304,1024]{1,0:T(8,128)(2,1)S(1)} %pad.7.refs_1_.refs_3_), channel_id=1, source_target_pairs={{0,1},{1,0},{2,3},{3,2},{4,5},{5,4},{6,7},{7,6},{8,9},{9,8},{10,11... | collective-permute-start | bytes 1867784 | tf_op jit(solution)/shard_map/ppermute | solution.py:743
  30.8 216.0 %reduce-scatter.2.cloned.1.call-start = ((), (), s32[]{:S(2)}) async-start(), calls=%async_computation.2 | async-start | bytes 2359296 | tf_op jit(solution)/shard_map/reduce_scatter | solution.py:1085
  41.8 21.9 %collective-permute-start.6 = (bf16[272,640]{1,0:T(8,128)(2,1)S(1)}, bf16[272,640]{1,0:T(8,128)(2,1)S(1)}, u32[]{:S(2)}, u32[]{:S(2)}) collective-permute-start(bf16[272,640]{1,0:T(8,128)(2,1)S(1)} %collective-permute-done.2.refs_3_), channel_id=1, source_target_pairs={{0,16},{16,0},{1,17},{17,1},{2,18},{18,2},{3,19},{19,3},{4,20},{20... | collective-permute-start | bytes 1044488 | tf_op jit(solution)/shard_map/ppermute | solution.py:740
  42.3 28.7 %collective-permute-start.7 = (bf16[272,640]{1,0:T(8,128)(2,1)S(1)}, bf16[272,640]{1,0:T(8,128)(2,1)S(1)}, u32[]{:S(2)}, u32[]{:S(2)}) collective-permute-start(bf16[272,640]{1,0:T(8,128)(2,1)S(1)} %collective-permute-done.3.refs_4_), channel_id=1, source_target_pairs={{0,16},{16,0},{1,17},{17,1},{2,18},{18,2},{3,19},{19,3},{4,20},{20... | collective-permute-start | bytes 1044488 | tf_op jit(solution)/shard_map/ppermute | solution.py:740
  119.9 19.7 %collective-permute-start.12 = (bf16[2048,1024]{1,0:T(8,128)(2,1)}, bf16[2048,1024]{1,0:T(8,128)(2,1)}, u32[]{:S(2)}, u32[]{:S(2)}) collective-permute-start(bf16[2048,1024]{1,0:T(8,128)(2,1)} %all-gather.4.cloned.1.call-done.refs_6_), channel_id=1, source_target_pairs={{0,8},{8,0},{1,9},{9,1},{2,10},{10,2},{3,11},{11,3},{4,12},{12,4},... | collective-permute-start | bytes 12582920 | tf_op jit(solution)/shard_map/ppermute | solution.py:737
  120.5 16.8 %collective-permute-start.11 = (bf16[304,1024]{1,0:T(8,128)(2,1)}, bf16[304,1024]{1,0:T(8,128)(2,1)}, u32[]{:S(2)}, u32[]{:S(2)}) collective-permute-start(bf16[304,1024]{1,0:T(8,128)(2,1)} %get-tuple-element.76.refs_1_.refs_14_), channel_id=1, source_target_pairs={{0,1},{1,0},{2,3},{3,2},{4,5},{5,4},{6,7},{7,6},{8,9},{9,8},{10,11... | collective-permute-start | bytes 1867784 | tf_op jit(solution)/shard_map/ppermute | solution.py:743
  158.1 17.1 %collective-permute-start.20 = (bf16[304,1024]{1,0:T(8,128)(2,1)}, bf16[304,1024]{1,0:T(8,128)(2,1)S(1)}, u32[]{:S(2)}, u32[]{:S(2)}) collective-permute-start(bf16[304,1024]{1,0:T(8,128)(2,1)} %get-tuple-element.80), channel_id=1, source_target_pairs={{0,1},{1,0},{2,3},{3,2},{4,5},{5,4},{6,7},{7,6},{8,9},{9,8},{10,11... | collective-permute-start | bytes 1867784 | tf_op jit(solution)/shard_map/ppermute | solution.py:743
  159.5 55.6 %collective-permute-start.19 = (bf16[304,1024]{1,0:T(8,128)(2,1)}, bf16[304,1024]{1,0:T(8,128)(2,1)S(1)}, u32[]{:S(2)}, u32[]{:S(2)}) collective-permute-start(bf16[304,1024]{1,0:T(8,128)(2,1)} %get-tuple-element.78), channel_id=1, source_target_pairs={{0,1},{1,0},{2,3},{3,2},{4,5},{5,4},{6,7},{7,6},{8,9},{9,8},{10,11... | collective-permute-start | bytes 1867784 | tf_op jit(solution)/shard_map/ppermute | solution.py:743
  171.5 180.8 %all-gather.6.cloned.1.call-start = ((), (), s32[]{:S(2)}) async-start(), calls=%async_computation.3 | async-start | bytes 2359296 | tf_op jit(solution)/shard_map/all_gather | solution.py:1086
  188.9 34.7 %collective-permute-start.25 = (bf16[1024,512]{1,0:T(8,128)(2,1)}, bf16[1024,512]{1,0:T(8,128)(2,1)S(1)}, u32[]{:S(2)}, u32[]{:S(2)}) collective-permute-start(bf16[1024,512]{1,0:T(8,128)(2,1)} %grad_fc1_send.1.refs_5_), channel_id=1, source_target_pairs={{0,16},{16,0},{1,17},{17,1},{2,18},{18,2},{3,19},{19,3},{4,20},{20... | collective-permute-start | bytes 3145736 | tf_op jit(solution)/shard_map/ppermute | solution.py:740
  212.9 17.3 %collective-permute-start.24 = (bf16[2,608,384]{2,1,0:T(8,128)(2,1)}, bf16[2,608,384]{2,1,0:T(8,128)(2,1)S(1)}, u32[]{:S(2)}, u32[]{:S(2)}) collective-permute-start(bf16[2,608,384]{2,1,0:T(8,128)(2,1)} %get-tuple-element.90.refs_2_), channel_id=1, source_target_pairs={{0,8},{8,0},{1,9},{9,1},{2,10},{10,2},{3,11},{11,3},{4,12},{12,4},... | collective-permute-start | bytes 2801672 | tf_op jit(solution)/shard_map/ppermute | solution.py:737
  213.0 33.8 %collective-permute-start.28 = (bf16[1024,128]{1,0:T(8,128)(2,1)S(1)}, bf16[1024,128]{1,0:T(8,128)(2,1)S(1)}, u32[]{:S(2)}, u32[]{:S(2)}) collective-permute-start(bf16[1024,128]{1,0:T(8,128)(2,1)S(1)} %copy-done.45), channel_id=1, source_target_pairs={{0,1},{1,0},{2,3},{3,2},{4,5},{5,4},{6,7},{7,6},{8,9},{9,8},{10,11... | collective-permute-start | bytes 786440 | tf_op jit(solution)/shard_map/ppermute | solution.py:743
  213.6 33.2 %collective-permute-start.29 = (bf16[1024,128]{1,0:T(8,128)(2,1)S(1)}, bf16[1024,128]{1,0:T(8,128)(2,1)S(1)}, u32[]{:S(2)}, u32[]{:S(2)}) collective-permute-start(bf16[1024,128]{1,0:T(8,128)(2,1)S(1)} %copy-done.44), channel_id=1, source_target_pairs={{0,16},{16,0},{1,17},{17,1},{2,18},{18,2},{3,19},{19,3},{4,20},{20... | collective-permute-start | bytes 786440 | tf_op jit(solution)/shard_map/ppermute | solution.py:740
  215.1 31.7 %collective-permute-start.30 = (bf16[1024,128]{1,0:T(8,128)(2,1)S(1)}, bf16[1024,128]{1,0:T(8,128)(2,1)S(1)}, u32[]{:S(2)}, u32[]{:S(2)}) collective-permute-start(bf16[1024,128]{1,0:T(8,128)(2,1)S(1)} %copy-done.43), channel_id=1, source_target_pairs={{0,17},{1,16},{16,1},{17,0},{2,19},{3,18},{18,3},{19,2},{4,21},{5,... | collective-permute-start | bytes 786440 | tf_op jit(solution)/shard_map/ppermute | solution.py:746
  236.9 33.8 %collective-permute-start.27 = (bf16[1024,384]{1,0:T(8,128)(2,1)}, bf16[1024,384]{1,0:T(8,128)(2,1)S(1)}, u32[]{:S(2)}, u32[]{:S(2)}) collective-permute-start(bf16[1024,384]{1,0:T(8,128)(2,1)} %grad_qkv_send.1.refs_5_), channel_id=1, source_target_pairs={{0,16},{16,0},{1,17},{17,1},{2,18},{18,2},{3,19},{19,3},{4,20},{20... | collective-permute-start | bytes 2359304 | tf_op jit(solution)/shard_map/ppermute | solution.py:740
  250.3 17.3 %collective-permute-start.32 = (bf16[256,128]{1,0:T(8,128)(2,1)}, bf16[256,128]{1,0:T(8,128)(2,1)S(1)}, u32[]{:S(2)}, u32[]{:S(2)}) collective-permute-start(bf16[256,128]{1,0:T(8,128)(2,1)} %get-tuple-element.100), channel_id=1, source_target_pairs={{0,4},{2,6},{4,0},{6,2},{1,5},{3,7},{5,1},{7,3},{8,12},{10,14},{12... | collective-permute-start | bytes 196616 | tf_op jit(solution)/shard_map/ppermute | solution.py:749
  253.7 50.8 %collective-permute-start.51 = (bf16[256,512]{1,0:T(8,128)(2,1)S(1)}, bf16[256,512]{1,0:T(8,128)(2,1)S(1)}, u32[]{:S(2)}, u32[]{:S(2)}) collective-permute-start(bf16[256,512]{1,0:T(8,128)(2,1)S(1)} %copy-done.39), channel_id=1, source_target_pairs={{0,2},{2,4},{4,6},{6,0},{1,3},{3,5},{5,7},{7,1},{8,10},{10,12},{12... | collective-permute-start | bytes 786440 | tf_op jit(solution)/shard_map/ppermute | solution.py:749
  256.3 49.2 %collective-permute-start.52 = (bf16[256,512]{1,0:T(8,128)(2,1)S(1)}, bf16[256,512]{1,0:T(8,128)(2,1)S(1)}, u32[]{:S(2)}, u32[]{:S(2)}) collective-permute-start(bf16[256,512]{1,0:T(8,128)(2,1)S(1)} %copy-done.38), channel_id=1, source_target_pairs={{0,4},{2,6},{4,0},{6,2},{1,5},{3,7},{5,1},{7,3},{8,12},{10,14},{12... | collective-permute-start | bytes 786440 | tf_op jit(solution)/shard_map/ppermute | solution.py:749
  267.6 38.6 %collective-permute-start.53 = (bf16[256,512]{1,0:T(8,128)(2,1)S(1)}, bf16[256,512]{1,0:T(8,128)(2,1)S(1)}, u32[]{:S(2)}, u32[]{:S(2)}) collective-permute-start(bf16[256,512]{1,0:T(8,128)(2,1)S(1)} %copy-done.37), channel_id=1, source_target_pairs={{0,6},{2,0},{4,2},{6,4},{1,7},{3,1},{5,3},{7,5},{8,14},{10,8},{12,... | collective-permute-start | bytes 786440 | tf_op jit(solution)/shard_map/ppermute | solution.py:749
  (117 other events, 1220.1 us)
Sparse Core Ops, SparseCore 0:
  30.9 88.9 all-gather.3
  171.6 75.0 reduce-scatter.1
  248.7 30.1 all-gather.5
